TPU v7x, 32 devices: a whole 2x2x4 slice. The times are simulated.
32 devices in a mesh: seq: 4 (over y, x), fsdp: 8 (over z, core).
Axes of the slice: x: 2, y: 2, z: 4, core: 2. Of those that a mesh axis runs over, the one named last changes fastest.
Arguments:
- inputs: bfloat16 [8, 1536, 768], P(None, ('seq', 'fsdp')), may hold values from -6 to 6
- w_query: bfloat16 [768, 768], P('fsdp'), may hold values from -0.21875 to 0.21875
- w_key: bfloat16 [768, 768], P('fsdp'), may hold values from -0.21875 to 0.21875
- w_value: bfloat16 [768, 768], P('fsdp'), may hold values from -0.21875 to 0.21875
- b_value: bfloat16 [768], P('fsdp'), may hold values from -3 to 3
- w_out: bfloat16 [768, 768], P('fsdp'), may hold values from -0.625 to 0.625
- b_out: bfloat16 [768], P('fsdp'), may hold values from -3 to 3
- norm1_gain: bfloat16 [768], P('fsdp'), may hold values from 0.099609375 to 1.8984375
- norm1_bias: bfloat16 [768], P('fsdp'), may hold values from -3 to 3
- w_in: bfloat16 [768, 3072], P('fsdp'), may hold values from -0.21875 to 0.21875
- b_in: bfloat16 [3072], P('fsdp'), may hold values from -3 to 3
- w_back: bfloat16 [3072, 768], P('fsdp'), may hold values from -0.15625 to 0.15625
- b_back: bfloat16 [768], P('fsdp'), may hold values from -3 to 3
- norm2_gain: bfloat16 [768], P('fsdp'), may hold values from 0.099609375 to 1.8984375
- norm2_bias: bfloat16 [768], P('fsdp'), may hold values from -3 to 3
- w_relative: bfloat16 [768, 12, 64], P('fsdp', 'seq'), may hold values from -0.21875 to 0.21875
- bias_content: bfloat16 [12, 64], P('seq', 'fsdp'), may hold values from -5 to 5
- bias_position: bfloat16 [12, 64], P('seq', 'fsdp'), may hold values from -5 to 5
- bias_type: bfloat16 [12, 64], P('seq', 'fsdp'), may hold values from -5 to 5
- type_embed: bfloat16 [2, 12, 64], P(None, 'seq', 'fsdp'), may hold values from -5 to 5
- lengths: int32 [8, 3], replicated, may hold values from 1 to 1024, 1536 in all within a row
- token_types: int32 [8, 1536], replicated, may hold values from 0 to 1
- owners: int32 [8], replicated, may hold values from 0 to 7, each once
- grad_output: bfloat16 [8, 1536, 768], P('fsdp', 'seq'), may hold values from -6 to 6
Outputs:
- activations: bfloat16 [8, 1536, 768], P('fsdp', 'seq')
- input_grad: bfloat16 [8, 1536, 768], P(None, ('seq', 'fsdp'))
- grad_w_query: float32 [768, 768], P(('seq', 'fsdp'))
- grad_w_key: float32 [768, 768], P(('seq', 'fsdp'))
- grad_w_value: float32 [768, 768], P(('seq', 'fsdp'))
- grad_b_value: float32 [768], P(('seq', 'fsdp'))
- grad_w_out: float32 [768, 768], P(('seq', 'fsdp'))
- grad_b_out: float32 [768], P(('seq', 'fsdp'))
- grad_norm1_gain: float32 [768], P(('seq', 'fsdp'))
- grad_norm1_bias: float32 [768], P(('seq', 'fsdp'))
- grad_w_in: float32 [768, 3072], P(('seq', 'fsdp'))
- grad_b_in: float32 [3072], P(('seq', 'fsdp'))
- grad_w_back: float32 [3072, 768], P(('seq', 'fsdp'))
- grad_b_back: float32 [768], P(('seq', 'fsdp'))
- grad_norm2_gain: float32 [768], P(('seq', 'fsdp'))
- grad_norm2_bias: float32 [768], P(('seq', 'fsdp'))
- grad_w_relative: float32 [768, 12, 64], P('fsdp', 'seq')
- grad_bias_content: float32 [12, 64], P('seq', 'fsdp')
- grad_bias_position: float32 [12, 64], P('seq', 'fsdp')
- grad_bias_type: float32 [12, 64], P('seq', 'fsdp')
- grad_type_embed: float32 [2, 12, 64], P(None, 'seq', 'fsdp')
Inputs may be any that keep to these rules, and one draw needn't show every extreme that they name: Each row holds the lengths of the 3 sequences of one pack, in order; a row sums to 1536 and its largest entry is 1024. Pack j is processed by fsdp index owners[j]; every index owns one pack.
All inputs are finite; a program needn't handle non-finite values.
Results may differ from a plain program's by a relative error of at most 0.017.
The roundings to bfloat16 on the way count: a program that leaves them out, or rounds other values in their place, can miss the bound.
Values may be sent and summed in bfloat16 or wider, within the bound.
No kernel may reach another device: no remote copies, remote signals or barrier semaphores. Data moves between devices by JAX's collectives and lax.ppermute only.
A program may use at most 192 MiB of HBM per device.

v0:
```python
import jax
import jax.numpy as jnp
from jax import lax
from jax.experimental import pallas as pl
from jax.experimental.pallas import tpu as pltpu
from jax.sharding import PartitionSpec as P

DH = 64
LONGEST = 1024
QB = 256
BLOCKED = -1e30
BF = jnp.bfloat16
F32 = jnp.float32
VM = pl.BlockSpec(memory_space=pltpu.VMEM)
SM = pl.BlockSpec(memory_space=pltpu.SMEM)
VMEM_LIMIT = 60 * 1024 * 1024


def lanes_of(rows, width=128):
    return lax.broadcasted_iota(jnp.int32, (rows, width), 1)


def split3(value):
    high = value.astype(BF).astype(F32)
    rest = value - high
    middle = rest.astype(BF).astype(F32)
    return high, middle, rest - middle


def masks_of(place):
    return 0, place[3], place[4], 3


def pick(lane, first, columns, base):
    for number, column in enumerate(columns):
        base = jnp.where(lane == first + number, column, base)
    return base


def project_body(place, x0, x1, x2, x3, w_ref, head_ref, tcol_ref, qx_ref, pq_ref, kx_ref, kxt_ref, vx_ref, vxt_ref, rolled):
    own, start, near = place[0], place[1], place[2]
    scale = DH ** -0.5
    rows = qx_ref.shape[1]
    part = x0.shape[0]
    for mask, piece in zip(masks_of(place), (x0, x1, x2, x3)):
        y = jnp.dot(piece[...], w_ref[...], preferred_element_type=F32)
        base = pl.multiple_of((own ^ mask) * part, 8)
        for c in range(5):
            column = y[:, c * 128 : (c + 1) * 128]
            rolled[c, pl.ds(base, part), :] = column
            rolled[c, pl.ds(pl.multiple_of(base + rows, 8), part), :] = column

    def block(r, carry):
        row = pl.multiple_of(r * QB, QB)
        lane = lanes_of(QB)
        kind = tcol_ref[pl.ds(row, QB), :]
        index = row + lax.broadcasted_iota(jnp.int32, (QB, 1), 0)
        small = index >= LONGEST
        first = jnp.where(small & (index < LONGEST + near), 1.0, 0.0)
        second = jnp.where(small & (index >= LONGEST + near), 1.0, 0.0)
        one = jnp.where(kind == 1, 1.0, 0.0)
        zero = 1.0 - one
        for h in range(3):
            both = rolled[h, pl.ds(start + row, QB), :].astype(BF).astype(F32)
            if h < 2:
                v = rolled[3, pl.ds(start + row, QB), :]
                v = v if h == 0 else pltpu.roll(v, 64, 1)
            else:
                v = rolled[4, pl.ds(start + row, QB), :]
            head = head_ref[h]
            content = (both + head[0:1]) * scale
            position = ((both + head[1:2]) * scale).astype(BF)
            typed = (both + head[2:3]) * scale
            differ = jnp.sum(typed * head[3:4], axis=1, keepdims=True)
            same = jnp.sum(typed * head[4:5], axis=1, keepdims=True)
            for_zero = jnp.where(kind == 1, differ, same)
            for_one = jnp.where(kind == 1, same, differ)
            columns = [*split3(for_zero), *split3(for_one), second * BLOCKED, first * BLOCKED]
            qx = pick(lane, 64, columns, jnp.where(lane < 64, content, 0.0)).astype(BF)
            qx_ref[h, pl.ds(row, QB), :] = qx
            raw = pltpu.roll(both, 64, 1)
            pq_ref[h, pl.ds(row, QB), :] = jnp.where(lane < 64, position.astype(F32), raw).astype(BF)
            kx = pick(lane, 64, [zero, zero, zero, one, one, one, first, second], jnp.where(lane < 64, raw, 0.0))
            kx_ref[h, pl.ds(row, QB), :] = kx.astype(BF)
            kxt_ref[h, :, pl.ds(row, QB)] = jnp.transpose(kx, (1, 0)).astype(BF)
            vx = jnp.where(lane < 64, v + head[5:6], jnp.where(lane < 67, 1.0, 0.0)).astype(BF)
            vx_ref[h, pl.ds(row, QB), :] = vx
            vxt_ref[h, :, pl.ds(row, QB)] = jnp.transpose(vx.astype(F32), (1, 0)).astype(BF)
        return carry

    lax.fori_loop(0, rows // QB, block, 0)


def project(place, pieces, w_qkv, head, tcol):
    rows = 4 * pieces[0].shape[0]
    tall = jax.ShapeDtypeStruct((3, rows, 128), BF)
    wide = jax.ShapeDtypeStruct((3, 128, rows), BF)
    return pl.pallas_call(
        project_body,
        in_specs=[SM] + [VM] * 7,
        out_specs=[VM] * 6,
        out_shape=[tall, tall, tall, wide, tall, wide],
        scratch_shapes=[pltpu.VMEM((5, 2 * rows, 128), F32)],
        compiler_params=pltpu.CompilerParams(vmem_limit_bytes=VMEM_LIMIT),
        cost_estimate=pl.CostEstimate(flops=2 * rows * 768 * 640, bytes_accessed=10_000_000, transcendentals=0),
        name="project",
    )(place, *pieces, w_qkv, head, tcol)


def attend_body(place, qx_ref, pq_ref, kxt_ref, vx_ref, kpt_ref, wrt_ref, sn_ref, cs_ref, big_ref, small_ref, ox_ref, o0, o1, o2, o3, keys, left, outs):
    h, i = pl.program_id(0), pl.program_id(1)
    own, start = place[0], place[1]
    width = kpt_ref.shape[0]
    half = width // 2
    rows = kpt_ref.shape[1]

    @pl.when((h == 0) & (i == 0))
    def _():
        keys[0:width, :] = kpt_ref[...]

    @pl.when(i == 0)
    def _():
        keys[width:, :] = kxt_ref[0]

    rel = jnp.dot(pq_ref[0], wrt_ref[0], preferred_element_type=F32)
    r1, r2 = rel[:, :half], rel[:, half:]
    sn, cs = sn_ref[...], cs_ref[...]
    left[:, 0:half] = (r1 * sn + r2 * cs).astype(BF)
    left[:, half:width] = (r2 * sn - r1 * cs).astype(BF)
    left[:, width:] = qx_ref[0]

    def attend(low, high, store):
        score = jnp.dot(left[...], keys[:, low:high], preferred_element_type=F32)
        top = jnp.max(score, axis=1, keepdims=True)
        raised = jnp.exp(score - top).astype(BF)
        store[0] = raised
        mixed = jnp.dot(raised, vx_ref[0, low:high, :], preferred_element_type=F32)
        inverse = 1.0 / mixed[:, 64:65]
        lane = lanes_of(QB)
        ox = jnp.where(lane < 64, mixed * inverse, jnp.where(lane == 64, inverse, 0.0))
        ox_ref[0] = ox
        row = pl.multiple_of(i * QB, QB)
        outs[h, pl.ds(row, QB), :] = ox
        outs[h, pl.ds(pl.multiple_of(row + rows, QB), QB), :] = ox

    @pl.when(i < LONGEST // QB)
    def _():
        attend(0, LONGEST, big_ref)

    @pl.when(i >= LONGEST // QB)
    def _():
        attend(LONGEST, rows, small_ref)

    @pl.when((h == 2) & (i == pl.num_programs(1) - 1))
    def _():
        part = o0.shape[0]
        for mask, out in zip(masks_of(place), (o0, o1, o2, o3)):
            at = lax.rem((own ^ mask) * part + rows - start, rows)
            out[...] = jnp.concatenate([outs[g, pl.ds(at, part), :][:, 0:64] for g in range(3)], axis=1).astype(BF)


def attend(place, qx, pq, kxt, vx, kpt, wrt, sn, cs):
    rows = qx.shape[1]
    width = kpt.shape[0]
    blocks = rows // QB
    bigs = LONGEST // QB
    rest = rows - LONGEST
    per_block = lambda h, i: (h, i, 0)
    per_head = lambda h, i: (h, 0, 0)
    whole2 = lambda h, i: (0, 0)
    part = rows // 4
    out_piece = jax.ShapeDtypeStruct((part, 192), BF)
    return pl.pallas_call(
        attend_body,
        grid=(3, blocks),
        in_specs=[
            SM,
            pl.BlockSpec((1, QB, 128), per_block),
            pl.BlockSpec((1, QB, 128), per_block),
            pl.BlockSpec((1, 128, rows), per_head),
            pl.BlockSpec((1, rows, 128), per_head),
            pl.BlockSpec((width, rows), whole2, pipeline_mode=pl.Buffered(1)),
            pl.BlockSpec((1, 128, width), per_head),
            pl.BlockSpec((QB, width // 2), lambda h, i: (i, 0)),
            pl.BlockSpec((QB, width // 2), lambda h, i: (i, 0)),
        ],
        out_specs=[
            pl.BlockSpec((1, QB, LONGEST), lambda h, i: (h, jnp.minimum(i, bigs - 1), 0)),
            pl.BlockSpec((1, QB, rest), lambda h, i: (h, jnp.maximum(i - bigs, 0), 0)),
            pl.BlockSpec((1, QB, 128), per_block),
        ]
        + [pl.BlockSpec((part, 192), whole2)] * 4,
        out_shape=[
            jax.ShapeDtypeStruct((3, LONGEST, LONGEST), BF),
            jax.ShapeDtypeStruct((3, rest, rest), BF),
            jax.ShapeDtypeStruct((3, rows, 128), F32),
        ]
        + [out_piece] * 4,
        scratch_shapes=[
            pltpu.VMEM((width + 128, rows), BF),
            pltpu.VMEM((QB, width + 128), BF),
            pltpu.VMEM((3, 2 * rows, 128), F32),
        ],
        compiler_params=pltpu.CompilerParams(vmem_limit_bytes=VMEM_LIMIT, dimension_semantics=("arbitrary", "arbitrary")),
        cost_estimate=pl.CostEstimate(flops=12_000_000_000, bytes_accessed=20_000_000, transcendentals=4_000_000),
        name="attend",
    )(place, qx, pq, kxt, vx, kpt, wrt, sn, cs)


def back_body(place, d0, d1, d2, d3, big_ref, small_ref, ox_ref, qx_ref, pq_ref, kx_ref, vxt_ref, kp_ref, wr_ref, sn_ref, cs_ref, tcol_ref, head_ref, gkeep_ref, gsend_ref, rel_ref, sum_ref, douts, dkt, dvt, gwt, grads):
    h, i = pl.program_id(0), pl.program_id(1)
    own, start = place[0], place[1]
    rows, width = kp_ref.shape
    half = width // 2
    scale = DH ** -0.5
    part = d0.shape[0]
    last = pl.num_programs(1) - 1
    row = pl.multiple_of(i * QB, QB)
    again = pl.multiple_of(row + rows, QB)

    @pl.when((h == 0) & (i == 0))
    def _():
        blank = jnp.zeros((part, 64), F32)
        for mask, piece in zip(masks_of(place), (d0, d1, d2, d3)):
            values = piece[...].astype(F32)
            base = pl.multiple_of((own ^ mask) * part, 8)
            for g in range(3):
                padded = jnp.concatenate([values[:, g * 64 : (g + 1) * 64], blank], axis=1)
                douts[g, pl.ds(base, part), :] = padded
                douts[g, pl.ds(pl.multiple_of(base + rows, 8), part), :] = padded

    @pl.when(i == 0)
    def _():
        dkt[...] = jnp.zeros_like(dkt)
        dvt[...] = jnp.zeros_like(dvt)
        gwt[...] = jnp.zeros_like(gwt)
        sum_ref[...] = jnp.zeros_like(sum_ref)

    lane = lanes_of(QB)
    dout = douts[h, pl.ds(start + row, QB), :]
    ox = ox_ref[0]
    inverse = ox[:, 64:65]
    dot_row = jnp.sum(dout * ox, axis=1, keepdims=True)
    dox = pick(lane, 64, [-x for x in split3(dot_row)], dout).astype(BF)
    dout_t = jnp.transpose(dout * inverse, (1, 0))[0:64].astype(BF)
    qx = qx_ref[0]
    qc_t = jnp.transpose(qx.astype(F32), (1, 0))[0:64].astype(BF)
    pq = pq_ref[0].astype(F32)
    qp_t = jnp.transpose(pq, (1, 0))[0:64].astype(BF)
    sn, cs = sn_ref[...], cs_ref[...]

    def back(low, high, saved):
        raised = saved[0]
        dprob = jnp.dot(dox, vxt_ref[0, :, low:high], preferred_element_type=F32)
        dscore = (raised.astype(F32) * (dprob * inverse)).astype(BF)
        dvt[:, low:high] += jnp.dot(dout_t, raised, preferred_element_type=F32)
        dkt[:, low:high] += jnp.dot(qc_t, dscore, preferred_element_type=F32)
        da = jnp.dot(dscore, kp_ref[low:high, :], preferred_element_type=F32)
        dqx = jnp.dot(dscore, kx_ref[0, low:high, :], preferred_element_type=F32)
        da1, da2 = da[:, 0:half], da[:, half:width]
        drel = jnp.concatenate([(da1 * sn - da2 * cs).astype(BF), (da1 * cs + da2 * sn).astype(BF)], axis=1)
        dqp = jnp.dot(drel, wr_ref[0], preferred_element_type=F32)
        gwt[...] += jnp.dot(qp_t, drel, preferred_element_type=F32)
        kind = tcol_ref[...]
        over_zero, over_one = dqx[:, 64:65], dqx[:, 67:68]
        same = jnp.where(kind == 1, over_one, over_zero)
        differ = jnp.where(kind == 1, over_zero, over_one)
        head = head_ref[0]
        dqt = differ * head[3:4] + same * head[4:5]
        dqc = jnp.where(lane < 64, dqx, 0.0)
        dq = (dqc + dqp + dqt) * scale
        grads[h, pl.ds(row, QB), :] = dq
        typed = (pltpu.roll(pq, 64, 1) + head[2:3]) * scale
        sums = [dqc * scale, dqp * scale, dqt * scale, differ * typed, same * typed]
        for number, values in enumerate(sums):
            sum_ref[0, number : number + 1, :] += jnp.sum(values, axis=0, keepdims=True)

    @pl.when(i < LONGEST // QB)
    def _():
        back(0, LONGEST, big_ref)

    @pl.when(i >= LONGEST // QB)
    def _():
        back(LONGEST, rows, small_ref)

    @pl.when(i == last)
    def _():
        dk = jnp.transpose(dkt[...], (1, 0))
        dq = grads[h, 0:rows, :]
        pair = jnp.concatenate([dq[:, 0:64], dk], axis=1)
        grads[h, 0:rows, :] = pair
        grads[h, rows : 2 * rows, :] = pair
        dv = jnp.transpose(dvt[...], (1, 0)).astype(BF).astype(F32)
        sum_ref[0, 5:6, 0:64] = jnp.sum(dv, axis=0, keepdims=True)
        blank = jnp.zeros_like(dv)
        rel = jnp.transpose(gwt[...], (1, 0))
        empty = jnp.zeros_like(rel)

        @pl.when(h == 0)
        def _():
            padded = jnp.concatenate([dv, blank], axis=1)
            grads[3, 0:rows, :] = padded
            grads[3, rows : 2 * rows, :] = padded
            rel_ref[:, 0:128] = jnp.concatenate([empty, rel], axis=1)

        @pl.when(h == 1)
        def _():
            rel_ref[:, 128:256] = jnp.concatenate([rel, empty], axis=1)
            padded = grads[3, 0:rows, :] + jnp.concatenate([blank, dv], axis=1)
            grads[3, 0:rows, :] = padded
            grads[3, rows : 2 * rows, :] = padded

        @pl.when(h == 2)
        def _():
            padded = jnp.concatenate([dv, blank], axis=1)
            grads[4, 0:rows, :] = padded
            grads[4, rows : 2 * rows, :] = padded
            rel_ref[:, 128:256] += jnp.concatenate([empty, rel], axis=1)
            spots = ((gkeep_ref, 0), (gsend_ref, 0), (gkeep_ref, part), (gsend_ref, part))
            for mask, (out, low) in zip(masks_of(place), spots):
                at = lax.rem((own ^ mask) * part + rows - start, rows)
                for c in range(5):
                    out[low : low + part, c * 128 : (c + 1) * 128] = grads[c, pl.ds(at, part), :].astype(BF)


def attend_back(place, douts, big, small, ox, qx, pq, kx, vxt, kp, wr, sn, cs, tcol, head):
    rows, width = kp.shape
    blocks = rows // QB
    bigs = LONGEST // QB
    rest = rows - LONGEST
    part = rows // 4
    per_block = lambda h, i: (h, i, 0)
    per_head = lambda h, i: (h, 0, 0)
    whole2 = lambda h, i: (0, 0)
    return pl.pallas_call(
        back_body,
        grid=(3, blocks),
        in_specs=[SM]
        + [pl.BlockSpec((part, 192), whole2)] * 4
        + [
            pl.BlockSpec((1, QB, LONGEST), lambda h, i: (h, jnp.minimum(i, bigs - 1), 0)),
            pl.BlockSpec((1, QB, rest), lambda h, i: (h, jnp.maximum(i - bigs, 0), 0)),
            pl.BlockSpec((1, QB, 128), per_block),
            pl.BlockSpec((1, QB, 128), per_block),
            pl.BlockSpec((1, QB, 128), per_block),
            pl.BlockSpec((1, rows, 128), per_head),
            pl.BlockSpec((1, 128, rows), per_head),
            pl.BlockSpec((rows, width), whole2, pipeline_mode=pl.Buffered(1)),
            pl.BlockSpec((1, width, 128), per_head),
            pl.BlockSpec((QB, width // 2), lambda h, i: (i, 0)),
            pl.BlockSpec((QB, width // 2), lambda h, i: (i, 0)),
            pl.BlockSpec((QB, 1), lambda h, i: (i, 0)),
            pl.BlockSpec((1, 8, 128), per_head),
        ],
        out_specs=[pl.BlockSpec((2 * part, 640), whole2)] * 2
        + [pl.BlockSpec((width, 256), whole2), pl.BlockSpec((1, 8, 128), per_head)],
        out_shape=[jax.ShapeDtypeStruct((2 * part, 640), BF)] * 2
        + [jax.ShapeDtypeStruct((width, 256), F32), jax.ShapeDtypeStruct((3, 8, 128), F32)],
        scratch_shapes=[
            pltpu.VMEM((3, 2 * rows, 128), F32),
            pltpu.VMEM((64, rows), F32),
            pltpu.VMEM((64, rows), F32),
            pltpu.VMEM((64, width), F32),
            pltpu.VMEM((5, 2 * rows, 128), F32),
        ],
        compiler_params=pltpu.CompilerParams(vmem_limit_bytes=VMEM_LIMIT, dimension_semantics=("arbitrary", "arbitrary")),
        cost_estimate=pl.CostEstimate(flops=20_000_000_000, bytes_accessed=25_000_000, transcendentals=0),
        name="attend_back",
    )(place, *douts, big, small, ox, qx, pq, kx, vxt, kp, wr, sn, cs, tcol, head)


def reload_body(owners, in_ref, out_ref):
    def move(j, carry):
        out_ref[j] = in_ref[owners[j]]
        return carry

    lax.fori_loop(0, out_ref.shape[0], move, 0)


def reload(owners, returned):
    return pl.pallas_call(
        reload_body,
        in_specs=[SM, VM],
        out_specs=VM,
        out_shape=jax.ShapeDtypeStruct(returned.shape, returned.dtype),
        compiler_params=pltpu.CompilerParams(vmem_limit_bytes=VMEM_LIMIT),
        name="reload",
    )(owners, returned)


def qkv_blocks_body(place, x0, x1, x2, x3, tkeep_ref, tsend_ref, rel_ref, sums_ref, keep_ref, send_ref, acc):
    even = lax.rem(place[0], 2) == 0
    part = x0.shape[0]
    parts = ((x0, tkeep_ref, 0), (x2, tkeep_ref, part), (x1, tsend_ref, 0), (x3, tsend_ref, part))
    for number, (x, t, low) in enumerate(parts):
        value = lax.dot_general(x[...], t[low : low + part, :], (((0,), (0,)), ((), ())), preferred_element_type=F32)
        acc[...] = value if number == 0 else acc[...] + value
    notes = jnp.concatenate([sums_ref[0], sums_ref[1], sums_ref[2], jnp.zeros((8, 384), F32)], axis=1).astype(BF)

    def piece(f, s):
        value = acc[(8 * s + f) * 24 : (8 * s + f + 1) * 24, :]
        rel = rel_ref[96 * f + 24 * s : 96 * f + 24 * s + 24, :]
        return jnp.concatenate([value[:, 0:512], value[:, 512:640] + rel[:, 0:128], rel[:, 128:256]], axis=1)

    for g in range(4):
        slot = place[1 + g]
        for s in range(4):
            a, b = piece(2 * g, s), piece(2 * g + 1, s)
            keep_ref[slot, 24 * s : 24 * s + 24, :] = jnp.where(even, a, b).astype(BF)
            send_ref[slot, 24 * s : 24 * s + 24, :] = jnp.where(even, b, a).astype(BF)
        keep_ref[slot, 96:104, :] = notes
        send_ref[slot, 96:104, :] = notes


def qkv_blocks(place, pieces, tkeep, tsend, rel, sums):
    width = pieces[0].shape[1]
    out = jax.ShapeDtypeStruct((4, 104, width), BF)
    return pl.pallas_call(
        qkv_blocks_body,
        in_specs=[SM] + [VM] * 8,
        out_specs=[VM] * 2,
        out_shape=[out, out],
        scratch_shapes=[pltpu.VMEM((width, 640), F32)],
        compiler_params=pltpu.CompilerParams(vmem_limit_bytes=VMEM_LIMIT),
        cost_estimate=pl.CostEstimate(flops=2_000_000_000, bytes_accessed=8_000_000, transcendentals=0),
        name="qkv_blocks",
    )(place, *pieces, tkeep, tsend, rel, sums)


def merge_body(*refs):
    kb, cb, ki, ci, *more, out_ref = refs
    cut = kb.shape[1]
    back = kb[...].astype(F32) + cb[...].astype(F32)
    ins = ki[...].astype(F32) + ci[...].astype(F32)
    for m in more:
        back = back + m[:, :cut, :].astype(F32)
        ins = ins + m[:, cut:, :].astype(F32)
    out_ref[:, :cut, :] = back.astype(BF)
    out_ref[:, cut:, :] = ins.astype(BF)


def merge(parts, half):
    step = min(half, 2)
    first = half // step
    rows = parts[0].shape[1] + parts[2].shape[1]
    width = parts[0].shape[2]
    block = lambda p: pl.BlockSpec((step,) + p.shape[1:], lambda g: (first + g, 0, 0))
    return pl.pallas_call(
        merge_body,
        grid=(first,),
        in_specs=[block(p) for p in parts],
        out_specs=pl.BlockSpec((step, rows, width), lambda g: (g, 0, 0)),
        out_shape=jax.ShapeDtypeStruct((half, rows, width), BF),
        compiler_params=pltpu.CompilerParams(vmem_limit_bytes=VMEM_LIMIT, dimension_semantics=("arbitrary",)),
        cost_estimate=pl.CostEstimate(flops=half * rows * width * 6, bytes_accessed=half * rows * width * 8, transcendentals=0),
        name="merge",
    )(*parts)


EPS = 1e-09
GELU_A = (2.0 / 3.141592653589793) ** 0.5
GELU_B = 0.044715

def spread_norm(values):
    center = values - jnp.mean(values, axis=1, keepdims=True)
    inverse = lax.rsqrt(jnp.mean(center * center, axis=1, keepdims=True) + EPS)
    return center * inverse, inverse


def middle_body(
    place, a0, a1, a2, a3, x_ref, go_ref, w_ref, vec_ref, bin_ref,
    act_ref, h_ref, u_ref, dz_ref, df_ref, dbr_ref, dr_ref, d0, d1, d2, d3, sum_ref,
    wout, slope, high, normed, acc,
):
    own = place[0]
    width = x_ref.shape[1]
    cols = a0.shape[1]
    vector = lambda n: vec_ref[n : n + 1, :]
    for s in range(4):
        piece = w_ref[:, s, :, 2 * width : 2 * width + cols]
        wout[:, s * cols : (s + 1) * cols] = piece.reshape(width, cols)
    part = lambda mask: wout[pl.ds(pl.multiple_of((own ^ mask) * cols, 64), cols), :]
    masks = masks_of(place)
    total = x_ref[...].astype(F32) + vector(0)
    for mask, piece in zip(masks, (a0, a1, a2, a3)):
        total = total + jnp.dot(piece[...], part(mask), preferred_element_type=F32)
    unit, inverse_one = spread_norm(total)
    normed[...] = unit
    first = unit * vector(1) + vector(2)
    high[...] = first
    h_ref[...] = first.astype(BF)
    acc[...] = first + vector(3)

    def w_in_at(w):
        return w_ref[:, w, :, 0:width].reshape(width, width)

    def w_back_at(w):
        return w_ref[pl.ds(2 * w, 2), :, :, width : 2 * width].reshape(width, width)

    def forward(w, carry):
        at = pl.multiple_of(w * width, 128)
        z = jnp.dot(h_ref[...], w_in_at(w), preferred_element_type=F32) + bin_ref[:, pl.ds(at, width)]
        square = z * z
        bend = jnp.tanh(GELU_A * z * (1.0 + GELU_B * square))
        half = 0.5 + 0.5 * bend
        u = (z * half).astype(BF)
        u_ref[:, pl.ds(at, width)] = u
        slope[:, pl.ds(at, width)] = half + 0.5 * z * (1.0 - bend * bend) * (GELU_A * (1.0 + 3.0 * GELU_B * square))
        acc[...] += jnp.dot(u, w_back_at(w), preferred_element_type=F32)
        return carry

    lax.fori_loop(0, 4, forward, 0)
    unit, inverse_two = spread_norm(acc[...])
    act_ref[...] = (unit * vector(4) + vector(5)).astype(BF)

    def back(gradient, unit, inverse, gain):
        scaled = gradient * gain
        inner = scaled - jnp.mean(scaled, axis=1, keepdims=True)
        return (inner - unit * jnp.mean(scaled * unit, axis=1, keepdims=True)) * inverse

    def note(row, values):
        sum_ref[row : row + 1, :] = jnp.sum(values, axis=0, keepdims=True)

    gradient = go_ref[...].astype(F32)
    note(2, gradient * unit)
    note(3, gradient)
    second = back(gradient, unit, inverse_two, vector(4))
    df = second.astype(BF)
    df_ref[...] = df
    note(5, df.astype(F32))
    acc[...] = second

    def backward(w, carry):
        at = pl.multiple_of(w * width, 128)
        du = lax.dot_general(df_ref[...], w_back_at(w), (((1,), (1,)), ((), ())), preferred_element_type=F32)
        dz = (slope[:, pl.ds(at, width)] * du).astype(BF)
        dz_ref[:, pl.ds(at, width)] = dz
        sum_ref[pl.ds(8 + w, 1), :] = jnp.sum(dz.astype(F32), axis=0, keepdims=True)
        acc[...] += lax.dot_general(dz, w_in_at(w), (((1,), (1,)), ((), ())), preferred_element_type=F32)
        return carry

    lax.fori_loop(0, 4, backward, 0)
    gradient = acc[...]
    unit = normed[...]
    note(0, gradient * unit)
    note(1, gradient)
    dr = back(gradient, unit, inverse_one, vector(1))
    dr_ref[...] = dr
    dbr = dr.astype(BF)
    dbr_ref[...] = dbr
    note(4, dbr.astype(F32))
    sum_ref[6:8, :] = jnp.zeros((2, width), F32)
    sum_ref[12:16, :] = jnp.zeros((4, width), F32)
    for mask, out in zip(masks, (d0, d1, d2, d3)):
        value = lax.dot_general(dbr, part(mask), (((1,), (1,)), ((), ())), preferred_element_type=F32)
        out[...] = value.astype(BF)


def middle(place, pieces, x, out_grad, weights, vectors, bin_full):
    rows, width = x.shape
    cols = pieces[0].shape[1]
    hidden = bin_full.shape[1]
    low = lambda n: jax.ShapeDtypeStruct((rows, n), BF)
    full = lambda r, n: jax.ShapeDtypeStruct((r, n), F32)
    return pl.pallas_call(
        middle_body,
        in_specs=[SM] + [VM] * 9,
        out_specs=[VM] * 12,
        out_shape=[low(width), low(width), low(hidden), low(hidden), low(width), low(width), full(rows, width)]
        + [low(cols)] * 4
        + [full(16, width)],
        scratch_shapes=[
            pltpu.VMEM((width, width), BF),
            pltpu.VMEM((rows, hidden), F32),
            pltpu.VMEM((rows, width), F32),
            pltpu.VMEM((rows, width), F32),
            pltpu.VMEM((rows, width), F32),
        ],
        compiler_params=pltpu.CompilerParams(vmem_limit_bytes=VMEM_LIMIT),
        cost_estimate=pl.CostEstimate(flops=8_000_000_000, bytes_accessed=20_000_000, transcendentals=1_000_000),
        name="middle",
    )(place, *pieces, x, out_grad, weights, vectors, bin_full)


def angles_of(position, width):
    half_width = width // 2
    rate_table = 10000.0 ** (-(jnp.arange(half_width, dtype=jnp.float32) / half_width))
    turned = position.astype(jnp.float32)[:, None] * rate_table[None, :]
    return (jnp.sin(turned), jnp.cos(turned))


def contract_rows(left, right):
    return lax.dot_general(
        left, right, (((0,), (0,)), ((), ())), preferred_element_type=jnp.float32
    )


def contract_cols(left, right):
    return lax.dot_general(
        left, right, (((1,), (1,)), ((), ())), preferred_element_type=jnp.float32
    )


def across(values, other):
    seqs, fsdps = lax.axis_size("seq"), lax.axis_size("fsdp")
    pairs = []
    for s in range(seqs):
        for f in range(fsdps):
            to_s, to_f = other(s, f)
            pairs.append((s * fsdps + f, to_s * fsdps + to_f))
    return lax.ppermute(values, ("seq", "fsdp"), pairs)


def to_core(values):
    return across(values, lambda s, f: (s, f ^ 1))


def to_first(values):
    return across(values, lambda s, f: (s ^ (2 if f & 1 else 1), f))


def to_second(values):
    return across(values, lambda s, f: (s ^ (1 if f & 1 else 2), f))


def to_near(values):
    return across(values, lambda s, f: (s, f ^ 2))


def to_far(values):
    return across(values, lambda s, f: (s, f ^ 4))


def to_seq(values, k):
    return across(values, lambda s, f: (s ^ k, f))


def add_parts(parts, low, high):
    total = parts[0][low:high].astype(F32)
    for part in parts[1:]:
        total = total + part[low:high].astype(F32)
    return total


def outgoing(parts, count):
    return add_parts(parts, count // 2, count).astype(BF)


def back_blocks_body(place, u_ref, df_ref, keep_ref, send_ref):
    core = lax.rem(place[0], 2)
    group = u_ref.shape[1] // 4
    for g in range(1):
        acc = lax.dot_general(u_ref[...], df_ref[...], (((0,), (0,)), ((), ())), preferred_element_type=F32)
        at = pl.program_id(0) * 4
        for j in range(4):
            slot = place[1 + at + j]
            value = acc[j * group : (j + 1) * group].astype(BF)

            @pl.when(core == j % 2)
            def _():
                keep_ref[slot] = value

            @pl.when(core != j % 2)
            def _():
                send_ref[slot] = value


def back_blocks(place, u, df):
    rows, hidden = u.shape
    width = df.shape[1]
    out = jax.ShapeDtypeStruct((16, hidden // 32, width), BF)
    return pl.pallas_call(
        back_blocks_body,
        grid=(8,),
        in_specs=[SM, pl.BlockSpec((rows, hidden // 8), lambda g: (0, g)), pl.BlockSpec((rows, width), lambda g: (0, 0))],
        out_specs=[pl.BlockSpec((16, hidden // 32, width), lambda g: (0, 0, 0))] * 2,
        out_shape=[out, out],
        compiler_params=pltpu.CompilerParams(vmem_limit_bytes=VMEM_LIMIT, dimension_semantics=("arbitrary",)),
        cost_estimate=pl.CostEstimate(flops=2 * rows * hidden * width, bytes_accessed=8_000_000, transcendentals=0),
        name="back_blocks",
    )(place, u, df)


def in_blocks_body(place, h_ref, dz_ref, a_ref, db_ref, sum_ref, keep_ref, send_ref):
    even = lax.rem(place[0], 2) == 0
    core = lax.rem(place[0], 2)
    own = lax.div(place[0], 8)
    step = pl.program_id(0)

    def store(block, low, a, b):
        count = a.shape[0]
        keep_ref[place[1 + block + core], pl.ds(low, count), :] = jnp.where(even, a, b).astype(BF)
        send_ref[place[2 + block - core], pl.ds(low, count), :] = jnp.where(even, b, a).astype(BF)

    def put(block, low, acc):
        store(block, low, acc[0:24], acc[24:48])

    def chunk(which):
        for g in range(2):
            acc = lax.dot_general(
                h_ref[:, g * 384 : (g + 1) * 384], dz_ref[...], (((0,), (0,)), ((), ())), preferred_element_type=F32
            )
            for j in range(0, 16, 2):
                put(g * 16 + j, which * 24, acc[j * 24 : (j + 2) * 24])

    for which in range(4):
        pl.when(step == which)(lambda which=which: chunk(which))

    @pl.when(step == 4)
    def _():
        for g in range(2):
            acc = lax.dot_general(
                a_ref[:, g * 384 : (g + 1) * 384], db_ref[...], (((0,), (0,)), ((), ())), preferred_element_type=F32
            )
            for j in range(0, 16, 2):
                row = 2 * g + j // 8
                source = jnp.where(row == 0, 0, jnp.where(row == 3, 3, place[32 + row]))
                put((own ^ source) * 8 + j % 8, 96, acc[j * 24 : (j + 2) * 24])
        width = sum_ref.shape[1]
        line = lax.broadcasted_iota(jnp.int32, (8, width), 0)

        def note(j):
            wide = sum_ref[8 + j // 8 : 9 + j // 8, :] + jnp.zeros((8, width), F32)
            short, wide = (
                pltpu.roll(v, shift, 1) if shift % width else v
                for v, shift in ((sum_ref[0:8, :], width - 24 * j), (wide, width - 96 * (j % 8)))
            )
            return jnp.where(line == 6, wide, short)

        for j in range(0, 32, 2):
            store(j, 120, note(j), note(j + 1))


def in_blocks(place, hidden_low, dz, attn, dbr, sums):
    rows, width = hidden_low.shape
    chunks = dz.shape[1] // width
    out = jax.ShapeDtypeStruct((16, 128, width), BF)
    whole = pl.BlockSpec((rows, width), lambda g: (0, 0))
    return pl.pallas_call(
        in_blocks_body,
        grid=(chunks + 1,),
        in_specs=[SM, whole, pl.BlockSpec((rows, width), lambda g: (0, jnp.minimum(g, chunks - 1))), whole, whole]
        + [pl.BlockSpec(sums.shape, lambda g: (0, 0))],
        out_specs=[pl.BlockSpec((16, 128, width), lambda g: (0, 0, 0))] * 2,
        out_shape=[out, out],
        compiler_params=pltpu.CompilerParams(vmem_limit_bytes=VMEM_LIMIT, dimension_semantics=("arbitrary",)),
        cost_estimate=pl.CostEstimate(flops=2 * rows * width * (dz.shape[1] + width), bytes_accessed=12_000_000, transcendentals=0),
        name="in_blocks",
    )(place, hidden_low, dz, attn, dbr, sums)


def shards(
    inputs,
    w_query,
    w_key,
    w_value,
    b_value,
    w_out,
    b_out,
    norm1_gain,
    norm1_bias,
    w_in,
    b_in,
    w_back,
    b_back,
    norm2_gain,
    norm2_bias,
    w_relative,
    bias_content,
    bias_position,
    bias_type,
    type_embed,
    lengths,
    token_types,
    owners,
    grad_output,
):
    seqs, fsdps = lax.axis_size("seq"), lax.axis_size("fsdp")
    direct = seqs == 4 and fsdps == 8
    own, rank = lax.axis_index("seq"), lax.axis_index("fsdp")
    pack_count = owners.shape[0]
    sliver_rows = inputs.shape[1]
    width = inputs.shape[2]
    local_rows = w_query.shape[0]
    local_cols = width // seqs
    local_heads = w_relative.shape[1]
    scale = DH ** -0.5
    owner_table = owners[None, :] == jnp.arange(pack_count, dtype=jnp.int32)[:, None]
    owner_low = owner_table.astype(BF)
    dealt = jnp.dot(
        owner_low, inputs.reshape(pack_count, sliver_rows * width), preferred_element_type=F32
    )
    dealt = dealt.astype(BF).reshape(pack_count, sliver_rows, width)
    mine = lax.all_to_all(dealt, "fsdp", split_axis=0, concat_axis=1, tiled=True)[0]
    row_count = mine.shape[0]
    chosen = (owners == rank).astype(jnp.int32)
    pack_types = jnp.sum(chosen[:, None] * token_types, axis=0)
    pack_sizes = jnp.sum(chosen[:, None] * lengths, axis=0)
    pack_rows = pack_types.shape[0]

    def head_columns(weight):
        return lax.dynamic_slice_in_dim(weight, own * local_cols, local_cols, 1)

    block = jnp.concatenate(
        [head_columns(w) for w in (w_query, w_key, w_value)] + [w_relative.reshape(local_rows, local_cols)], axis=1
    )
    long_vectors = (b_value, b_out, norm1_gain, norm1_bias, b_back, norm2_gain, norm2_bias, b_in)
    head_vectors = (bias_content, bias_position, bias_type, type_embed[0], type_embed[1])

    def placed_at(value, row, lane):
        value = value.reshape(-1, value.shape[-1])
        return jnp.pad(value, ((row, 8 - row - value.shape[0]), (lane, width - lane - value.shape[1])))

    corner = placed_at(b_value, 0, 0)
    for number, value in enumerate(long_vectors[1:]):
        corner = corner + placed_at(value, number + 1, 0)
    for number, value in enumerate(head_vectors[:3]):
        corner = corner + placed_at(value, 0, (number + 3) * 128)
    for number, value in enumerate(head_vectors[3:]):
        corner = corner + placed_at(value, 3, (number + 3) * 128)
    early = lax.all_gather(jnp.concatenate([block, corner], axis=0), "fsdp", axis=0)
    qkvr = early[:, :local_rows].reshape(width, width)
    corners = early[:, local_rows:].astype(F32)
    full = [corners[:, n, : v.shape[0]].reshape(-1) for n, v in enumerate(long_vectors)]
    bv_full, bo_full, gain_one, shift_one, bback_full, gain_two, shift_two, bin_full = full
    heads = []
    for number, value in enumerate(head_vectors):
        row = 0 if number < 3 else 3
        lane = (number % 3 + 3) * 128
        each = corners[:, row : row + local_heads, lane : lane + value.shape[1]]
        heads.append(jnp.moveaxis(each, 0, 1).reshape(local_heads, DH))
    content_full, position_full, typebias_full, embed_zero, embed_one = heads
    bv_own = lax.dynamic_slice_in_dim(bv_full, own * local_cols, local_cols, 0)
    head = jnp.stack(
        [
            content_full,
            position_full,
            typebias_full,
            embed_zero,
            embed_one,
            bv_own.reshape(local_heads, DH),
        ],
        axis=1,
    )
    head = jnp.pad(head, ((0, 0), (0, 2), (0, 64)))

    deep = w_back.shape[0] // seqs
    late = jnp.concatenate(
        [
            lax.dynamic_slice_in_dim(w_in, own * width, width, 1),
            lax.dynamic_slice_in_dim(w_back, own * deep, deep, 0),
            head_columns(w_out),
            jnp.zeros((local_rows, 64), BF),
        ],
        axis=1,
    )
    late = lax.all_gather(late, ("fsdp", "seq"), axis=0).reshape(fsdps, seqs, local_rows, -1)
    if not direct:
        eighth_rows = width // 8
        turned_in = jnp.swapaxes(late, 1, 2).reshape(8, eighth_rows, seqs, -1)
        natural = late[..., width : 2 * width].reshape(8, seqs, eighth_rows, width)
        turned_in = jnp.swapaxes(turned_in, 1, 2)
        late = jnp.concatenate([turned_in[..., :width], natural, turned_in[..., 2 * width :]], axis=-1)

    longest = jnp.argmax(pack_sizes).astype(jnp.int32)
    start = jnp.sum(jnp.where(jnp.arange(3) < longest, pack_sizes, 0))
    near = jnp.sum(jnp.where(jnp.arange(3) == (longest + 1) % 3, pack_sizes, 0))
    parity = rank & 1
    place = jnp.stack([own, start, near, 1 + parity, 2 - parity]).astype(jnp.int32)
    row_index = jnp.arange(pack_rows, dtype=jnp.int32)
    position = jnp.where(
        row_index < LONGEST,
        row_index,
        jnp.where(row_index < LONGEST + near, row_index - LONGEST, row_index - LONGEST - near),
    )
    sine, cosine = angles_of(position, width)
    key_pos = jnp.concatenate([cosine, sine], axis=-1).astype(BF)
    key_pos_t = key_pos.T
    turned_types = lax.dynamic_slice_in_dim(
        jnp.concatenate([pack_types, pack_types]), start, pack_rows, 0
    )[:, None]
    wrel = qkvr[:, 3 * local_cols :].reshape(width, local_heads, DH)
    wrel_rows = jnp.pad(jnp.transpose(wrel, (1, 0, 2)), ((0, 0), (0, 0), (0, 64)))
    wrel_cols = jnp.pad(jnp.transpose(wrel, (1, 2, 0)), ((0, 0), (0, 64), (0, 0)))
    together = lambda n: qkvr[:, n * local_cols : (n + 1) * local_cols].reshape(width, local_heads, DH)
    paired = jnp.concatenate([together(0), together(1)], axis=2).reshape(width, 2 * local_cols)
    w_qkv = jnp.concatenate([paired, qkvr[:, 2 * local_cols : 3 * local_cols], jnp.zeros((width, 64), BF)], axis=1)

    pieces = [mine, to_first(mine), to_second(mine)]
    pieces.append(to_second(pieces[1]))
    qx, pq, kx, kxt, vx, vxt = project(place, pieces, w_qkv, head, turned_types)
    big, small, ox, *head_out = attend(place, qx, pq, kxt, vx, key_pos_t, wrel_cols, sine, cosine)
    order = own ^ jnp.arange(seqs, dtype=jnp.int32)
    deal = lambda v: [v[0], to_first(v[1]), to_second(v[2]), to_seq(v[3], 3)]
    attn = deal(head_out)
    mid_vectors = jnp.stack([bo_full, gain_one, shift_one, bback_full, gain_two, shift_two, gain_two, gain_two])
    result, hidden_low, act_low, pre_grad, ffn_grad, branch_grad, sum_one_grad, *douts, short_sums = middle(
        place, attn, mine, grad_output[0], late, mid_vectors, bin_full[None]
    )
    activations = result.reshape(1, row_count, width)
    douts = deal(douts)
    attn_rows = jnp.concatenate(attn, axis=1)
    devices = seqs * fsdps
    device = own * fsdps + rank
    fine = width // devices
    deep = act_low.shape[1] // devices
    kept_place = jnp.where((order == 1) | (order == 2), jnp.where(parity == 1, 3 - order, order), order)
    if direct:
        relative = jnp.arange(32, dtype=jnp.int32) ^ device
        bit = lambda n: (relative >> n) & 1
        flip = (bit(0) ^ parity) == 1
        one, two = jnp.where(flip, bit(4), bit(3)), jnp.where(flip, bit(3), bit(4))
        slots = one * 8 + two * 4 + bit(1) * 2 + bit(2)
        table = jnp.concatenate([device[None], slots, place[3:5]]).astype(jnp.int32)
        kept_in, sent_in = in_blocks(table, hidden_low, pre_grad, attn_rows, branch_grad, short_sums)
        core_in = to_core(sent_in)
        kept_back, sent_back = back_blocks(table, act_low, ffn_grad)
        parts = [kept_back, to_core(sent_back), kept_in, core_in]
        out = merge(parts, 8)
        douts, out = lax.optimization_barrier((douts, out))
        parts.append(to_first(out))
    else:
        scatter = lambda v: lax.psum_scatter(v, ("seq", "fsdp"), scatter_dimension=0, tiled=True)
        w_back_grad = scatter(contract_rows(act_low, ffn_grad))
        w_in_grad = scatter(contract_rows(hidden_low, pre_grad))
        spun = contract_rows(attn_rows, branch_grad).reshape(seqs, local_cols, width)
        w_out_grad = scatter(jnp.take(spun, kept_place, axis=0).reshape(width, width))

    tkeep, tsend, rel, sums = attend_back(
        place, douts, big, small, ox, qx, pq, kx, vxt, key_pos, wrel_rows, sine, cosine, turned_types, head
    )
    if direct:
        out = merge(parts, 4)
        tkeep, tsend, out = lax.optimization_barrier((tkeep, tsend, out))
        parts.append(to_second(out))
    dx_send = contract_cols(tsend, w_qkv).astype(BF)
    tkeep, tsend, dx_send = lax.optimization_barrier((tkeep, tsend, dx_send))
    dx_first = to_first(dx_send)
    dx_keep = contract_cols(tkeep, w_qkv)
    dx_out = (dx_keep[row_count:] + dx_first[row_count:].astype(F32)).astype(BF)
    if direct:
        spots = ((rank >> 1) ^ jnp.arange(4, dtype=jnp.int32)) & 3
        spots = (spots & 1) * 2 + (spots >> 1)
        qkv_table = jnp.concatenate([rank[None], spots]).astype(jnp.int32)
        kept, sent = qkv_blocks(qkv_table, pieces, tkeep, tsend, rel, sums)
        qkv_parts = [kept, to_core(sent)]
        dx_out, qkv_parts = lax.optimization_barrier((dx_out, qkv_parts))
    dx_second = to_second(dx_out)
    if direct:
        qkv_parts.append(to_near(outgoing(qkv_parts, 4)))
        parts.append(to_near(merge(parts, 2)))
    input_rows = sum_one_grad + dx_keep[:row_count] + dx_first[:row_count].astype(F32) + dx_second.astype(F32)
    input_rows = input_rows.astype(BF).reshape(fsdps, sliver_rows, width)
    if direct:
        input_rows, qkv_parts, parts = lax.optimization_barrier((input_rows, qkv_parts, parts))
    returned = lax.all_to_all(input_rows, "fsdp", split_axis=0, concat_axis=0, tiled=True)
    input_grad = reload(owners, returned)
    if direct:
        qkv_parts.append(to_far(outgoing(qkv_parts, 2)))
        parts.append(to_far(merge(parts, 1)))
        total = add_parts(qkv_parts, 0, 1)[0]
        cut = kept_back.shape[1]
        tails = [p[:, :cut] for p in parts[4:]]
        w_back_grad = add_parts(parts[:2] + tails, 0, 1)[0]
        tails = [p[:, cut:] for p in parts[4:]]
        in_total = add_parts(parts[2:4] + tails, 0, 1)[0]
        w_in_grad = jnp.concatenate([in_total[c * 24 : (c + 1) * 24] for c in range(4)], axis=1)
        w_out_grad = in_total[96:120]
        short_grads, in_bias_grad = in_total[120:128, :fine], in_total[126, :deep]
    else:
        short_sums = lax.psum(short_sums, ("seq", "fsdp"))
        short_grads = lax.dynamic_slice(short_sums, (0, device * fine), (8, fine))
        in_bias_grad = lax.dynamic_slice(short_sums, (8 + device * deep // width, device * deep % width), (1, deep))[0]
        grad = contract_rows(pieces[0], tkeep[:row_count]) + contract_rows(pieces[2], tkeep[row_count:])
        grad = grad + contract_rows(pieces[1], tsend[:row_count]) + contract_rows(pieces[3], tsend[row_count:])
        grad = jnp.swapaxes(grad.reshape(seqs, fsdps, fine, 640), 0, 1).reshape(fsdps, local_rows, 640)
        tall = rel.reshape(fsdps, local_rows, 256)
        bundle = jnp.concatenate([grad[..., :512], grad[..., 512:] + tall[..., :128], tall[..., 128:]], axis=2)
        notes = jnp.concatenate([sums[0], sums[1], sums[2], jnp.zeros((8, 384), F32)], axis=1)
        bundle = jnp.concatenate([bundle, jnp.broadcast_to(notes[None], (fsdps,) + notes.shape)], axis=1)
        total = lax.psum_scatter(bundle, "fsdp", scatter_dimension=0, tiled=True)[0]
    own_qkv = total[:local_rows].astype(BF).reshape(seqs, fine, width)
    block_for = lambda mask: lax.dynamic_index_in_dim(own_qkv, own ^ mask, 0, keepdims=True)
    swapped = jnp.concatenate(deal([block_for(m) for m in (0, place[3], place[4], 3)]), axis=0)
    swapped = jnp.take(swapped, kept_place, axis=0).astype(F32)
    both = swapped[:, :, : 2 * local_cols].reshape(seqs, fine, local_heads, 2, DH)
    both = jnp.transpose(both, (3, 1, 0, 2, 4)).reshape(2, fine, width)
    w_value_grad = jnp.transpose(swapped[:, :, 2 * local_cols : 3 * local_cols], (1, 0, 2)).reshape(fine, width)
    rel_total = total[:local_rows, 3 * local_cols :].reshape(local_rows, local_heads, DH)
    notes = total[local_rows:, :384].reshape(8, 3, 128)
    eighth = DH // fsdps
    mine_sums = lax.dynamic_slice(notes, (0, 0, rank * eighth), (8, 3, eighth))
    value_bias_grad = lax.dynamic_slice(notes[5, :, :DH].reshape(-1), (rank * fine,), (fine,))
    return (
        activations,
        input_grad,
        both[0],
        both[1],
        w_value_grad,
        value_bias_grad,
        w_out_grad,
        short_grads[4],
        short_grads[0],
        short_grads[1],
        w_in_grad,
        in_bias_grad,
        w_back_grad,
        short_grads[5],
        short_grads[2],
        short_grads[3],
        rel_total,
        mine_sums[0],
        mine_sums[1],
        mine_sums[2],
        mine_sums[3:5],
    )


def solution(mesh):
    placed = (
        P(None, ("seq", "fsdp"), None),
        P("fsdp", None),
        P("fsdp", None),
        P("fsdp", None),
        P("fsdp"),
        P("fsdp", None),
        P("fsdp"),
        P("fsdp"),
        P("fsdp"),
        P("fsdp", None),
        P("fsdp"),
        P("fsdp", None),
        P("fsdp"),
        P("fsdp"),
        P("fsdp"),
        P("fsdp", "seq", None),
        P("seq", "fsdp"),
        P("seq", "fsdp"),
        P("seq", "fsdp"),
        P(None, "seq", "fsdp"),
        P(),
        P(),
        P(),
        P("fsdp", "seq", None),
    )
    return jax.shard_map(
        shards,
        mesh=mesh,
        in_specs=placed,
        out_specs=(
            P("fsdp", "seq", None),
            P(None, ("seq", "fsdp"), None),
            P(("seq", "fsdp"), None),
            P(("seq", "fsdp"), None),
            P(("seq", "fsdp"), None),
            P(("seq", "fsdp")),
            P(("seq", "fsdp"), None),
            P(("seq", "fsdp")),
            P(("seq", "fsdp")),
            P(("seq", "fsdp")),
            P(("seq", "fsdp"), None),
            P(("seq", "fsdp")),
            P(("seq", "fsdp"), None),
            P(("seq", "fsdp")),
            P(("seq", "fsdp")),
            P(("seq", "fsdp")),
            P("fsdp", "seq", None),
            P("seq", "fsdp"),
            P("seq", "fsdp"),
            P("seq", "fsdp"),
            P(None, "seq", "fsdp"),
        ),
        check_vma=False,
    )
```

profile of v0, /device:TPU:0, one launch (start us, length us, event | category | flops | bytes accessed | tf_op | source)
XLA Modules:
  0.0 360.6 jit_solution(2166944731268875769)
XLA Ops:
  16.7 6.4 %all-to-all-start = ((bf16[8,48,768]{2,1,0:T(8,128)(2,1)}), bf16[8,48,768]{2,1,0:T(8,128)(2,1)}, u32[]{:S(2)}, u32[]{:S(2)}) async-start(bf16[8,48,768]{2,1,0:T(8,128)(2,1)} %copy.66), calls=%async_computation | async-start | bytes 1179648 | tf_op jit(solution)/shard_map/all_to_all | solution.py:794
  30.4 10.4 %multiply_cosine_fusion = (f32[1536,384]{1,0:T(8,128)}, bf16[1536,384]{1,0:T(8,128)(2,1)S(1)}, bf16[1536,384]{1,0:T(8,128)(2,1)}, f32[1536,384]{1,0:T(8,128)}) fusion(f32[384]{0:T(512)S(1)} %negate_power_fusion, f32[1536]{0:T(1024)S(1)} %fusion.7), kind=kLoop, calls=%fused_computation.3 | loop fusion | flops 1769472 | bytes 7085568 | tf_op jit(solution)/shard_map/cos | solution.py:589
  40.9 8.4 %all-to-all-done = bf16[8,48,768]{2,1,0:T(8,128)(2,1)} async-done(((bf16[8,48,768]{2,1,0:T(8,128)(2,1)}), bf16[8,48,768]{2,1,0:T(8,128)(2,1)}, u32[]{:S(2)}, u32[]{:S(2)}) %all-to-all-start) | async-done | bytes 589856 | tf_op jit(solution)/shard_map/all_to_all | solution.py:794
  49.3 1.5 collective-permute-start
  50.7 3.0 pad_maximum_fusion
  53.8 2.4 copy.74.kpt_ref
  56.3 1.9 stack.29.place
  58.8 1.5 collective-permute-start.1
  61.0 1.4 slice.323
  67.8 3.6 %collective-permute-done.1.x2 = bf16[384,768]{1,0:T(8,128)(2,1)} collective-permute-done((bf16[384,768]{1,0:T(8,128)(2,1)}, bf16[384,768]{1,0:T(8,128)(2,1)}, u32[]{:S(2)}, u32[]{:S(2)}) %collective-permute-start.1) | collective-permute-done | bytes 589856 | tf_op jit(solution)/shard_map/ppermute | solution.py:611
  71.5 6.3 %collective-permute-done.2.x3 = bf16[384,768]{1,0:T(8,128)(2,1)} collective-permute-done((bf16[384,768]{1,0:T(8,128)(2,1)}, bf16[384,768]{1,0:T(8,128)(2,1)}, u32[]{:S(2)}, u32[]{:S(2)}) %collective-permute-start.2) | collective-permute-done | bytes 589856 | tf_op jit(solution)/shard_map/ppermute | solution.py:611
  77.8 13.9 %project.1 = (bf16[3,1536,128]{2,1,0:T(8,128)(2,1)}, bf16[3,1536,128]{2,1,0:T(8,128)(2,1)}, bf16[3,1536,128]{2,1,0:T(8,128)(2,1)}, bf16[3,128,1536]{2,1,0:T(8,12...) custom-call(s32[5]{0:T(128)} %stack.29.place, bf16[384,768]{1,0:T(8,128)(2,1)} %bitcast.6.x0.x_ref, ...), custom_call_target="tpu_custom_call" | custom-call | flops 1509949440 | bytes 10000000 | tf_op jit(solution)/shard_map/project/pallas_call | solution.py:98
  91.7 30.1 %attend.1 = (bf16[3,1024,1024]{2,1,0:T(8,128)(2,1)}, bf16[3,512,512]{2,1,0:T(8,128)(2,1)}, f32[3,1536,128]{2,1,0:T(8,128)}, bf16[384,192]{1,0:T(8,128)(2,1)}, bf...) custom-call(s32[5]{0:T(128)} %stack.29.place, ...), custom_call_target="tpu_custom_call" | custom-call | flops 12000000000 | bytes 20000000 | tf_op jit(solution)/shard_map/attend/pallas_call | solution.py:173
  122.4 1.5 collective-permute-start.4
  123.9 1.4 collective-permute-start.5
  127.1 3.5 collective-permute-done.3.a1
  130.6 4.5 %collective-permute-done.5.a3 = bf16[384,192]{1,0:T(8,128)(2,1)S(1)} collective-permute-done((bf16[384,192]{1,0:T(8,128)(2,1)}, bf16[384,192]{1,0:T(8,128)(2,1)S(1)}, u32[]{:S(2)}, u32[]{:S(2)}) %collective-permute-start.5) | collective-permute-done | bytes 147488 | tf_op jit(solution)/shard_map/ppermute | solution.py:611
  135.2 2.1 pad_maximum_fusion.2.a_ref
  137.3 7.9 %all-gather.7.cloned.1.call-done = bf16[3072,1792]{1,0:T(8,128)(2,1)} async-done(((bf16[96,1792]{1,0:T(8,128)(2,1)}), bf16[3072,1792]{1,0:T(8,128)(2,1)}) %all-gather.7.cloned.1.call-update) | async-done | bytes 11010064 | tf_op jit(solution)/shard_map/all_gather | solution.py:857
  145.2 22.3 %middle.1 = (bf16[384,768]{1,0:T(8,128)(2,1)}, bf16[384,768]{1,0:T(8,128)(2,1)}, bf16[384,3072]{1,0:T(8,128)(2,1)}, bf16[384,3072]{1,0:T(8,128)(2,1)}, bf16[384,...) custom-call(s32[5]{0:T(128)} %stack.29.place, ...), custom_call_target="tpu_custom_call" | custom-call | flops 8000000000 | bytes 20000000 | tf_op jit(solution)/shard_map/middle/pallas_call | solution.py:565
  167.5 8.9 %in_blocks.1 = (bf16[16,128,768]{2,1,0:T(8,128)(2,1)}, bf16[16,128,768]{2,1,0:T(8,128)(2,1)}) custom-call(s32[35]{0:T(128)} %pad_add_fusion.1.place, bf16[384,768]{1,0:T(8,128)(2,1)} %get-tuple-element.101.h_ref, bf16[384,3072]{1,0:T(8,128)(2,1)} %get-tuple-element.102.dz_ref, bf16[384,768]{1,0:T(8,128)(2,1)} %pad_maximum_fusion.2.a_ref, ...), custom_call_target="tpu_custom_call" | custom-call | flops 2264924160 | bytes 12000000 | tf_op jit(solution)/shard_map/in_blocks/pallas_call | solution.py:739
  176.6 9.3 %back_blocks.1 = (bf16[16,96,768]{2,1,0:T(8,128)(2,1)}, bf16[16,96,768]{2,1,0:T(8,128)(2,1)}) custom-call(s32[35]{0:T(128)} %pad_add_fusion.1.place, bf16[384,3072]{1,0:T(8,128)(2,1)} %get-tuple-element.97.u_ref, bf16[384,768]{1,0:T(8,128)(2,1)} %get-tuple-element.98.df_ref), custom_call_target="tpu_custom_call" | custom-call | flops 1811939328 | bytes 8000000 | tf_op jit(solution)/shard_map/back_blocks/pallas_call | solution.py:672
  187.7 1.9 collective-permute-start.8
  190.7 1.4 copy-done.3
  192.1 1.7 copy-done.2
  193.8 4.8 %merge.4 = bf16[8,224,768]{2,1,0:T(8,128)(2,1)} custom-call(bf16[16,96,768]{2,1,0:T(8,128)(2,1)} %get-tuple-element.141.refs_0_, bf16[16,96,768]{2,1,0:T(8,128)(2,1)} %copy-done.3, bf16[16,128,768]{2,1,0:T(8,128)(2,1)} %get-tuple-element.136.refs_2_, bf16[16,128,768]{2,1,0:T(8,128)(2,1)} %copy-done.2), custom_call_target="tpu_custom_call" | custom-call | flops 8257536 | bytes 11010048 | tf_op jit(solution)/shard_map/merge/pallas_call | solution.py:448
  201.5 2.0 pad.79.wr_ref
  203.5 36.3 %attend_back.1 = (bf16[768,640]{1,0:T(8,128)(2,1)}, bf16[768,640]{1,0:T(8,128)(2,1)}, f32[768,256]{1,0:T(8,128)}, f32[3,8,128]{2,1,0:T(8,128)}) custom-call(s32[5]{0:T(128)} %stack.29.place, bf16[384,192]{1,0:T(8,128)(2,1)} %get-tuple-element.107.d0, bf16[384,192]{1,0:T(8,128)(2,1)} %copy-done.22, bf16[384,192]{1,0:T(8,128)(2,1)} %collective-permute-done.7.d2, ...), custom_call_target="tpu_custom_call" | custom-call | flops 20000000000 | bytes 25000000 | tf_op jit(solution)/shard_map/attend_back/pallas_call | solution.py:335
  239.9 1.6 copy-done.4
  241.5 3.2 merge.5
  244.7 3.8 %convolution_convert_fusion.1 = bf16[768,768]{1,0:T(8,128)(2,1)} fusion(bf16[768,640]{1,0:T(8,128)(2,1)} %get-tuple-element.123.tsend_ref, bf16[768,640]{1,0:T(8,128)(2,1)} %maximum_maximum_fusion.w_ref), kind=kOutput, calls=%fused_computation.5 | convolution fusion | flops 755564544 | bytes 3145728 | tf_op jit(solution)/shard_map/dot_general | solution.py:599
  249.3 1.5 collective-permute-start.16
  251.4 6.0 %qkv_blocks.1 = (bf16[4,104,768]{2,1,0:T(8,128)(2,1)}, bf16[4,104,768]{2,1,0:T(8,128)(2,1)}) custom-call(s32[5]{0:T(128)} %pad_add_fusion.2.place, bf16[384,768]{1,0:T(8,128)(2,1)} %bitcast.6.x0.x_ref, bf16[384,768]{1,0:T(8,128)(2,1)} %collective-permute-done.x1, bf16[384,768]{1,0:T(8,128)(2,1)} %collective-permute-done.1.x2, ...), custom_call_target="tpu_custom_call" | custom-call | flops 2000000000 | bytes 8000000 | tf_op jit(solution)/shard_map/qkv_blocks/pallas_call | solution.py:418
  257.5 4.1 %fusion.21 = f32[768,768]{1,0:T(8,128)} fusion(bf16[768,640]{1,0:T(8,128)(2,1)} %get-tuple-element.121.tkeep_ref, bf16[768,640]{1,0:T(8,128)(2,1)} %maximum_maximum_fusion.w_ref), kind=kOutput, calls=%fused_computation.111 | convolution fusion | flops 754974720 | bytes 4325376 | tf_op jit(solution)/shard_map/dot_general | solution.py:599
  261.5 16.1 %collective-permute-done.12 = bf16[768,768]{1,0:T(8,128)(2,1)} collective-permute-done((bf16[768,768]{1,0:T(8,128)(2,1)}, bf16[768,768]{1,0:T(8,128)(2,1)}, u32[]{:S(2)}, u32[]{:S(2)}) %collective-permute-start.12) | collective-permute-done | bytes 1179680 | tf_op jit(solution)/shard_map/ppermute | solution.py:611
  277.7 2.4 fusion
  281.2 3.1 merge.6
  285.8 1.6 collective-permute-start.15
  287.4 2.8 collective-permute-done.14
  290.3 2.6 fusion.3
  292.9 14.8 %collective-permute-done.15 = bf16[2,104,768]{2,1,0:T(8,128)(2,1)S(1)} collective-permute-done((bf16[2,104,768]{2,1,0:T(8,128)(2,1)S(1)}, bf16[2,104,768]{2,1,0:T(8,128)(2,1)S(1)}, u32[]{:S(2)}, u32[]{:S(2)}) %collective-permute-start.15) | collective-permute-done | bytes 319520 | tf_op jit(solution)/shard_map/ppermute | solution.py:611
  310.1 3.6 all-to-all-start.1
  313.8 2.5 merge.7
  316.2 2.9 collective-permute-start.22
  321.4 1.4 collective-permute-start.20
  331.4 13.8 %collective-permute-done.22 = bf16[1,224,768]{2,1,0:T(8,128)(2,1)S(1)} collective-permute-done((bf16[1,224,768]{2,1,0:T(8,128)(2,1)}, bf16[1,224,768]{2,1,0:T(8,128)(2,1)S(1)}, u32[]{:S(2)}, u32[]{:S(2)}) %collective-permute-start.22) | collective-permute-done | bytes 344096 | tf_op jit(solution)/shard_map/ppermute | solution.py:611
  348.3 1.9 add_bitcast_fusion
  351.8 2.0 reload.1
  (177 shorter events, 50.5 us)
Async XLA Ops:
  7.2 2.4 copy-start
  7.2 8.1 %copy-start.12 = (bf16[8,48,768]{2,1,0:T(8,128)(2,1)S(1)}, bf16[8,48,768]{2,1,0:T(8,128)(2,1)}, u32[]{:S(2)}) copy-start(bf16[8,48,768]{2,1,0:T(8,128)(2,1)} %param.24) | copy-start | bytes 1769476
  7.2 53.7 %all-gather.5.cloned.1.call-start = ((), (), s32[]{:S(2)}) async-start(), calls=%async_computation.2 | async-start | bytes 1437696 | tf_op jit(solution)/shard_map/all_gather | solution.py:821
  12.4 3.1 copy-start.19
  12.4 132.8 %all-gather.7.cloned.1.call-start = ((), (), s32[]{:S(2)}) async-start(), calls=%async_computation.3 | async-start | bytes 11354112 | tf_op jit(solution)/shard_map/all_gather | solution.py:857
  15.5 7.6 %copy-start.20 = (s32[8,3]{0,1:T(4,128)S(1)}, s32[8,3]{0,1:T(4,128)}, u32[]{:S(2)}) copy-start(s32[8,3]{0,1:T(4,128)} %param.44) | copy-start | bytes 292
  15.5 9.0 %copy-start.18 = (s32[8,1536]{1,0:T(8,128)S(1)}, s32[8,1536]{1,0:T(8,128)}, u32[]{:S(2)}) copy-start(s32[8,1536]{1,0:T(8,128)} %param.45) | copy-start | bytes 147460
  16.7 32.5 %all-to-all-start = ((bf16[8,48,768]{2,1,0:T(8,128)(2,1)}), bf16[8,48,768]{2,1,0:T(8,128)(2,1)}, u32[]{:S(2)}, u32[]{:S(2)}) async-start(bf16[8,48,768]{2,1,0:T(8,128)(2,1)} %copy.66), calls=%async_computation | async-start | bytes 1179648 | tf_op jit(solution)/shard_map/all_to_all | solution.py:794
  49.3 11.0 %collective-permute-start = (bf16[384,768]{1,0:T(8,128)(2,1)}, bf16[384,768]{1,0:T(8,128)(2,1)}, u32[]{:S(2)}, u32[]{:S(2)}) collective-permute-start(bf16[384,768]{1,0:T(8,128)(2,1)} %bitcast.6.x0.x_ref), channel_id=1, source_target_pairs={{0,8},{1,17},{2,10},{3,19},{4,12},{5,21},{6,14},{7,23},{8,0},{9,25... | collective-permute-start | bytes 1769480 | tf_op jit(solution)/shard_map/ppermute | solution.py:611
  58.8 12.7 %collective-permute-start.1 = (bf16[384,768]{1,0:T(8,128)(2,1)}, bf16[384,768]{1,0:T(8,128)(2,1)}, u32[]{:S(2)}, u32[]{:S(2)}) collective-permute-start(bf16[384,768]{1,0:T(8,128)(2,1)} %bitcast.6.x0.x_ref), channel_id=1, source_target_pairs={{0,16},{1,9},{2,18},{3,11},{4,20},{5,13},{6,22},{7,15},{8,24},{9,1... | collective-permute-start | bytes 1769480 | tf_op jit(solution)/shard_map/ppermute | solution.py:611
  60.3 17.5 %collective-permute-start.2 = (bf16[384,768]{1,0:T(8,128)(2,1)}, bf16[384,768]{1,0:T(8,128)(2,1)}, u32[]{:S(2)}, u32[]{:S(2)}) collective-permute-start(bf16[384,768]{1,0:T(8,128)(2,1)} %collective-permute-done.x1), channel_id=1, source_target_pairs={{0,16},{1,9},{2,18},{3,11},{4,20},{5,13},{6,22},{7,15},{8,24},{9,1... | collective-permute-start | bytes 1769480 | tf_op jit(solution)/shard_map/ppermute | solution.py:611
  121.8 8.8 %collective-permute-start.3 = (bf16[384,192]{1,0:T(8,128)(2,1)}, bf16[384,192]{1,0:T(8,128)(2,1)S(1)}, u32[]{:S(2)}, u32[]{:S(2)}) collective-permute-start(bf16[384,192]{1,0:T(8,128)(2,1)} %get-tuple-element.88), channel_id=1, source_target_pairs={{0,8},{1,17},{2,10},{3,19},{4,12},{5,21},{6,14},{7,23},{8,0},{9,25... | collective-permute-start | bytes 442376 | tf_op jit(solution)/shard_map/ppermute | solution.py:611
  122.4 8.2 %collective-permute-start.4 = (bf16[384,192]{1,0:T(8,128)(2,1)}, bf16[384,192]{1,0:T(8,128)(2,1)S(1)}, u32[]{:S(2)}, u32[]{:S(2)}) collective-permute-start(bf16[384,192]{1,0:T(8,128)(2,1)} %get-tuple-element.89), channel_id=1, source_target_pairs={{0,16},{1,9},{2,18},{3,11},{4,20},{5,13},{6,22},{7,15},{8,24},{9,1... | collective-permute-start | bytes 442376 | tf_op jit(solution)/shard_map/ppermute | solution.py:611
  123.9 11.3 %collective-permute-start.5 = (bf16[384,192]{1,0:T(8,128)(2,1)}, bf16[384,192]{1,0:T(8,128)(2,1)S(1)}, u32[]{:S(2)}, u32[]{:S(2)}) collective-permute-start(bf16[384,192]{1,0:T(8,128)(2,1)} %get-tuple-element.90), channel_id=1, source_target_pairs={{0,24},{1,25},{2,26},{3,27},{4,28},{5,29},{6,30},{7,31},{8,16},{9,... | collective-permute-start | bytes 442376 | tf_op jit(solution)/shard_map/ppermute | solution.py:611
  130.6 14.6 %copy-start.15 = (bf16[384,192]{1,0:T(8,128)(2,1)}, bf16[384,192]{1,0:T(8,128)(2,1)S(1)}, u32[]{:S(2)}) copy-start(bf16[384,192]{1,0:T(8,128)(2,1)S(1)} %collective-permute-done.3.a1) | copy-start | bytes 442372
  130.6 14.6 %copy-start.16 = (bf16[384,192]{1,0:T(8,128)(2,1)}, bf16[384,192]{1,0:T(8,128)(2,1)S(1)}, u32[]{:S(2)}) copy-start(bf16[384,192]{1,0:T(8,128)(2,1)S(1)} %collective-permute-done.4.a2) | copy-start | bytes 442372
  135.2 10.0 %copy-start.17 = (bf16[384,192]{1,0:T(8,128)(2,1)}, bf16[384,192]{1,0:T(8,128)(2,1)S(1)}, u32[]{:S(2)}) copy-start(bf16[384,192]{1,0:T(8,128)(2,1)S(1)} %collective-permute-done.5.a3) | copy-start | bytes 442372
  176.4 14.3 %collective-permute-start.10 = (bf16[16,128,768]{2,1,0:T(8,128)(2,1)}, bf16[16,128,768]{2,1,0:T(8,128)(2,1)S(1)}, u32[]{:S(2)}, u32[]{:S(2)}) collective-permute-start(bf16[16,128,768]{2,1,0:T(8,128)(2,1)} %get-tuple-element.106), channel_id=1, source_target_pairs={{0,1},{1,0},{2,3},{3,2},{4,5},{5,4},{6,7},{7,6},{8,9},{9,8},{10,11... | collective-permute-start | bytes 9437192 | tf_op jit(solution)/shard_map/ppermute | solution.py:611
  176.6 11.1 %copy-start.21 = (bf16[384,192]{1,0:T(8,128)(2,1)S(1)}, bf16[384,192]{1,0:T(8,128)(2,1)}, u32[]{:S(2)}) copy-start(bf16[384,192]{1,0:T(8,128)(2,1)} %get-tuple-element.96) | copy-start | bytes 442372
  185.9 4.7 %collective-permute-start.9 = (bf16[16,96,768]{2,1,0:T(8,128)(2,1)}, bf16[16,96,768]{2,1,0:T(8,128)(2,1)S(1)}, u32[]{:S(2)}, u32[]{:S(2)}) collective-permute-start(bf16[16,96,768]{2,1,0:T(8,128)(2,1)} %get-tuple-element.100), channel_id=1, source_target_pairs={{0,1},{1,0},{2,3},{3,2},{4,5},{5,4},{6,7},{7,6},{8,9},{9,8},{10,11... | collective-permute-start | bytes 7077896 | tf_op jit(solution)/shard_map/ppermute | solution.py:611
  186.2 12.4 %collective-permute-start.6 = (bf16[384,192]{1,0:T(8,128)(2,1)}, bf16[384,192]{1,0:T(8,128)(2,1)S(1)}, u32[]{:S(2)}, u32[]{:S(2)}) collective-permute-start(bf16[384,192]{1,0:T(8,128)(2,1)} %get-tuple-element.94), channel_id=1, source_target_pairs={{0,8},{1,17},{2,10},{3,19},{4,12},{5,21},{6,14},{7,23},{8,0},{9,25... | collective-permute-start | bytes 442376 | tf_op jit(solution)/shard_map/ppermute | solution.py:611
  187.4 11.1 %collective-permute-start.7 = (bf16[384,192]{1,0:T(8,128)(2,1)}, bf16[384,192]{1,0:T(8,128)(2,1)}, u32[]{:S(2)}, u32[]{:S(2)}) collective-permute-start(bf16[384,192]{1,0:T(8,128)(2,1)} %get-tuple-element.95), channel_id=1, source_target_pairs={{0,16},{1,9},{2,18},{3,11},{4,20},{5,13},{6,22},{7,15},{8,24},{9,1... | collective-permute-start | bytes 442376 | tf_op jit(solution)/shard_map/ppermute | solution.py:611
  187.7 11.2 %collective-permute-start.8 = (bf16[384,192]{1,0:T(8,128)(2,1)S(1)}, bf16[384,192]{1,0:T(8,128)(2,1)}, u32[]{:S(2)}, u32[]{:S(2)}) collective-permute-start(bf16[384,192]{1,0:T(8,128)(2,1)S(1)} %copy-done.21), channel_id=1, source_target_pairs={{0,24},{1,25},{2,26},{3,27},{4,28},{5,29},{6,30},{7,31},{8,16},{9,... | collective-permute-start | bytes 442376 | tf_op jit(solution)/shard_map/ppermute | solution.py:611
  190.7 1.4 copy-start.3
  192.1 1.7 copy-start.2
  199.2 40.6 %collective-permute-start.11 = (bf16[8,224,768]{2,1,0:T(8,128)(2,1)}, bf16[8,224,768]{2,1,0:T(8,128)(2,1)S(1)}, u32[]{:S(2)}, u32[]{:S(2)}) collective-permute-start(bf16[8,224,768]{2,1,0:T(8,128)(2,1)} %merge.4), channel_id=1, source_target_pairs={{0,8},{1,17},{2,10},{3,19},{4,12},{5,21},{6,14},{7,23},{8,0},{9,25... | collective-permute-start | bytes 8257544 | tf_op jit(solution)/shard_map/ppermute | solution.py:611
  239.9 1.6 copy-start.4
  244.7 4.6 %copy-start.9 = (bf16[4,224,768]{2,1,0:T(8,128)(2,1)S(1)}, bf16[4,224,768]{2,1,0:T(8,128)(2,1)}, u32[]{:S(2)}) copy-start(bf16[4,224,768]{2,1,0:T(8,128)(2,1)} %merge.5) | copy-start | bytes 4128772
  248.5 29.2 %collective-permute-start.12 = (bf16[768,768]{1,0:T(8,128)(2,1)}, bf16[768,768]{1,0:T(8,128)(2,1)}, u32[]{:S(2)}, u32[]{:S(2)}) collective-permute-start(bf16[768,768]{1,0:T(8,128)(2,1)} %convolution_convert_fusion.1), channel_id=1, source_target_pairs={{0,8},{1,17},{2,10},{3,19},{4,12},{5,21},{6,14},{7,23},{8,0},{9,25... | collective-permute-start | bytes 3538952 | tf_op jit(solution)/shard_map/ppermute | solution.py:611
  249.3 30.7 %collective-permute-start.16 = (bf16[4,224,768]{2,1,0:T(8,128)(2,1)S(1)}, bf16[4,224,768]{2,1,0:T(8,128)(2,1)S(1)}, u32[]{:S(2)}, u32[]{:S(2)}) collective-permute-start(bf16[4,224,768]{2,1,0:T(8,128)(2,1)S(1)} %copy-done.9), channel_id=1, source_target_pairs={{0,16},{1,9},{2,18},{3,11},{4,20},{5,13},{6,22},{7,15},{8,24},{9,1... | collective-permute-start | bytes 4128776 | tf_op jit(solution)/shard_map/ppermute | solution.py:611
  257.5 22.6 %collective-permute-start.13 = (bf16[4,104,768]{2,1,0:T(8,128)(2,1)}, bf16[4,104,768]{2,1,0:T(8,128)(2,1)}, u32[]{:S(2)}, u32[]{:S(2)}) collective-permute-start(bf16[4,104,768]{2,1,0:T(8,128)(2,1)} %get-tuple-element.127), channel_id=1, source_target_pairs={{0,1},{1,0},{2,3},{3,2},{4,5},{5,4},{6,7},{7,6},{8,9},{9,8},{10,11... | collective-permute-start | bytes 1916936 | tf_op jit(solution)/shard_map/ppermute | solution.py:611
  280.1 10.2 %collective-permute-start.14 = (bf16[384,768]{1,0:T(8,128)(2,1)}, bf16[384,768]{1,0:T(8,128)(2,1)}, u32[]{:S(2)}, u32[]{:S(2)}) collective-permute-start(bf16[384,768]{1,0:T(8,128)(2,1)} %fusion), channel_id=1, source_target_pairs={{0,16},{1,9},{2,18},{3,11},{4,20},{5,13},{6,22},{7,15},{8,24},{9,1... | collective-permute-start | bytes 1769480 | tf_op jit(solution)/shard_map/ppermute | solution.py:611
  280.1 4.7 %copy-start.11 = (bf16[4,104,768]{2,1,0:T(8,128)(2,1)S(1)}, bf16[4,104,768]{2,1,0:T(8,128)(2,1)}, u32[]{:S(2)}) copy-start(bf16[4,104,768]{2,1,0:T(8,128)(2,1)} %get-tuple-element.133) | copy-start | bytes 1916932
  280.1 1.1 copy-start.5
  281.2 9.1 %copy-start.10 = (f32[384,768]{1,0:T(8,128)S(1)}, f32[384,768]{1,0:T(8,128)}, u32[]{:S(2)}) copy-start(f32[384,768]{1,0:T(8,128)} %get-tuple-element.92) | copy-start | bytes 3538948
  284.2 23.5 %collective-permute-start.17 = (bf16[2,224,768]{2,1,0:T(8,128)(2,1)}, bf16[2,224,768]{2,1,0:T(8,128)(2,1)S(1)}, u32[]{:S(2)}, u32[]{:S(2)}) collective-permute-start(bf16[2,224,768]{2,1,0:T(8,128)(2,1)} %merge.6), channel_id=1, source_target_pairs={{0,2},{1,3},{2,0},{3,1},{4,6},{5,7},{6,4},{7,5},{8,10},{9,11},{10,... | collective-permute-start | bytes 2064392 | tf_op jit(solution)/shard_map/ppermute | solution.py:611
  285.8 21.9 %collective-permute-start.15 = (bf16[2,104,768]{2,1,0:T(8,128)(2,1)S(1)}, bf16[2,104,768]{2,1,0:T(8,128)(2,1)S(1)}, u32[]{:S(2)}, u32[]{:S(2)}) collective-permute-start(bf16[2,104,768]{2,1,0:T(8,128)(2,1)S(1)} %add_convert_fusion), channel_id=1, source_target_pairs={{0,2},{1,3},{2,0},{3,1},{4,6},{5,7},{6,4},{7,5},{8,10},{9,11},{10,... | collective-permute-start | bytes 958472 | tf_op jit(solution)/shard_map/ppermute | solution.py:611
  307.7 6.0 %copy-start.7 = (bf16[2,224,768]{2,1,0:T(8,128)(2,1)}, bf16[2,224,768]{2,1,0:T(8,128)(2,1)S(1)}, u32[]{:S(2)}) copy-start(bf16[2,224,768]{2,1,0:T(8,128)(2,1)S(1)} %collective-permute-done.17.refs_6_) | copy-start | bytes 2064388
  309.4 9.7 %collective-permute-start.18 = (bf16[1,104,768]{2,1,0:T(8,128)(2,1)S(1)}, bf16[1,104,768]{2,1,0:T(8,128)(2,1)S(1)}, u32[]{:S(2)}, u32[]{:S(2)}) collective-permute-start(bf16[1,104,768]{2,1,0:T(8,128)(2,1)S(1)} %add_convert_fusion.1), channel_id=1, source_target_pairs={{0,4},{1,5},{2,6},{3,7},{4,0},{5,1},{6,2},{7,3},{8,12},{9,13},{10,... | collective-permute-start | bytes 479240 | tf_op jit(solution)/shard_map/ppermute | solution.py:611
  310.1 40.8 %all-to-all-start.1 = ((bf16[8,48,768]{2,1,0:T(8,128)(2,1)}), bf16[8,48,768]{2,1,0:T(8,128)(2,1)S(1)}, u32[]{:S(2)}, u32[]{:S(2)}) async-start(bf16[8,48,768]{2,1,0:T(8,128)(2,1)} %bitcast.34), calls=%async_computation.1 | async-start | bytes 1179648 | tf_op jit(solution)/shard_map/all_to_all | solution.py:956
  313.8 5.4 %copy-start.14 = (bf16[2,104,768]{2,1,0:T(8,128)(2,1)S(1)}, bf16[2,104,768]{2,1,0:T(8,128)(2,1)}, u32[]{:S(2)}) copy-start(bf16[2,104,768]{2,1,0:T(8,128)(2,1)} %copy-done.13) | copy-start | bytes 958468
  316.2 29.0 %collective-permute-start.22 = (bf16[1,224,768]{2,1,0:T(8,128)(2,1)}, bf16[1,224,768]{2,1,0:T(8,128)(2,1)S(1)}, u32[]{:S(2)}, u32[]{:S(2)}) collective-permute-start(bf16[1,224,768]{2,1,0:T(8,128)(2,1)} %merge.7), channel_id=1, source_target_pairs={{0,4},{1,5},{2,6},{3,7},{4,0},{5,1},{6,2},{7,3},{8,12},{9,13},{10,... | collective-permute-start | bytes 1032200 | tf_op jit(solution)/shard_map/ppermute | solution.py:611
  320.2 7.6 %collective-permute-start.21 = (bf16[1,24,768]{2,1,0:T(8,128)(2,1)S(1)}, bf16[1,24,768]{2,1,0:T(8,128)(2,1)S(1)}, u32[]{:S(2)}, u32[]{:S(2)}) collective-permute-start(bf16[1,24,768]{2,1,0:T(8,128)(2,1)S(1)} %get-tuple-element.198), channel_id=1, source_target_pairs={{0,24},{1,25},{2,26},{3,27},{4,28},{5,29},{6,30},{7,31},{8,16},{9,... | collective-permute-start | bytes 110600 | tf_op jit(solution)/shard_map/ppermute | solution.py:611
  321.4 6.3 %collective-permute-start.20 = (bf16[1,24,768]{2,1,0:T(8,128)(2,1)S(1)}, bf16[1,24,768]{2,1,0:T(8,128)(2,1)S(1)}, u32[]{:S(2)}, u32[]{:S(2)}) collective-permute-start(bf16[1,24,768]{2,1,0:T(8,128)(2,1)S(1)} %get-tuple-element.199), channel_id=1, source_target_pairs={{0,16},{1,9},{2,18},{3,11},{4,20},{5,13},{6,22},{7,15},{8,24},{9,1... | collective-permute-start | bytes 110600 | tf_op jit(solution)/shard_map/ppermute | solution.py:611
  322.9 4.9 %collective-permute-start.19 = (bf16[1,24,768]{2,1,0:T(8,128)(2,1)S(1)}, bf16[1,24,768]{2,1,0:T(8,128)(2,1)S(1)}, u32[]{:S(2)}, u32[]{:S(2)}) collective-permute-start(bf16[1,24,768]{2,1,0:T(8,128)(2,1)S(1)} %get-tuple-element.200), channel_id=1, source_target_pairs={{0,8},{1,17},{2,10},{3,19},{4,12},{5,21},{6,14},{7,23},{8,0},{9,25... | collective-permute-start | bytes 110600 | tf_op jit(solution)/shard_map/ppermute | solution.py:611
  328.4 16.8 %copy-start.8 = (bf16[2,224,768]{2,1,0:T(8,128)(2,1)S(1)}, bf16[2,224,768]{2,1,0:T(8,128)(2,1)}, u32[]{:S(2)}) copy-start(bf16[2,224,768]{2,1,0:T(8,128)(2,1)} %copy-done.7) | copy-start | bytes 2064388
  347.6 6.1 %copy-start.1 = (bf16[96,768]{1,0:T(8,128)(2,1)S(1)}, bf16[96,768]{1,0:T(8,128)(2,1)}, u32[]{:S(2)}) copy-start(bf16[96,768]{1,0:T(8,128)(2,1)} %param.25) | copy-start | bytes 442372
  351.0 0.8 copy-start.6
  (2 other events, 1.4 us)
Sparse Core Ops, SparseCore 0:
  12.5 36.4 all-gather.4
  52.4 92.7 all-gather.6
where the time goes:
time: 362 us; the launch traced here: 361 us
  Pallas kernels  142 us (39%)
  waiting for transfers between devices  83.4 us (23%)
  local copies, waits for them, and re-layouts  40.2 us (11%)
  other arithmetic  34.7 us (10%)
  starting transfers between devices  34 us (9%)
  between operations  17.8 us (5%)
  matrix products  8.15 us (2%)
    ppermute x23, waiting for transfers between devices, across(): return lax.ppermute(values, ('seq', 'fsdp'), pairs)  67 us
    pallas_call x1, Pallas kernels, attend_back(): pl.pallas_call(back_body, grid=(3, blocks), in_specs=[SM] + [pl.BlockSpec...  36.3 us
    pallas_call x1, Pallas kernels, attend(): pl.pallas_call(attend_body, grid=(3, blocks), in_specs=[SM, pl.BlockSpec(...  30.1 us
    ppermute x23, starting transfers between devices, across(): return lax.ppermute(values, ('seq', 'fsdp'), pairs)  24 us
    pallas_call x1, Pallas kernels, middle(): pl.pallas_call(middle_body, in_specs=[SM] + [VM] * 9, out_specs=[VM] * 12...  22.3 us
    pallas_call x1, Pallas kernels, project(): pl.pallas_call(project_body, in_specs=[SM] + [VM] * 7, out_specs=[VM] * 6...  13.9 us
    pallas_call x4, Pallas kernels, merge(): pl.pallas_call(merge_body, grid=(first,), in_specs=[block(p) for p in par...  13.5 us
    cos x1, other arithmetic, angles_of(): return (jnp.sin(turned), jnp.cos(turned))  10.4 us
  transfers between devices with their start and end apart: 27, of which 12 were waited for; matrix products, arithmetic and copies ran while one was open for 18% of the time, Pallas kernels for 29%

commit v1 on v0

--- a/solution.py
+++ b/solution.py
@@ -1,3 +1,5 @@
+import functools
+
 import jax
 import jax.numpy as jnp
 from jax import lax
@@ -369,90 +371,95 @@
     )(place, *douts, big, small, ox, qx, pq, kx, vxt, kp, wr, sn, cs, tcol, head)
 
 
-def reload_body(owners, in_ref, out_ref):
+def reload_body(outward, owners, in_ref, out_ref):
     def move(j, carry):
-        out_ref[j] = in_ref[owners[j]]
+        if outward:
+            out_ref[owners[j]] = in_ref[j]
+        else:
+            out_ref[j] = in_ref[owners[j]]
         return carry
 
     lax.fori_loop(0, out_ref.shape[0], move, 0)
 
 
-def reload(owners, returned):
+def reload(owners, rows, outward):
     return pl.pallas_call(
-        reload_body,
+        functools.partial(reload_body, outward),
         in_specs=[SM, VM],
         out_specs=VM,
-        out_shape=jax.ShapeDtypeStruct(returned.shape, returned.dtype),
+        out_shape=jax.ShapeDtypeStruct(rows.shape, rows.dtype),
         compiler_params=pltpu.CompilerParams(vmem_limit_bytes=VMEM_LIMIT),
-        name="reload",
-    )(owners, returned)
-
-
-def qkv_blocks_body(place, x0, x1, x2, x3, tkeep_ref, tsend_ref, rel_ref, sums_ref, keep_ref, send_ref, acc):
-    even = lax.rem(place[0], 2) == 0
+        name="deal" if outward else "reload",
+    )(owners, rows)
+
+
+def qkv_blocks_body(x0, x1, x2, x3, tkeep_ref, tsend_ref, rel_ref, sums_ref, out_ref, acc):
     part = x0.shape[0]
+    count, high, _ = out_ref.shape
+    rows = high - 8
+    fine = rows // 4
     parts = ((x0, tkeep_ref, 0), (x2, tkeep_ref, part), (x1, tsend_ref, 0), (x3, tsend_ref, part))
     for number, (x, t, low) in enumerate(parts):
         value = lax.dot_general(x[...], t[low : low + part, :], (((0,), (0,)), ((), ())), preferred_element_type=F32)
         acc[...] = value if number == 0 else acc[...] + value
     notes = jnp.concatenate([sums_ref[0], sums_ref[1], sums_ref[2], jnp.zeros((8, 384), F32)], axis=1).astype(BF)
-
-    def piece(f, s):
-        value = acc[(8 * s + f) * 24 : (8 * s + f + 1) * 24, :]
-        rel = rel_ref[96 * f + 24 * s : 96 * f + 24 * s + 24, :]
-        return jnp.concatenate([value[:, 0:512], value[:, 512:640] + rel[:, 0:128], rel[:, 128:256]], axis=1)
-
-    for g in range(4):
-        slot = place[1 + g]
+    for f in range(count):
         for s in range(4):
-            a, b = piece(2 * g, s), piece(2 * g + 1, s)
-            keep_ref[slot, 24 * s : 24 * s + 24, :] = jnp.where(even, a, b).astype(BF)
-            send_ref[slot, 24 * s : 24 * s + 24, :] = jnp.where(even, b, a).astype(BF)
-        keep_ref[slot, 96:104, :] = notes
-        send_ref[slot, 96:104, :] = notes
-
-
-def qkv_blocks(place, pieces, tkeep, tsend, rel, sums):
+            value = acc[(count * s + f) * fine : (count * s + f + 1) * fine, :]
+            rel = rel_ref[rows * f + fine * s : rows * f + fine * (s + 1), :]
+            low, high = fine * s, fine * (s + 1)
+            out_ref[f, low:high, 0:512] = value[:, 0:512].astype(BF)
+            out_ref[f, low:high, 512:640] = (value[:, 512:640] + rel[:, 0:128]).astype(BF)
+            out_ref[f, low:high, 640:768] = rel[:, 128:256].astype(BF)
+        out_ref[f, rows : rows + 8, :] = notes
+
+
+def qkv_blocks(count, pieces, tkeep, tsend, rel, sums):
     width = pieces[0].shape[1]
-    out = jax.ShapeDtypeStruct((4, 104, width), BF)
     return pl.pallas_call(
         qkv_blocks_body,
-        in_specs=[SM] + [VM] * 8,
-        out_specs=[VM] * 2,
-        out_shape=[out, out],
+        in_specs=[VM] * 8,
+        out_specs=VM,
+        out_shape=jax.ShapeDtypeStruct((count, width // count + 8, width), BF),
         scratch_shapes=[pltpu.VMEM((width, 640), F32)],
         compiler_params=pltpu.CompilerParams(vmem_limit_bytes=VMEM_LIMIT),
         cost_estimate=pl.CostEstimate(flops=2_000_000_000, bytes_accessed=8_000_000, transcendentals=0),
         name="qkv_blocks",
-    )(place, *pieces, tkeep, tsend, rel, sums)
-
-
-def merge_body(*refs):
-    kb, cb, ki, ci, *more, out_ref = refs
-    cut = kb.shape[1]
-    back = kb[...].astype(F32) + cb[...].astype(F32)
-    ins = ki[...].astype(F32) + ci[...].astype(F32)
-    for m in more:
-        back = back + m[:, :cut, :].astype(F32)
-        ins = ins + m[:, cut:, :].astype(F32)
-    out_ref[:, :cut, :] = back.astype(BF)
-    out_ref[:, cut:, :] = ins.astype(BF)
-
-
-def merge(parts, half):
+    )(*pieces, tkeep, tsend, rel, sums)
+
+
+def merge_body(split, *refs):
+    count = len(refs) - (2 if split else 1)
+    sums = []
+    for group in (refs[: count // 2], refs[count // 2 : count]):
+        total = group[0][...].astype(F32)
+        for ref in group[1:]:
+            total = total + ref[...].astype(F32)
+        sums.append(total.astype(BF))
+    if split:
+        refs[count][...], refs[count + 1][...] = sums
+    else:
+        cut = sums[0].shape[1]
+        refs[count][:, :cut, :] = sums[0]
+        refs[count][:, cut:, :] = sums[1]
+
+
+def merge(backs, ins, half, split=True):
     step = min(half, 2)
     first = half // step
-    rows = parts[0].shape[1] + parts[2].shape[1]
-    width = parts[0].shape[2]
+    width = backs[0].shape[2]
+    heights = [backs[0].shape[1], ins[0].shape[1]]
+    heights = heights if split else [sum(heights)]
     block = lambda p: pl.BlockSpec((step,) + p.shape[1:], lambda g: (first + g, 0, 0))
+    parts = backs + ins
     return pl.pallas_call(
-        merge_body,
+        functools.partial(merge_body, split),
         grid=(first,),
         in_specs=[block(p) for p in parts],
-        out_specs=pl.BlockSpec((step, rows, width), lambda g: (g, 0, 0)),
-        out_shape=jax.ShapeDtypeStruct((half, rows, width), BF),
+        out_specs=[pl.BlockSpec((step, h, width), lambda g: (g, 0, 0)) for h in heights],
+        out_shape=[jax.ShapeDtypeStruct((half, h, width), BF) for h in heights],
         compiler_params=pltpu.CompilerParams(vmem_limit_bytes=VMEM_LIMIT, dimension_semantics=("arbitrary",)),
-        cost_estimate=pl.CostEstimate(flops=half * rows * width * 6, bytes_accessed=half * rows * width * 8, transcendentals=0),
+        cost_estimate=pl.CostEstimate(flops=half * 224 * width * 6, bytes_accessed=half * 224 * width * 8, transcendentals=0),
         name="merge",
     )(*parts)
 
@@ -642,10 +649,6 @@
     return total
 
 
-def outgoing(parts, count):
-    return add_parts(parts, count // 2, count).astype(BF)
-
-
 def back_blocks_body(place, u_ref, df_ref, keep_ref, send_ref):
     core = lax.rem(place[0], 2)
     group = u_ref.shape[1] // 4
@@ -681,7 +684,7 @@
     )(place, u, df)
 
 
-def in_blocks_body(place, h_ref, dz_ref, a_ref, db_ref, sum_ref, keep_ref, send_ref):
+def in_blocks_body(place, h_ref, dz_ref, a0, a1, a2, a3, db_ref, sum_ref, keep_ref, send_ref):
     even = lax.rem(place[0], 2) == 0
     core = lax.rem(place[0], 2)
     own = lax.div(place[0], 8)
@@ -708,14 +711,10 @@
 
     @pl.when(step == 4)
     def _():
-        for g in range(2):
-            acc = lax.dot_general(
-                a_ref[:, g * 384 : (g + 1) * 384], db_ref[...], (((0,), (0,)), ((), ())), preferred_element_type=F32
-            )
-            for j in range(0, 16, 2):
-                row = 2 * g + j // 8
-                source = jnp.where(row == 0, 0, jnp.where(row == 3, 3, place[32 + row]))
-                put((own ^ source) * 8 + j % 8, 96, acc[j * 24 : (j + 2) * 24])
+        for mask, piece in zip((0, place[33], place[34], 3), (a0, a1, a2, a3)):
+            acc = lax.dot_general(piece[...], db_ref[...], (((0,), (0,)), ((), ())), preferred_element_type=F32)
+            for j in range(0, 8, 2):
+                put((own ^ mask) * 8 + j, 96, acc[j * 24 : (j + 2) * 24])
         width = sum_ref.shape[1]
         line = lax.broadcasted_iota(jnp.int32, (8, width), 0)
 
@@ -739,14 +738,16 @@
     return pl.pallas_call(
         in_blocks_body,
         grid=(chunks + 1,),
-        in_specs=[SM, whole, pl.BlockSpec((rows, width), lambda g: (0, jnp.minimum(g, chunks - 1))), whole, whole]
+        in_specs=[SM, whole, pl.BlockSpec((rows, width), lambda g: (0, jnp.minimum(g, chunks - 1)))]
+        + [pl.BlockSpec(attn[0].shape, lambda g: (0, 0))] * 4
+        + [whole]
         + [pl.BlockSpec(sums.shape, lambda g: (0, 0))],
         out_specs=[pl.BlockSpec((16, 128, width), lambda g: (0, 0, 0))] * 2,
         out_shape=[out, out],
         compiler_params=pltpu.CompilerParams(vmem_limit_bytes=VMEM_LIMIT, dimension_semantics=("arbitrary",)),
         cost_estimate=pl.CostEstimate(flops=2 * rows * width * (dz.shape[1] + width), bytes_accessed=12_000_000, transcendentals=0),
         name="in_blocks",
-    )(place, hidden_low, dz, attn, dbr, sums)
+    )(place, hidden_low, dz, *attn, dbr, sums)
 
 
 def shards(
@@ -785,12 +786,7 @@
     local_cols = width // seqs
     local_heads = w_relative.shape[1]
     scale = DH ** -0.5
-    owner_table = owners[None, :] == jnp.arange(pack_count, dtype=jnp.int32)[:, None]
-    owner_low = owner_table.astype(BF)
-    dealt = jnp.dot(
-        owner_low, inputs.reshape(pack_count, sliver_rows * width), preferred_element_type=F32
-    )
-    dealt = dealt.astype(BF).reshape(pack_count, sliver_rows, width)
+    dealt = reload(owners, inputs, True)
     mine = lax.all_to_all(dealt, "fsdp", split_axis=0, concat_axis=1, tiled=True)[0]
     row_count = mine.shape[0]
     chosen = (owners == rank).astype(jnp.int32)
@@ -888,6 +884,7 @@
 
     pieces = [mine, to_first(mine), to_second(mine)]
     pieces.append(to_second(pieces[1]))
+    pieces, wrel_rows = lax.optimization_barrier((pieces, wrel_rows))
     qx, pq, kx, kxt, vx, vxt = project(place, pieces, w_qkv, head, turned_types)
     big, small, ox, *head_out = attend(place, qx, pq, kxt, vx, key_pos_t, wrel_cols, sine, cosine)
     order = own ^ jnp.arange(seqs, dtype=jnp.int32)
@@ -899,7 +896,6 @@
     )
     activations = result.reshape(1, row_count, width)
     douts = deal(douts)
-    attn_rows = jnp.concatenate(attn, axis=1)
     devices = seqs * fsdps
     device = own * fsdps + rank
     fine = width // devices
@@ -910,75 +906,67 @@
         bit = lambda n: (relative >> n) & 1
         flip = (bit(0) ^ parity) == 1
         one, two = jnp.where(flip, bit(4), bit(3)), jnp.where(flip, bit(3), bit(4))
-        slots = one * 8 + two * 4 + bit(1) * 2 + bit(2)
-        table = jnp.concatenate([device[None], slots, place[3:5]]).astype(jnp.int32)
-        kept_in, sent_in = in_blocks(table, hidden_low, pre_grad, attn_rows, branch_grad, short_sums)
-        core_in = to_core(sent_in)
-        kept_back, sent_back = back_blocks(table, act_low, ffn_grad)
-        parts = [kept_back, to_core(sent_back), kept_in, core_in]
-        out = merge(parts, 8)
-        douts, out = lax.optimization_barrier((douts, out))
-        parts.append(to_first(out))
+        me, masks = device[None], place[3:5]
+        in_table = jnp.concatenate([me, one * 8 + two * 4 + bit(1) * 2 + bit(2), masks]).astype(jnp.int32)
+        back_table = jnp.concatenate([me, bit(1) * 8 + one * 4 + two * 2 + bit(2), masks]).astype(jnp.int32)
+        kept, sent = in_blocks(in_table, hidden_low, pre_grad, attn, branch_grad, short_sums)
+        ins = [kept, to_core(sent)]
+        kept, sent = back_blocks(back_table, act_low, ffn_grad)
+        backs = [kept, to_core(sent)]
+        back_out, in_out = merge(backs, ins, 8)
+        douts, back_out, in_out = lax.optimization_barrier((douts, back_out, in_out))
+        backs.append(to_near(back_out))
+        ins.append(to_first(in_out))
     else:
         scatter = lambda v: lax.psum_scatter(v, ("seq", "fsdp"), scatter_dimension=0, tiled=True)
         w_back_grad = scatter(contract_rows(act_low, ffn_grad))
         w_in_grad = scatter(contract_rows(hidden_low, pre_grad))
-        spun = contract_rows(attn_rows, branch_grad).reshape(seqs, local_cols, width)
+        spun = contract_rows(jnp.concatenate(attn, axis=1), branch_grad).reshape(seqs, local_cols, width)
         w_out_grad = scatter(jnp.take(spun, kept_place, axis=0).reshape(width, width))
 
     tkeep, tsend, rel, sums = attend_back(
         place, douts, big, small, ox, qx, pq, kx, vxt, key_pos, wrel_rows, sine, cosine, turned_types, head
     )
     if direct:
-        out = merge(parts, 4)
-        tkeep, tsend, out = lax.optimization_barrier((tkeep, tsend, out))
-        parts.append(to_second(out))
-    dx_send = contract_cols(tsend, w_qkv).astype(BF)
-    tkeep, tsend, dx_send = lax.optimization_barrier((tkeep, tsend, dx_send))
-    dx_first = to_first(dx_send)
-    dx_keep = contract_cols(tkeep, w_qkv)
-    dx_out = (dx_keep[row_count:] + dx_first[row_count:].astype(F32)).astype(BF)
-    if direct:
-        spots = ((rank >> 1) ^ jnp.arange(4, dtype=jnp.int32)) & 3
-        spots = (spots & 1) * 2 + (spots >> 1)
-        qkv_table = jnp.concatenate([rank[None], spots]).astype(jnp.int32)
-        kept, sent = qkv_blocks(qkv_table, pieces, tkeep, tsend, rel, sums)
-        qkv_parts = [kept, to_core(sent)]
-        dx_out, qkv_parts = lax.optimization_barrier((dx_out, qkv_parts))
-    dx_second = to_second(dx_out)
-    if direct:
-        qkv_parts.append(to_near(outgoing(qkv_parts, 4)))
-        parts.append(to_near(merge(parts, 2)))
-    input_rows = sum_one_grad + dx_keep[:row_count] + dx_first[:row_count].astype(F32) + dx_second.astype(F32)
-    input_rows = input_rows.astype(BF).reshape(fsdps, sliver_rows, width)
-    if direct:
-        input_rows, qkv_parts, parts = lax.optimization_barrier((input_rows, qkv_parts, parts))
-    returned = lax.all_to_all(input_rows, "fsdp", split_axis=0, concat_axis=0, tiled=True)
-    input_grad = reload(owners, returned)
-    if direct:
-        qkv_parts.append(to_far(outgoing(qkv_parts, 2)))
-        parts.append(to_far(merge(parts, 1)))
-        total = add_parts(qkv_parts, 0, 1)[0]
-        cut = kept_back.shape[1]
-        tails = [p[:, :cut] for p in parts[4:]]
-        w_back_grad = add_parts(parts[:2] + tails, 0, 1)[0]
-        tails = [p[:, cut:] for p in parts[4:]]
-        in_total = add_parts(parts[2:4] + tails, 0, 1)[0]
-        w_in_grad = jnp.concatenate([in_total[c * 24 : (c + 1) * 24] for c in range(4)], axis=1)
-        w_out_grad = in_total[96:120]
-        short_grads, in_bias_grad = in_total[120:128, :fine], in_total[126, :deep]
+        bundle = qkv_blocks(fsdps, pieces, tkeep, tsend, rel, sums)
     else:
-        short_sums = lax.psum(short_sums, ("seq", "fsdp"))
-        short_grads = lax.dynamic_slice(short_sums, (0, device * fine), (8, fine))
-        in_bias_grad = lax.dynamic_slice(short_sums, (8 + device * deep // width, device * deep % width), (1, deep))[0]
         grad = contract_rows(pieces[0], tkeep[:row_count]) + contract_rows(pieces[2], tkeep[row_count:])
         grad = grad + contract_rows(pieces[1], tsend[:row_count]) + contract_rows(pieces[3], tsend[row_count:])
         grad = jnp.swapaxes(grad.reshape(seqs, fsdps, fine, 640), 0, 1).reshape(fsdps, local_rows, 640)
         tall = rel.reshape(fsdps, local_rows, 256)
         bundle = jnp.concatenate([grad[..., :512], grad[..., 512:] + tall[..., :128], tall[..., 128:]], axis=2)
         notes = jnp.concatenate([sums[0], sums[1], sums[2], jnp.zeros((8, 384), F32)], axis=1)
-        bundle = jnp.concatenate([bundle, jnp.broadcast_to(notes[None], (fsdps,) + notes.shape)], axis=1)
-        total = lax.psum_scatter(bundle, "fsdp", scatter_dimension=0, tiled=True)[0]
+        bundle = jnp.concatenate([bundle, jnp.broadcast_to(notes[None], (fsdps,) + notes.shape)], axis=1).astype(BF)
+    total = lax.psum_scatter(bundle, "fsdp", scatter_dimension=0, tiled=True)[0].astype(F32)
+    dx_send = contract_cols(tsend, w_qkv).astype(BF)
+    if direct:
+        dx_send, backs, ins, bundle = lax.optimization_barrier((dx_send, backs, ins, bundle))
+        back_out, in_out = merge(backs, ins, 4)
+        backs.append(to_first(back_out))
+        ins.append(to_second(in_out))
+    dx_first = to_first(dx_send)
+    dx_keep = contract_cols(tkeep, w_qkv)
+    if direct:
+        dx_first, backs, ins = lax.optimization_barrier((dx_first, backs, ins))
+    dx_out = (dx_keep[row_count:] + dx_first[row_count:].astype(F32)).astype(BF)
+    dx_second = to_second(dx_out)
+    if direct:
+        back_out, in_out = merge(backs, ins, 2)
+        backs.append(to_second(back_out))
+        ins.append(to_near(in_out))
+        dx_second, backs, ins = lax.optimization_barrier((dx_second, backs, ins))
+    input_rows = sum_one_grad + dx_keep[:row_count] + dx_first[:row_count].astype(F32) + dx_second.astype(F32)
+    input_rows = input_rows.astype(BF).reshape(fsdps, sliver_rows, width)
+    returned = lax.all_to_all(input_rows, "fsdp", split_axis=0, concat_axis=0, tiled=True)
+    input_grad = reload(owners, returned, False)
+    if direct:
+        far_out, total = lax.optimization_barrier((merge(backs, ins, 1, False)[0], total))
+        far = to_far(far_out)
+        cut = kept.shape[1]
+    if not direct:
+        short_sums = lax.psum(short_sums, ("seq", "fsdp"))
+        short_grads = lax.dynamic_slice(short_sums, (0, device * fine), (8, fine))
+        in_bias_grad = lax.dynamic_slice(short_sums, (8 + device * deep // width, device * deep % width), (1, deep))[0]
     own_qkv = total[:local_rows].astype(BF).reshape(seqs, fine, width)
     block_for = lambda mask: lax.dynamic_index_in_dim(own_qkv, own ^ mask, 0, keepdims=True)
     swapped = jnp.concatenate(deal([block_for(m) for m in (0, place[3], place[4], 3)]), axis=0)
@@ -986,6 +974,13 @@
     both = swapped[:, :, : 2 * local_cols].reshape(seqs, fine, local_heads, 2, DH)
     both = jnp.transpose(both, (3, 1, 0, 2, 4)).reshape(2, fine, width)
     w_value_grad = jnp.transpose(swapped[:, :, 2 * local_cols : 3 * local_cols], (1, 0, 2)).reshape(fine, width)
+    if direct:
+        _, _, far, _ = lax.optimization_barrier((both, w_value_grad, far, input_grad))
+        w_back_grad = add_parts(backs + [far[:, :cut]], 0, 1)[0]
+        in_total = add_parts(ins + [far[:, cut:]], 0, 1)[0]
+        w_in_grad = jnp.concatenate([in_total[c * 24 : (c + 1) * 24] for c in range(4)], axis=1)
+        w_out_grad = in_total[96:120]
+        short_grads, in_bias_grad = in_total[120:128, :fine], in_total[126, :deep]
     rel_total = total[:local_rows, 3 * local_cols :].reshape(local_rows, local_heads, DH)
     notes = total[local_rows:, :384].reshape(8, 3, 128)
     eighth = DH // fsdps

time: 362 us -> 341 us (0.942)
  waiting for transfers between devices: 83.4 us -> 71.8 us
  local copies, waits for them, and re-layouts: 40.2 us -> 34.4 us
  other arithmetic: 34.7 us -> 31 us
    ppermute x23, waiting for transfers between devices: 67 us -> 46.5 us  [across(): return lax.ppermute(values, ('seq', 'fsdp'), pairs)]
    all_to_all x1, waiting for transfers between devices: 0.01 us -> 13.2 us  [shards(): lax.all_to_all(input_rows, 'fsdp', split_axis=0, concat_axis=0, tiled=True)]
    all_gather x1, waiting for transfers between devices: 7.94 us -> 4.27 us  [shards(): lax.all_gather(late, ('fsdp', 'seq'), axis=0)]
    unnamed x53 -> x54, local copies, waits for them, and re-layouts: 10.3 us -> 7 us
    pallas_call x6 -> x7, Pallas kernels: 21.5 us -> 22.9 us  [the longest x4 13.1 us: merge(): pl.pallas_call(functools.partial(merge_body, split), grid=(first,), in_sp...]
  transfers between devices with their start and end apart: 27 -> 28, of which waited for: 12 -> 12; matrix products, arithmetic and copies ran while one was open for 18% -> 16% of each run, Pallas kernels for 29% -> 33%
where the time goes in v1:
time: 341 us; the launch traced here: 339 us
  Pallas kernels  144 us (42%)
  waiting for transfers between devices  71.8 us (21%)
  local copies, waits for them, and re-layouts  34.4 us (10%)
  starting transfers between devices  34.3 us (10%)
  other arithmetic  31 us (9%)
  between operations  17.5 us (5%)
  matrix products  6.29 us (2%)
    ppermute x23, waiting for transfers between devices, across(): return lax.ppermute(values, ('seq', 'fsdp'), pairs)  46.5 us
    pallas_call x1, Pallas kernels, attend_back(): pl.pallas_call(back_body, grid=(3, blocks), in_specs=[SM] + [pl.BlockSpec...  36.3 us
    pallas_call x1, Pallas kernels, attend(): pl.pallas_call(attend_body, grid=(3, blocks), in_specs=[SM, pl.BlockSpec(...  30.2 us
    ppermute x23, starting transfers between devices, across(): return lax.ppermute(values, ('seq', 'fsdp'), pairs)  24.1 us
    pallas_call x1, Pallas kernels, middle(): pl.pallas_call(middle_body, in_specs=[SM] + [VM] * 9, out_specs=[VM] * 12...  22.3 us
    pallas_call x1, Pallas kernels, project(): pl.pallas_call(project_body, in_specs=[SM] + [VM] * 7, out_specs=[VM] * 6...  14 us
    all_to_all x1, waiting for transfers between devices, shards(): lax.all_to_all(input_rows, 'fsdp', split_axis=0, concat_axis=0, tiled=True)  13.2 us
    pallas_call x4, Pallas kernels, merge(): pl.pallas_call(functools.partial(merge_body, split), grid=(first,), in_sp...  13.1 us
  transfers between devices with their start and end apart: 28, of which 12 were waited for; matrix products, arithmetic and copies ran while one was open for 16% of the time, Pallas kernels for 33%

profile of v1, /device:TPU:0, one launch (start us, length us, event | category | flops | bytes accessed | tf_op | source)
XLA Modules:
  0.0 339.3 jit_solution(10525719549557444991)
XLA Ops:
  15.3 2.0 deal.1
  17.3 6.4 %all-to-all-start = ((bf16[8,48,768]{2,1,0:T(8,128)(2,1)}), bf16[8,48,768]{2,1,0:T(8,128)(2,1)}, u32[]{:S(2)}, u32[]{:S(2)}) async-start(bf16[8,48,768]{2,1,0:T(8,128)(2,1)} %deal.1), calls=%async_computation | async-start | bytes 1179648 | tf_op jit(solution)/shard_map/all_to_all | solution.py:790
  25.2 1.3 fusion.10
  28.5 1.2 broadcast_in_dim.38.tcol_ref
  31.1 10.4 %multiply_cosine_fusion = (f32[1536,384]{1,0:T(8,128)}, bf16[1536,384]{1,0:T(8,128)(2,1)S(1)}, bf16[1536,384]{1,0:T(8,128)(2,1)}, f32[1536,384]{1,0:T(8,128)}) fusion(f32[384]{0:T(512)S(1)} %negate_power_fusion, f32[1536]{0:T(1024)S(1)} %fusion.7), kind=kLoop, calls=%fused_computation.2 | loop fusion | flops 1769472 | bytes 7085568 | tf_op jit(solution)/shard_map/cos | solution.py:596
  41.5 7.8 %all-to-all-done = bf16[8,48,768]{2,1,0:T(8,128)(2,1)} async-done(((bf16[8,48,768]{2,1,0:T(8,128)(2,1)}), bf16[8,48,768]{2,1,0:T(8,128)(2,1)}, u32[]{:S(2)}, u32[]{:S(2)}) %all-to-all-start) | async-done | bytes 589856 | tf_op jit(solution)/shard_map/all_to_all | solution.py:790
  49.3 1.5 collective-permute-start
  50.7 3.0 pad_maximum_fusion
  53.7 2.5 copy.72.kpt_ref
  56.3 1.9 stack.29.place
  58.8 1.5 collective-permute-start.1
  60.9 1.3 slice.278
  66.4 4.5 %collective-permute-done.1.x2 = bf16[384,768]{1,0:T(8,128)(2,1)S(1)} collective-permute-done((bf16[384,768]{1,0:T(8,128)(2,1)}, bf16[384,768]{1,0:T(8,128)(2,1)S(1)}, u32[]{:S(2)}, u32[]{:S(2)}) %collective-permute-start.1) | collective-permute-done | bytes 589856 | tf_op jit(solution)/shard_map/ppermute | solution.py:618
  70.9 6.4 %collective-permute-done.2.x3 = bf16[384,768]{1,0:T(8,128)(2,1)} collective-permute-done((bf16[384,768]{1,0:T(8,128)(2,1)}, bf16[384,768]{1,0:T(8,128)(2,1)}, u32[]{:S(2)}, u32[]{:S(2)}) %collective-permute-start.2) | collective-permute-done | bytes 589856 | tf_op jit(solution)/shard_map/ppermute | solution.py:618
  80.0 14.0 %project.1 = (bf16[3,1536,128]{2,1,0:T(8,128)(2,1)}, bf16[3,1536,128]{2,1,0:T(8,128)(2,1)}, bf16[3,1536,128]{2,1,0:T(8,128)(2,1)}, bf16[3,128,1536]{2,1,0:T(8,12...) custom-call(s32[5]{0:T(128)} %stack.29.place, bf16[384,768]{1,0:T(8,128)(2,1)} %bitcast.5.x0.x_ref, ...), custom_call_target="tpu_custom_call" | custom-call | flops 1509949440 | bytes 10000000 | tf_op jit(solution)/shard_map/project/pallas_call | solution.py:100
  94.0 30.2 %attend.1 = (bf16[3,1024,1024]{2,1,0:T(8,128)(2,1)}, bf16[3,512,512]{2,1,0:T(8,128)(2,1)}, f32[3,1536,128]{2,1,0:T(8,128)}, bf16[384,192]{1,0:T(8,128)(2,1)}, bf...) custom-call(s32[5]{0:T(128)} %stack.29.place, ...), custom_call_target="tpu_custom_call" | custom-call | flops 12000000000 | bytes 20000000 | tf_op jit(solution)/shard_map/attend/pallas_call | solution.py:175
  124.2 1.5 collective-permute-start.3
  129.5 2.7 collective-permute-done.3.a1
  132.3 4.3 %collective-permute-done.5.a3 = bf16[384,192]{1,0:T(8,128)(2,1)S(1)} collective-permute-done((bf16[384,192]{1,0:T(8,128)(2,1)}, bf16[384,192]{1,0:T(8,128)(2,1)S(1)}, u32[]{:S(2)}, u32[]{:S(2)}) %collective-permute-start.5) | collective-permute-done | bytes 147488 | tf_op jit(solution)/shard_map/ppermute | solution.py:618
  136.6 4.3 %all-gather.7.cloned.1.call-done = bf16[3072,1792]{1,0:T(8,128)(2,1)} async-done(((bf16[96,1792]{1,0:T(8,128)(2,1)}), bf16[3072,1792]{1,0:T(8,128)(2,1)}) %all-gather.7.cloned.1.call-update) | async-done | bytes 11010064 | tf_op jit(solution)/shard_map/all_gather | solution.py:853
  140.9 22.3 %middle.1 = (bf16[384,768]{1,0:T(8,128)(2,1)}, bf16[384,768]{1,0:T(8,128)(2,1)}, bf16[384,3072]{1,0:T(8,128)(2,1)}, bf16[384,3072]{1,0:T(8,128)(2,1)}, bf16[384,...) custom-call(s32[5]{0:T(128)} %stack.29.place, ...), custom_call_target="tpu_custom_call" | custom-call | flops 8000000000 | bytes 20000000 | tf_op jit(solution)/shard_map/middle/pallas_call | solution.py:572
  163.2 9.0 %in_blocks.1 = (bf16[16,128,768]{2,1,0:T(8,128)(2,1)}, bf16[16,128,768]{2,1,0:T(8,128)(2,1)}) custom-call(s32[35]{0:T(128)} %get-tuple-element.251.place, bf16[384,768]{1,0:T(8,128)(2,1)} %get-tuple-element.125.h_ref, bf16[384,3072]{1,0:T(8,128)(2,1)} %get-tuple-element.126.dz_ref, bf16[384,192]{1,0:T(8,128)(2,1)} %get-tuple-element.111.a0, ...), custom_call_target="tpu_custom_call" | custom-call | flops 2264924160 | bytes 12000000 | tf_op jit(solution)/shard_map/in_blocks/pallas_call | solution.py:738
  172.4 9.4 %back_blocks.1 = (bf16[16,96,768]{2,1,0:T(8,128)(2,1)}, bf16[16,96,768]{2,1,0:T(8,128)(2,1)}) custom-call(s32[35]{0:T(128)} %get-tuple-element.250.place, bf16[384,3072]{1,0:T(8,128)(2,1)} %get-tuple-element.121.u_ref, bf16[384,768]{1,0:T(8,128)(2,1)} %get-tuple-element.122.df_ref), custom_call_target="tpu_custom_call" | custom-call | flops 1811939328 | bytes 8000000 | tf_op jit(solution)/shard_map/back_blocks/pallas_call | solution.py:675
  182.1 1.4 collective-permute-start.6
  184.1 1.5 collective-permute-start.8
  186.5 1.4 copy-done.3
  187.9 1.7 copy-done.2
  189.6 4.6 %merge.4 = (bf16[8,96,768]{2,1,0:T(8,128)(2,1)}, bf16[8,128,768]{2,1,0:T(8,128)(2,1)}) custom-call(bf16[16,96,768]{2,1,0:T(8,128)(2,1)} %get-tuple-element.170.refs_0_, bf16[16,96,768]{2,1,0:T(8,128)(2,1)} %copy-done.3, bf16[16,128,768]{2,1,0:T(8,128)(2,1)} %get-tuple-element.175.refs_2_.refs_3_.refs_4_.refs_5_, bf16[16,128,768]{2,1,0:T(8,128)(2,1)} %copy-done.2), custom_call_target="tpu_custom_call" | custom-call | flops 8257536 | bytes 11010048 | tf_op jit(solution)/shard_map/merge/pallas_call | solution.py:455
  196.5 36.3 %attend_back.1 = (bf16[768,640]{1,0:T(8,128)(2,1)}, bf16[768,640]{1,0:T(8,128)(2,1)}, f32[768,256]{1,0:T(8,128)}, f32[3,8,128]{2,1,0:T(8,128)}) custom-call(s32[5]{0:T(128)} %stack.29.place, bf16[384,192]{1,0:T(8,128)(2,1)} %get-tuple-element.133.d0, bf16[384,192]{1,0:T(8,128)(2,1)} %copy-done.20, bf16[384,192]{1,0:T(8,128)(2,1)} %copy-done.23, ...), custom_call_target="tpu_custom_call" | custom-call | flops 20000000000 | bytes 25000000 | tf_op jit(solution)/shard_map/attend_back/pallas_call | solution.py:337
  232.7 5.9 %qkv_blocks.1 = bf16[8,104,768]{2,1,0:T(8,128)(2,1)} custom-call(bf16[384,768]{1,0:T(8,128)(2,1)} %bitcast.5.x0.x_ref, bf16[384,768]{1,0:T(8,128)(2,1)} %collective-permute-done.x1, bf16[384,768]{1,0:T(8,128)(2,1)} %copy-done.16, bf16[384,768]{1,0:T(8,128)(2,1)} %collective-permute-done.2.x3, bf16[768,640]{1,0:T(8,128)(2,1)} %get-tuple-element.143.tkeep_ref, ...), custom_call_target="tpu_custom_call" | custom-call | flops 2000000000 | bytes 8000000 | tf_op jit(solution)/shard_map/qkv_blocks/pallas_call | solution.py:419
  238.7 3.7 %convolution_convert_fusion = bf16[768,768]{1,0:T(8,128)(2,1)} fusion(bf16[768,640]{1,0:T(8,128)(2,1)} %get-tuple-element.144.tsend_ref, bf16[768,640]{1,0:T(8,128)(2,1)} %maximum_maximum_fusion.w_ref), kind=kOutput, calls=%fused_computation.4 | convolution fusion | flops 755564544 | bytes 3145728 | tf_op jit(solution)/shard_map/dot_general | solution.py:606
  243.9 3.2 merge.5
  249.1 2.6 fusion.17
  251.7 21.9 %collective-permute-done.14.refs_3_ = bf16[4,96,768]{2,1,0:T(8,128)(2,1)S(1)} collective-permute-done((bf16[4,96,768]{2,1,0:T(8,128)(2,1)}, bf16[4,96,768]{2,1,0:T(8,128)(2,1)S(1)}, u32[]{:S(2)}, u32[]{:S(2)}) %collective-permute-start.14) | collective-permute-done | bytes 589856 | tf_op jit(solution)/shard_map/ppermute | solution.py:618
  273.6 2.5 fusion
  276.9 2.8 merge.6
  279.7 1.4 collective-permute-start.18
  284.3 5.1 %collective-permute-done.17.refs_4_ = bf16[2,96,768]{2,1,0:T(8,128)(2,1)} collective-permute-done((bf16[2,96,768]{2,1,0:T(8,128)(2,1)}, bf16[2,96,768]{2,1,0:T(8,128)(2,1)}, u32[]{:S(2)}, u32[]{:S(2)}) %collective-permute-start.17) | collective-permute-done | bytes 294944 | tf_op jit(solution)/shard_map/ppermute | solution.py:618
  289.5 2.5 merge.7
  292.1 1.5 collective-permute-start.19
  294.1 1.5 collective-permute-start.21
  295.6 1.3 collective-permute-start.22
  296.9 2.3 fusion.3
  299.2 3.7 %all-to-all-start.1 = ((bf16[8,48,768]{2,1,0:T(8,128)(2,1)}), bf16[8,48,768]{2,1,0:T(8,128)(2,1)S(1)}, u32[]{:S(2)}, u32[]{:S(2)}) async-start(bf16[8,48,768]{2,1,0:T(8,128)(2,1)} %bitcast.32), calls=%async_computation.1 | async-start | bytes 1179648 | tf_op jit(solution)/shard_map/all_to_all | solution.py:960
  310.7 13.2 %all-to-all-done.1.in_ref = bf16[8,48,768]{2,1,0:T(8,128)(2,1)S(1)} async-done(((bf16[8,48,768]{2,1,0:T(8,128)(2,1)}), bf16[8,48,768]{2,1,0:T(8,128)(2,1)S(1)}, u32[]{:S(2)}, u32[]{:S(2)}) %all-to-all-start.1) | async-done | bytes 589856 | tf_op jit(solution)/shard_map/all_to_all | solution.py:960
  324.8 2.0 reload.1
  326.8 2.1 add_bitcast_fusion
  328.9 1.5 convert_add_fusion
  (176 shorter events, 45.2 us)
Async XLA Ops:
  7.2 2.4 copy-start
  7.2 53.7 %all-gather.5.cloned.1.call-start = ((), (), s32[]{:S(2)}) async-start(), calls=%async_computation.4 | async-start | bytes 1437696 | tf_op jit(solution)/shard_map/all_gather | solution.py:817
  12.4 128.5 %all-gather.7.cloned.1.call-start = ((), (), s32[]{:S(2)}) async-start(), calls=%async_computation.5 | async-start | bytes 11354112 | tf_op jit(solution)/shard_map/all_gather | solution.py:853
  14.4 9.2 %copy-start.13 = (s32[8]{0:T(128)S(1)}, s32[8]{0:T(128)}, u32[]{:S(2)}) copy-start(s32[8]{0:T(128)} %owners.3) | copy-start | bytes 100
  14.4 9.3 %copy-start.14 = (s32[8,3]{0,1:T(4,128)S(1)}, s32[8,3]{0,1:T(4,128)}, u32[]{:S(2)}) copy-start(s32[8,3]{0,1:T(4,128)} %param.44) | copy-start | bytes 292
  14.4 10.7 %copy-start.12 = (s32[8,1536]{1,0:T(8,128)S(1)}, s32[8,1536]{1,0:T(8,128)}, u32[]{:S(2)}) copy-start(s32[8,1536]{1,0:T(8,128)} %param.45) | copy-start | bytes 147460
  17.3 32.0 %all-to-all-start = ((bf16[8,48,768]{2,1,0:T(8,128)(2,1)}), bf16[8,48,768]{2,1,0:T(8,128)(2,1)}, u32[]{:S(2)}, u32[]{:S(2)}) async-start(bf16[8,48,768]{2,1,0:T(8,128)(2,1)} %deal.1), calls=%async_computation | async-start | bytes 1179648 | tf_op jit(solution)/shard_map/all_to_all | solution.py:790
  23.6 259.8 %reduce-scatter.2.cloned.1.call-start = ((), (), s32[]{:S(2)}) async-start(), calls=%async_computation.3 | async-start | bytes 1437696 | tf_op jit(solution)/shard_map/reduce_scatter | solution.py:940
  49.3 11.0 %collective-permute-start = (bf16[384,768]{1,0:T(8,128)(2,1)}, bf16[384,768]{1,0:T(8,128)(2,1)}, u32[]{:S(2)}, u32[]{:S(2)}) collective-permute-start(bf16[384,768]{1,0:T(8,128)(2,1)} %bitcast.5.x0.x_ref), channel_id=1, source_target_pairs={{0,8},{1,17},{2,10},{3,19},{4,12},{5,21},{6,14},{7,23},{8,0},{9,25... | collective-permute-start | bytes 1769480 | tf_op jit(solution)/shard_map/ppermute | solution.py:618
  58.8 12.1 %collective-permute-start.1 = (bf16[384,768]{1,0:T(8,128)(2,1)}, bf16[384,768]{1,0:T(8,128)(2,1)S(1)}, u32[]{:S(2)}, u32[]{:S(2)}) collective-permute-start(bf16[384,768]{1,0:T(8,128)(2,1)} %bitcast.5.x0.x_ref), channel_id=1, source_target_pairs={{0,16},{1,9},{2,18},{3,11},{4,20},{5,13},{6,22},{7,15},{8,24},{9,1... | collective-permute-start | bytes 1769480 | tf_op jit(solution)/shard_map/ppermute | solution.py:618
  60.3 17.0 %collective-permute-start.2 = (bf16[384,768]{1,0:T(8,128)(2,1)}, bf16[384,768]{1,0:T(8,128)(2,1)}, u32[]{:S(2)}, u32[]{:S(2)}) collective-permute-start(bf16[384,768]{1,0:T(8,128)(2,1)} %collective-permute-done.x1), channel_id=1, source_target_pairs={{0,16},{1,9},{2,18},{3,11},{4,20},{5,13},{6,22},{7,15},{8,24},{9,1... | collective-permute-start | bytes 1769480 | tf_op jit(solution)/shard_map/ppermute | solution.py:618
  70.9 9.1 %copy-start.16 = (bf16[384,768]{1,0:T(8,128)(2,1)}, bf16[384,768]{1,0:T(8,128)(2,1)S(1)}, u32[]{:S(2)}) copy-start(bf16[384,768]{1,0:T(8,128)(2,1)S(1)} %collective-permute-done.1.x2) | copy-start | bytes 1769476
  124.2 8.1 %collective-permute-start.3 = (bf16[384,192]{1,0:T(8,128)(2,1)}, bf16[384,192]{1,0:T(8,128)(2,1)S(1)}, u32[]{:S(2)}, u32[]{:S(2)}) collective-permute-start(bf16[384,192]{1,0:T(8,128)(2,1)} %get-tuple-element.112), channel_id=1, source_target_pairs={{0,8},{1,17},{2,10},{3,19},{4,12},{5,21},{6,14},{7,23},{8,0},{9,25... | collective-permute-start | bytes 442376 | tf_op jit(solution)/shard_map/ppermute | solution.py:618
  125.7 6.6 %collective-permute-start.4 = (bf16[384,192]{1,0:T(8,128)(2,1)}, bf16[384,192]{1,0:T(8,128)(2,1)S(1)}, u32[]{:S(2)}, u32[]{:S(2)}) collective-permute-start(bf16[384,192]{1,0:T(8,128)(2,1)} %get-tuple-element.113), channel_id=1, source_target_pairs={{0,16},{1,9},{2,18},{3,11},{4,20},{5,13},{6,22},{7,15},{8,24},{9,1... | collective-permute-start | bytes 442376 | tf_op jit(solution)/shard_map/ppermute | solution.py:618
  126.8 9.8 %collective-permute-start.5 = (bf16[384,192]{1,0:T(8,128)(2,1)}, bf16[384,192]{1,0:T(8,128)(2,1)S(1)}, u32[]{:S(2)}, u32[]{:S(2)}) collective-permute-start(bf16[384,192]{1,0:T(8,128)(2,1)} %get-tuple-element.114), channel_id=1, source_target_pairs={{0,24},{1,25},{2,26},{3,27},{4,28},{5,29},{6,30},{7,31},{8,16},{9,... | collective-permute-start | bytes 442376 | tf_op jit(solution)/shard_map/ppermute | solution.py:618
  132.3 8.6 %copy-start.17 = (bf16[384,192]{1,0:T(8,128)(2,1)}, bf16[384,192]{1,0:T(8,128)(2,1)S(1)}, u32[]{:S(2)}) copy-start(bf16[384,192]{1,0:T(8,128)(2,1)S(1)} %collective-permute-done.3.a1) | copy-start | bytes 442372
  132.3 8.6 %copy-start.19 = (bf16[384,192]{1,0:T(8,128)(2,1)}, bf16[384,192]{1,0:T(8,128)(2,1)S(1)}, u32[]{:S(2)}) copy-start(bf16[384,192]{1,0:T(8,128)(2,1)S(1)} %collective-permute-done.4.a2) | copy-start | bytes 442372
  136.6 4.3 %copy-start.22 = (bf16[384,192]{1,0:T(8,128)(2,1)}, bf16[384,192]{1,0:T(8,128)(2,1)S(1)}, u32[]{:S(2)}) copy-start(bf16[384,192]{1,0:T(8,128)(2,1)S(1)} %collective-permute-done.5.a3) | copy-start | bytes 442372
  172.2 14.4 %collective-permute-start.10 = (bf16[16,128,768]{2,1,0:T(8,128)(2,1)}, bf16[16,128,768]{2,1,0:T(8,128)(2,1)S(1)}, u32[]{:S(2)}, u32[]{:S(2)}) collective-permute-start(bf16[16,128,768]{2,1,0:T(8,128)(2,1)} %get-tuple-element.130), channel_id=1, source_target_pairs={{0,1},{1,0},{2,3},{3,2},{4,5},{5,4},{6,7},{7,6},{8,9},{9,8},{10,11... | collective-permute-start | bytes 9437192 | tf_op jit(solution)/shard_map/ppermute | solution.py:618
  172.4 11.1 %copy-start.21 = (bf16[384,192]{1,0:T(8,128)(2,1)S(1)}, bf16[384,192]{1,0:T(8,128)(2,1)}, u32[]{:S(2)}) copy-start(bf16[384,192]{1,0:T(8,128)(2,1)} %get-tuple-element.119) | copy-start | bytes 442372
  172.4 11.7 %copy-start.18 = (bf16[384,192]{1,0:T(8,128)(2,1)S(1)}, bf16[384,192]{1,0:T(8,128)(2,1)}, u32[]{:S(2)}) copy-start(bf16[384,192]{1,0:T(8,128)(2,1)} %get-tuple-element.120) | copy-start | bytes 442372
  181.8 4.7 %collective-permute-start.9 = (bf16[16,96,768]{2,1,0:T(8,128)(2,1)}, bf16[16,96,768]{2,1,0:T(8,128)(2,1)S(1)}, u32[]{:S(2)}, u32[]{:S(2)}) collective-permute-start(bf16[16,96,768]{2,1,0:T(8,128)(2,1)} %get-tuple-element.124), channel_id=1, source_target_pairs={{0,1},{1,0},{2,3},{3,2},{4,5},{5,4},{6,7},{7,6},{8,9},{9,8},{10,11... | collective-permute-start | bytes 7077896 | tf_op jit(solution)/shard_map/ppermute | solution.py:618
  182.1 12.2 %collective-permute-start.6 = (bf16[384,192]{1,0:T(8,128)(2,1)}, bf16[384,192]{1,0:T(8,128)(2,1)S(1)}, u32[]{:S(2)}, u32[]{:S(2)}) collective-permute-start(bf16[384,192]{1,0:T(8,128)(2,1)} %get-tuple-element.118), channel_id=1, source_target_pairs={{0,8},{1,17},{2,10},{3,19},{4,12},{5,21},{6,14},{7,23},{8,0},{9,25... | collective-permute-start | bytes 442376 | tf_op jit(solution)/shard_map/ppermute | solution.py:618
  183.5 10.8 %collective-permute-start.7 = (bf16[384,192]{1,0:T(8,128)(2,1)S(1)}, bf16[384,192]{1,0:T(8,128)(2,1)S(1)}, u32[]{:S(2)}, u32[]{:S(2)}) collective-permute-start(bf16[384,192]{1,0:T(8,128)(2,1)S(1)} %copy-done.21), channel_id=1, source_target_pairs={{0,16},{1,9},{2,18},{3,11},{4,20},{5,13},{6,22},{7,15},{8,24},{9,1... | collective-permute-start | bytes 442376 | tf_op jit(solution)/shard_map/ppermute | solution.py:618
  184.1 10.5 %collective-permute-start.8 = (bf16[384,192]{1,0:T(8,128)(2,1)S(1)}, bf16[384,192]{1,0:T(8,128)(2,1)}, u32[]{:S(2)}, u32[]{:S(2)}) collective-permute-start(bf16[384,192]{1,0:T(8,128)(2,1)S(1)} %copy-done.18), channel_id=1, source_target_pairs={{0,24},{1,25},{2,26},{3,27},{4,28},{5,29},{6,30},{7,31},{8,16},{9,... | collective-permute-start | bytes 442376 | tf_op jit(solution)/shard_map/ppermute | solution.py:618
  187.9 1.7 copy-start.2
  194.2 2.2 copy-start.20
  194.2 2.2 copy-start.23
  194.6 47.7 %collective-permute-start.12 = (bf16[8,128,768]{2,1,0:T(8,128)(2,1)}, bf16[8,128,768]{2,1,0:T(8,128)(2,1)S(1)}, u32[]{:S(2)}, u32[]{:S(2)}) collective-permute-start(bf16[8,128,768]{2,1,0:T(8,128)(2,1)} %get-tuple-element.146), channel_id=1, source_target_pairs={{0,8},{1,17},{2,10},{3,19},{4,12},{5,21},{6,14},{7,23},{8,0},{9,25... | collective-permute-start | bytes 4718600 | tf_op jit(solution)/shard_map/ppermute | solution.py:618
  195.7 46.6 %collective-permute-start.11 = (bf16[8,96,768]{2,1,0:T(8,128)(2,1)}, bf16[8,96,768]{2,1,0:T(8,128)(2,1)S(1)}, u32[]{:S(2)}, u32[]{:S(2)}) collective-permute-start(bf16[8,96,768]{2,1,0:T(8,128)(2,1)} %get-tuple-element.145), channel_id=1, source_target_pairs={{0,2},{1,3},{2,0},{3,1},{4,6},{5,7},{6,4},{7,5},{8,10},{9,11},{10,... | collective-permute-start | bytes 3538952 | tf_op jit(solution)/shard_map/ppermute | solution.py:618
  242.4 31.2 %collective-permute-start.13 = (bf16[768,768]{1,0:T(8,128)(2,1)}, bf16[768,768]{1,0:T(8,128)(2,1)}, u32[]{:S(2)}, u32[]{:S(2)}) collective-permute-start(bf16[768,768]{1,0:T(8,128)(2,1)} %convolution_convert_fusion), channel_id=1, source_target_pairs={{0,8},{1,17},{2,10},{3,19},{4,12},{5,21},{6,14},{7,23},{8,0},{9,25... | collective-permute-start | bytes 3538952 | tf_op jit(solution)/shard_map/ppermute | solution.py:618
  247.0 26.6 %collective-permute-start.15 = (bf16[4,128,768]{2,1,0:T(8,128)(2,1)}, bf16[4,128,768]{2,1,0:T(8,128)(2,1)S(1)}, u32[]{:S(2)}, u32[]{:S(2)}) collective-permute-start(bf16[4,128,768]{2,1,0:T(8,128)(2,1)} %get-tuple-element.157), channel_id=1, source_target_pairs={{0,16},{1,9},{2,18},{3,11},{4,20},{5,13},{6,22},{7,15},{8,24},{9,1... | collective-permute-start | bytes 2359304 | tf_op jit(solution)/shard_map/ppermute | solution.py:618
  247.9 25.7 %collective-permute-start.14 = (bf16[4,96,768]{2,1,0:T(8,128)(2,1)}, bf16[4,96,768]{2,1,0:T(8,128)(2,1)S(1)}, u32[]{:S(2)}, u32[]{:S(2)}) collective-permute-start(bf16[4,96,768]{2,1,0:T(8,128)(2,1)} %get-tuple-element.156), channel_id=1, source_target_pairs={{0,8},{1,17},{2,10},{3,19},{4,12},{5,21},{6,14},{7,23},{8,0},{9,25... | collective-permute-start | bytes 1769480 | tf_op jit(solution)/shard_map/ppermute | solution.py:618
  251.7 21.9 %copy-start.9 = (f32[768,768]{1,0:T(8,128)}, f32[768,768]{1,0:T(8,128)S(1)}, u32[]{:S(2)}) copy-start(f32[768,768]{1,0:T(8,128)S(1)} %fusion.17) | copy-start | bytes 7077892
  273.6 3.3 copy-start.7
  273.6 3.3 copy-start.6
  276.1 13.4 %collective-permute-start.16 = (bf16[384,768]{1,0:T(8,128)(2,1)}, bf16[384,768]{1,0:T(8,128)(2,1)}, u32[]{:S(2)}, u32[]{:S(2)}) collective-permute-start(bf16[384,768]{1,0:T(8,128)(2,1)} %fusion), channel_id=1, source_target_pairs={{0,16},{1,9},{2,18},{3,11},{4,20},{5,13},{6,22},{7,15},{8,24},{9,1... | collective-permute-start | bytes 1769480 | tf_op jit(solution)/shard_map/ppermute | solution.py:618
  279.7 9.8 %collective-permute-start.18 = (bf16[2,128,768]{2,1,0:T(8,128)(2,1)}, bf16[2,128,768]{2,1,0:T(8,128)(2,1)}, u32[]{:S(2)}, u32[]{:S(2)}) collective-permute-start(bf16[2,128,768]{2,1,0:T(8,128)(2,1)} %get-tuple-element.168), channel_id=1, source_target_pairs={{0,2},{1,3},{2,0},{3,1},{4,6},{5,7},{6,4},{7,5},{8,10},{9,11},{10,... | collective-permute-start | bytes 1179656 | tf_op jit(solution)/shard_map/ppermute | solution.py:618
  281.7 7.7 %collective-permute-start.17 = (bf16[2,96,768]{2,1,0:T(8,128)(2,1)}, bf16[2,96,768]{2,1,0:T(8,128)(2,1)}, u32[]{:S(2)}, u32[]{:S(2)}) collective-permute-start(bf16[2,96,768]{2,1,0:T(8,128)(2,1)} %get-tuple-element.167), channel_id=1, source_target_pairs={{0,16},{1,9},{2,18},{3,11},{4,20},{5,13},{6,22},{7,15},{8,24},{9,1... | collective-permute-start | bytes 884744 | tf_op jit(solution)/shard_map/ppermute | solution.py:618
  284.3 12.6 %copy-start.10 = (f32[768,768]{1,0:T(8,128)S(1)}, f32[768,768]{1,0:T(8,128)}, u32[]{:S(2)}) copy-start(f32[768,768]{1,0:T(8,128)} %copy-done.9) | copy-start | bytes 7077892
  284.3 12.6 %copy-start.11 = (f32[384,768]{1,0:T(8,128)S(1)}, f32[384,768]{1,0:T(8,128)}, u32[]{:S(2)}) copy-start(f32[384,768]{1,0:T(8,128)} %get-tuple-element.116) | copy-start | bytes 3538948
  292.1 14.9 %collective-permute-start.19 = (bf16[1,24,768]{2,1,0:T(8,128)(2,1)S(1)}, bf16[1,24,768]{2,1,0:T(8,128)(2,1)S(1)}, u32[]{:S(2)}, u32[]{:S(2)}) collective-permute-start(bf16[1,24,768]{2,1,0:T(8,128)(2,1)S(1)} %get-tuple-element.240), channel_id=1, source_target_pairs={{0,8},{1,17},{2,10},{3,19},{4,12},{5,21},{6,14},{7,23},{8,0},{9,25... | collective-permute-start | bytes 110600 | tf_op jit(solution)/shard_map/ppermute | solution.py:618
  293.5 13.4 %collective-permute-start.20 = (bf16[1,24,768]{2,1,0:T(8,128)(2,1)S(1)}, bf16[1,24,768]{2,1,0:T(8,128)(2,1)S(1)}, u32[]{:S(2)}, u32[]{:S(2)}) collective-permute-start(bf16[1,24,768]{2,1,0:T(8,128)(2,1)S(1)} %get-tuple-element.239), channel_id=1, source_target_pairs={{0,16},{1,9},{2,18},{3,11},{4,20},{5,13},{6,22},{7,15},{8,24},{9,1... | collective-permute-start | bytes 110600 | tf_op jit(solution)/shard_map/ppermute | solution.py:618
  294.1 12.8 %collective-permute-start.21 = (bf16[1,24,768]{2,1,0:T(8,128)(2,1)S(1)}, bf16[1,24,768]{2,1,0:T(8,128)(2,1)S(1)}, u32[]{:S(2)}, u32[]{:S(2)}) collective-permute-start(bf16[1,24,768]{2,1,0:T(8,128)(2,1)S(1)} %get-tuple-element.238), channel_id=1, source_target_pairs={{0,24},{1,25},{2,26},{3,27},{4,28},{5,29},{6,30},{7,31},{8,16},{9,... | collective-permute-start | bytes 110600 | tf_op jit(solution)/shard_map/ppermute | solution.py:618
  295.6 31.1 %collective-permute-start.22 = (bf16[1,224,768]{2,1,0:T(8,128)(2,1)}, bf16[1,224,768]{2,1,0:T(8,128)(2,1)}, u32[]{:S(2)}, u32[]{:S(2)}) collective-permute-start(bf16[1,224,768]{2,1,0:T(8,128)(2,1)} %merge.7), channel_id=1, source_target_pairs={{0,4},{1,5},{2,6},{3,7},{4,0},{5,1},{6,2},{7,3},{8,12},{9,13},{10,... | collective-permute-start | bytes 1032200 | tf_op jit(solution)/shard_map/ppermute | solution.py:618
  299.2 8.5 %copy-start.15 = (pred[4]{0:T(512)(128)(4,1)S(1)}, pred[4]{0:T(512)(128)(4,1)}, u32[]{:S(2)}) copy-start(pred[4]{0:T(512)(128)(4,1)} %compare_and_fusion) | copy-start | bytes 16
  299.2 24.7 %all-to-all-start.1 = ((bf16[8,48,768]{2,1,0:T(8,128)(2,1)}), bf16[8,48,768]{2,1,0:T(8,128)(2,1)S(1)}, u32[]{:S(2)}, u32[]{:S(2)}) async-start(bf16[8,48,768]{2,1,0:T(8,128)(2,1)} %bitcast.32), calls=%async_computation.1 | async-start | bytes 1179648 | tf_op jit(solution)/shard_map/all_to_all | solution.py:960
  326.8 6.0 %copy-start.1 = (bf16[96,768]{1,0:T(8,128)(2,1)S(1)}, bf16[96,768]{1,0:T(8,128)(2,1)}, u32[]{:S(2)}) copy-start(bf16[96,768]{1,0:T(8,128)(2,1)} %param.25) | copy-start | bytes 442372
  (4 other events, 4.9 us)
Sparse Core Ops, SparseCore 0:
  12.5 36.1 all-gather.4
  51.5 89.3 all-gather.6
  238.8 31.7 reduce-scatter.1

commit v2 on v1

--- a/solution.py
+++ b/solution.py
@@ -15,7 +15,7 @@
 F32 = jnp.float32
 VM = pl.BlockSpec(memory_space=pltpu.VMEM)
 SM = pl.BlockSpec(memory_space=pltpu.SMEM)
-VMEM_LIMIT = 60 * 1024 * 1024
+MIB = 1024 * 1024
 
 
 def lanes_of(rows, width=128):
@@ -103,7 +103,7 @@
         out_specs=[VM] * 6,
         out_shape=[tall, tall, tall, wide, tall, wide],
         scratch_shapes=[pltpu.VMEM((5, 2 * rows, 128), F32)],
-        compiler_params=pltpu.CompilerParams(vmem_limit_bytes=VMEM_LIMIT),
+        compiler_params=pltpu.CompilerParams(vmem_limit_bytes=32 * MIB),
         cost_estimate=pl.CostEstimate(flops=2 * rows * 768 * 640, bytes_accessed=10_000_000, transcendentals=0),
         name="project",
     )(place, *pieces, w_qkv, head, tcol)
@@ -203,7 +203,7 @@
             pltpu.VMEM((QB, width + 128), BF),
             pltpu.VMEM((3, 2 * rows, 128), F32),
         ],
-        compiler_params=pltpu.CompilerParams(vmem_limit_bytes=VMEM_LIMIT, dimension_semantics=("arbitrary", "arbitrary")),
+        compiler_params=pltpu.CompilerParams(vmem_limit_bytes=32 * MIB, dimension_semantics=("arbitrary", "arbitrary")),
         cost_estimate=pl.CostEstimate(flops=12_000_000_000, bytes_accessed=20_000_000, transcendentals=4_000_000),
         name="attend",
     )(place, qx, pq, kxt, vx, kpt, wrt, sn, cs)
@@ -365,7 +365,7 @@
             pltpu.VMEM((64, width), F32),
             pltpu.VMEM((5, 2 * rows, 128), F32),
         ],
-        compiler_params=pltpu.CompilerParams(vmem_limit_bytes=VMEM_LIMIT, dimension_semantics=("arbitrary", "arbitrary")),
+        compiler_params=pltpu.CompilerParams(vmem_limit_bytes=44 * MIB, dimension_semantics=("arbitrary", "arbitrary")),
         cost_estimate=pl.CostEstimate(flops=20_000_000_000, bytes_accessed=25_000_000, transcendentals=0),
         name="attend_back",
     )(place, *douts, big, small, ox, qx, pq, kx, vxt, kp, wr, sn, cs, tcol, head)
@@ -388,7 +388,7 @@
         in_specs=[SM, VM],
         out_specs=VM,
         out_shape=jax.ShapeDtypeStruct(rows.shape, rows.dtype),
-        compiler_params=pltpu.CompilerParams(vmem_limit_bytes=VMEM_LIMIT),
+        compiler_params=pltpu.CompilerParams(vmem_limit_bytes=6 * MIB),
         name="deal" if outward else "reload",
     )(owners, rows)
 
@@ -422,7 +422,7 @@
         out_specs=VM,
         out_shape=jax.ShapeDtypeStruct((count, width // count + 8, width), BF),
         scratch_shapes=[pltpu.VMEM((width, 640), F32)],
-        compiler_params=pltpu.CompilerParams(vmem_limit_bytes=VMEM_LIMIT),
+        compiler_params=pltpu.CompilerParams(vmem_limit_bytes=24 * MIB),
         cost_estimate=pl.CostEstimate(flops=2_000_000_000, bytes_accessed=8_000_000, transcendentals=0),
         name="qkv_blocks",
     )(*pieces, tkeep, tsend, rel, sums)
@@ -458,7 +458,7 @@
         in_specs=[block(p) for p in parts],
         out_specs=[pl.BlockSpec((step, h, width), lambda g: (g, 0, 0)) for h in heights],
         out_shape=[jax.ShapeDtypeStruct((half, h, width), BF) for h in heights],
-        compiler_params=pltpu.CompilerParams(vmem_limit_bytes=VMEM_LIMIT, dimension_semantics=("arbitrary",)),
+        compiler_params=pltpu.CompilerParams(vmem_limit_bytes=(14 if half == 8 else 60) * MIB, dimension_semantics=("arbitrary",)),
         cost_estimate=pl.CostEstimate(flops=half * 224 * width * 6, bytes_accessed=half * 224 * width * 8, transcendentals=0),
         name="merge",
     )(*parts)
@@ -583,7 +583,7 @@
             pltpu.VMEM((rows, width), F32),
             pltpu.VMEM((rows, width), F32),
         ],
-        compiler_params=pltpu.CompilerParams(vmem_limit_bytes=VMEM_LIMIT),
+        compiler_params=pltpu.CompilerParams(vmem_limit_bytes=44 * MIB),
         cost_estimate=pl.CostEstimate(flops=8_000_000_000, bytes_accessed=20_000_000, transcendentals=1_000_000),
         name="middle",
     )(place, *pieces, x, out_grad, weights, vectors, bin_full)
@@ -678,7 +678,7 @@
         in_specs=[SM, pl.BlockSpec((rows, hidden // 8), lambda g: (0, g)), pl.BlockSpec((rows, width), lambda g: (0, 0))],
         out_specs=[pl.BlockSpec((16, hidden // 32, width), lambda g: (0, 0, 0))] * 2,
         out_shape=[out, out],
-        compiler_params=pltpu.CompilerParams(vmem_limit_bytes=VMEM_LIMIT, dimension_semantics=("arbitrary",)),
+        compiler_params=pltpu.CompilerParams(vmem_limit_bytes=24 * MIB, dimension_semantics=("arbitrary",)),
         cost_estimate=pl.CostEstimate(flops=2 * rows * hidden * width, bytes_accessed=8_000_000, transcendentals=0),
         name="back_blocks",
     )(place, u, df)
@@ -744,7 +744,7 @@
         + [pl.BlockSpec(sums.shape, lambda g: (0, 0))],
         out_specs=[pl.BlockSpec((16, 128, width), lambda g: (0, 0, 0))] * 2,
         out_shape=[out, out],
-        compiler_params=pltpu.CompilerParams(vmem_limit_bytes=VMEM_LIMIT, dimension_semantics=("arbitrary",)),
+        compiler_params=pltpu.CompilerParams(vmem_limit_bytes=26 * MIB, dimension_semantics=("arbitrary",)),
         cost_estimate=pl.CostEstimate(flops=2 * rows * width * (dz.shape[1] + width), bytes_accessed=12_000_000, transcendentals=0),
         name="in_blocks",
     )(place, hidden_low, dz, *attn, dbr, sums)

time: 341 us -> 330 us (0.968)
  Pallas kernels: 144 us -> 121 us
  local copies, waits for them, and re-layouts: 34.4 us -> 52.4 us
  waiting for transfers between devices: 71.8 us -> 66.5 us
    unnamed x54 -> x94, local copies, waits for them, and re-layouts: 7 us -> 13.4 us
    slice x3, local copies, waits for them, and re-layouts: 0.68 us -> 5.16 us  [shards(): qkvr[:, n * local_cols:(n + 1) * local_cols].reshape(width, local_heads, DH)]
    ppermute x23, waiting for transfers between devices: 46.5 us -> 42.2 us  [across(): return lax.ppermute(values, ('seq', 'fsdp'), pairs)]
    pallas_call x1, Pallas kernels: 30.2 us -> 26 us  [attend(): pl.pallas_call(attend_body, grid=(3, blocks), in_specs=[SM, pl.BlockSpec(...]
    pallas_call x1, Pallas kernels: 8.97 us -> 5.03 us  [in_blocks(): pl.pallas_call(in_blocks_body, grid=(chunks + 1,), in_specs=[SM, whole, p...]
    pallas_call x1, Pallas kernels: 9.37 us -> 5.57 us  [back_blocks(): pl.pallas_call(back_blocks_body, grid=(8,), in_specs=[SM, pl.BlockSpec((r...]
  transfers between devices with their start and end apart: 28 -> 28, of which waited for: 12 -> 10; matrix products, arithmetic and copies ran while one was open for 16% -> 20% of each run, Pallas kernels for 33% -> 28%
where the time goes in v2:
time: 330 us; the launch traced here: 329 us
  Pallas kernels  121 us (37%)
  waiting for transfers between devices  66.5 us (20%)
  local copies, waits for them, and re-layouts  52.4 us (16%)
  starting transfers between devices  34.2 us (10%)
  other arithmetic  33.4 us (10%)
  between operations  17.8 us (5%)
    ppermute x23, waiting for transfers between devices, across(): return lax.ppermute(values, ('seq', 'fsdp'), pairs)  42.2 us
    pallas_call x1, Pallas kernels, attend_back(): pl.pallas_call(back_body, grid=(3, blocks), in_specs=[SM] + [pl.BlockSpec...  33.4 us
    pallas_call x1, Pallas kernels, attend(): pl.pallas_call(attend_body, grid=(3, blocks), in_specs=[SM, pl.BlockSpec(...  26 us
    ppermute x23, starting transfers between devices, across(): return lax.ppermute(values, ('seq', 'fsdp'), pairs)  24.2 us
    pallas_call x1, Pallas kernels, middle(): pl.pallas_call(middle_body, in_specs=[SM] + [VM] * 9, out_specs=[VM] * 12...  20.9 us
    unnamed x94, local copies, waits for them, and re-layouts  13.4 us
    all_to_all x1, waiting for transfers between devices, shards(): lax.all_to_all(input_rows, 'fsdp', split_axis=0, concat_axis=0, tiled=True)  11.8 us
    pallas_call x1, Pallas kernels, project(): pl.pallas_call(project_body, in_specs=[SM] + [VM] * 7, out_specs=[VM] * 6...  11.2 us
  transfers between devices with their start and end apart: 28, of which 10 were waited for; matrix products, arithmetic and copies ran while one was open for 20% of the time, Pallas kernels for 28%

profile of v2, /device:TPU:0, one launch (start us, length us, event | category | flops | bytes accessed | tf_op | source)
XLA Modules:
  0.0 328.6 jit_solution(5291607743359443656)
XLA Ops:
  15.4 1.4 deal.1
  16.8 6.4 %all-to-all-start = ((bf16[8,48,768]{2,1,0:T(8,128)(2,1)}), bf16[8,48,768]{2,1,0:T(8,128)(2,1)}, u32[]{:S(2)}, u32[]{:S(2)}) async-start(bf16[8,48,768]{2,1,0:T(8,128)(2,1)} %deal.1), calls=%async_computation | async-start | bytes 1179648 | tf_op jit(solution)/shard_map/all_to_all | solution.py:790
  29.7 10.4 %multiply_cosine_fusion = (f32[1536,384]{1,0:T(8,128)S(1)}, bf16[1536,384]{1,0:T(8,128)(2,1)}, bf16[1536,384]{1,0:T(8,128)(2,1)}, f32[1536,384]{1,0:T(8,128)}) fusion(f32[384]{0:T(512)S(1)} %negate_power_fusion, f32[1536]{0:T(1024)S(1)} %fusion.7), kind=kLoop, calls=%fused_computation.2 | loop fusion | flops 1769472 | bytes 7085568 | tf_op jit(solution)/shard_map/cos | solution.py:596
  40.1 9.2 %all-to-all-done = bf16[8,48,768]{2,1,0:T(8,128)(2,1)} async-done(((bf16[8,48,768]{2,1,0:T(8,128)(2,1)}), bf16[8,48,768]{2,1,0:T(8,128)(2,1)}, u32[]{:S(2)}, u32[]{:S(2)}) %all-to-all-start) | async-done | bytes 589856 | tf_op jit(solution)/shard_map/all_to_all | solution.py:790
  49.3 1.5 collective-permute-start
  50.8 4.1 %pad_maximum_fusion = (bf16[1536,768]{1,0:T(8,128)(2,1)}, bf16[768,1536]{0,1:T(8,128)(2,1)}) fusion(bf16[1536,384]{1,0:T(8,128)(2,1)} %get-tuple-element.245, bf16[1536,384]{1,0:T(8,128)(2,1)} %get-tuple-element.246), kind=kLoop, calls=%fused_computation.3 | loop fusion | flops 4718592 | bytes 7077888 | tf_op jit(solution)/shard_map/concatenate | solution.py:873
  54.9 4.3 %copy.72.kpt_ref = bf16[768,1536]{1,0:T(8,128)(2,1)} copy(bf16[768,1536]{0,1:T(8,128)(2,1)} %get-tuple-element.207) | data formatting | bytes 4718592 | tf_op jit(solution)/shard_map/transpose | solution.py:874
  60.7 1.5 collective-permute-start.1
  65.0 1.4 fusion.13
  66.4 1.9 copy.67
  68.3 1.9 copy.68
  70.2 1.9 pad_maximum_fusion.1
  72.1 2.1 copy.69
  74.9 1.9 copy.65
  76.8 2.0 copy.66
  78.8 2.2 pad.77.wr_ref
  81.0 1.8 pad.79.wrt_ref
  84.2 11.2 %project.1 = (bf16[3,1536,128]{2,1,0:T(8,128)(2,1)S(1)}, bf16[3,1536,128]{2,1,0:T(8,128)(2,1)S(1)}, bf16[3,1536,128]{2,1,0:T(8,128)(2,1)S(1)}, bf16[3,128,1536]{...) custom-call(s32[5]{0:T(128)S(1)} %stack.29.place, ...), custom_call_target="tpu_custom_call" | custom-call | flops 1509949440 | bytes 10000000 | tf_op jit(solution)/shard_map/project/pallas_call | solution.py:100
  96.6 26.0 %attend.1 = (bf16[3,1024,1024]{2,1,0:T(8,128)(2,1)}, bf16[3,512,512]{2,1,0:T(8,128)(2,1)S(1)}, f32[3,1536,128]{2,1,0:T(8,128)S(1)}, bf16[384,192]{1,0:T(8,128)(2...) custom-call(s32[5]{0:T(128)S(1)} %stack.29.place, ...), custom_call_target="tpu_custom_call" | custom-call | flops 12000000000 | bytes 20000000 | tf_op jit(solution)/shard_map/attend/pallas_call | solution.py:175
  123.3 1.5 copy-done.35
  126.3 1.5 collective-permute-start.4
  127.8 1.6 collective-permute-start.5
  130.0 3.9 %collective-permute-done.3.a1 = bf16[384,192]{1,0:T(8,128)(2,1)S(1)} collective-permute-done((bf16[384,192]{1,0:T(8,128)(2,1)}, bf16[384,192]{1,0:T(8,128)(2,1)S(1)}, u32[]{:S(2)}, u32[]{:S(2)}) %collective-permute-start.3) | collective-permute-done | bytes 147488 | tf_op jit(solution)/shard_map/ppermute | solution.py:618
  133.9 3.4 %collective-permute-done.5.a3 = bf16[384,192]{1,0:T(8,128)(2,1)S(1)} collective-permute-done((bf16[384,192]{1,0:T(8,128)(2,1)}, bf16[384,192]{1,0:T(8,128)(2,1)S(1)}, u32[]{:S(2)}, u32[]{:S(2)}) %collective-permute-start.5) | collective-permute-done | bytes 147488 | tf_op jit(solution)/shard_map/ppermute | solution.py:618
  137.4 3.2 all-gather.7.cloned.1.call-done
  141.5 20.9 %middle.1 = (bf16[384,768]{1,0:T(8,128)(2,1)}, bf16[384,768]{1,0:T(8,128)(2,1)S(1)}, bf16[384,3072]{1,0:T(8,128)(2,1)S(1)}, bf16[384,3072]{1,0:T(8,128)(2,1)}, b...) custom-call(s32[5]{0:T(128)S(1)} %stack.29.place, ...), custom_call_target="tpu_custom_call" | custom-call | flops 8000000000 | bytes 20000000 | tf_op jit(solution)/shard_map/middle/pallas_call | solution.py:572
  164.6 1.7 copy-done.32
  166.2 5.0 %in_blocks.1 = (bf16[16,128,768]{2,1,0:T(8,128)(2,1)S(1)}, bf16[16,128,768]{2,1,0:T(8,128)(2,1)S(1)}) custom-call(s32[35]{0:T(128)S(1)} %get-tuple-element.251.place, bf16[384,768]{1,0:T(8,128)(2,1)S(1)} %get-tuple-element.125.h_ref, bf16[384,3072]{1,0:T(8,128)(2,1)S(1)} %copy-done.32, bf16[384,192]{1,0:T(8,128)(2,1)S(1)} %copy-done.34, ...), custom_call_target="tpu_custom_call" | custom-call | flops 2264924160 | bytes 12000000 | tf_op jit(solution)/shard_map/in_blocks/pallas_call | solution.py:738
  171.6 5.6 %back_blocks.1 = (bf16[16,96,768]{2,1,0:T(8,128)(2,1)S(1)}, bf16[16,96,768]{2,1,0:T(8,128)(2,1)S(1)}) custom-call(s32[35]{0:T(128)S(1)} %get-tuple-element.250.place, bf16[384,3072]{1,0:T(8,128)(2,1)S(1)} %get-tuple-element.121.u_ref, bf16[384,768]{1,0:T(8,128)(2,1)S(1)} %get-tuple-element.122.df_ref), custom_call_target="tpu_custom_call" | custom-call | flops 1811939328 | bytes 8000000 | tf_op jit(solution)/shard_map/back_blocks/pallas_call | solution.py:675
  181.9 2.1 merge.4
  184.3 1.6 copy-done.3
  185.9 4.1 %collective-permute-done.8.d3 = bf16[384,192]{1,0:T(8,128)(2,1)S(1)} collective-permute-done((bf16[384,192]{1,0:T(8,128)(2,1)S(1)}, bf16[384,192]{1,0:T(8,128)(2,1)S(1)}, u32[]{:S(2)}, u32[]{:S(2)}) %collective-permute-start.8) | collective-permute-done | bytes 147488 | tf_op jit(solution)/shard_map/ppermute | solution.py:618
  191.7 33.4 %attend_back.1 = (bf16[768,640]{1,0:T(8,128)(2,1)S(1)}, bf16[768,640]{1,0:T(8,128)(2,1)S(1)}, f32[768,256]{1,0:T(8,128)S(1)}, f32[3,8,128]{2,1,0:T(8,128)S(1)}) custom-call(s32[5]{0:T(128)S(1)} %stack.29.place, bf16[384,192]{1,0:T(8,128)(2,1)S(1)} %get-tuple-element.133.d0, bf16[384,192]{1,0:T(8,128)(2,1)S(1)} %collective-permute-done.6.d1, ...), custom_call_target="tpu_custom_call" | custom-call | flops 20000000000 | bytes 25000000 | tf_op jit(solution)/shard_map/attend_back/pallas_call | solution.py:337
  225.2 5.3 %qkv_blocks.1 = bf16[8,104,768]{2,1,0:T(8,128)(2,1)} custom-call(bf16[384,768]{1,0:T(8,128)(2,1)} %bitcast.5.x0.x_ref, bf16[384,768]{1,0:T(8,128)(2,1)} %collective-permute-done.x1, bf16[384,768]{1,0:T(8,128)(2,1)} %collective-permute-done.1.x2, bf16[384,768]{1,0:T(8,128)(2,1)} %collective-permute-done.2.x3, ...), custom_call_target="tpu_custom_call" | custom-call | flops 2000000000 | bytes 8000000 | tf_op jit(solution)/shard_map/qkv_blocks/pallas_call | solution.py:419
  230.5 2.1 convolution_convert_fusion
  232.6 1.5 collective-permute-start.13
  234.1 3.3 %merge.5 = (bf16[4,96,768]{2,1,0:T(8,128)(2,1)}, bf16[4,128,768]{2,1,0:T(8,128)(2,1)}) custom-call(bf16[16,96,768]{2,1,0:T(8,128)(2,1)} %copy-done.4, bf16[16,96,768]{2,1,0:T(8,128)(2,1)} %copy-done.5, bf16[8,96,768]{2,1,0:T(8,128)(2,1)} %collective-permute-done.11.refs_2_, bf16[16,128,768]{2,1,0:T(8,128)(2,1)} %copy-done.2, ...), custom_call_target="tpu_custom_call" | custom-call | flops 4128768 | bytes 5505024 | tf_op jit(solution)/shard_map/merge/pallas_call | solution.py:455
  240.4 23.4 %collective-permute-done.14.refs_3_ = bf16[4,96,768]{2,1,0:T(8,128)(2,1)S(1)} collective-permute-done((bf16[4,96,768]{2,1,0:T(8,128)(2,1)}, bf16[4,96,768]{2,1,0:T(8,128)(2,1)S(1)}, u32[]{:S(2)}, u32[]{:S(2)}) %collective-permute-start.14) | collective-permute-done | bytes 589856 | tf_op jit(solution)/shard_map/ppermute | solution.py:618
  263.8 2.4 fusion
  267.7 2.8 merge.6
  273.2 6.3 %collective-permute-done.17.refs_4_ = bf16[2,96,768]{2,1,0:T(8,128)(2,1)} collective-permute-done((bf16[2,96,768]{2,1,0:T(8,128)(2,1)}, bf16[2,96,768]{2,1,0:T(8,128)(2,1)}, u32[]{:S(2)}, u32[]{:S(2)}) %collective-permute-start.17) | collective-permute-done | bytes 294944 | tf_op jit(solution)/shard_map/ppermute | solution.py:618
  279.8 2.5 merge.7
  287.8 2.3 fusion.3
  290.2 3.5 %all-to-all-start.1 = ((bf16[8,48,768]{2,1,0:T(8,128)(2,1)}), bf16[8,48,768]{2,1,0:T(8,128)(2,1)S(1)}, u32[]{:S(2)}, u32[]{:S(2)}) async-start(bf16[8,48,768]{2,1,0:T(8,128)(2,1)} %bitcast.121), calls=%async_computation.1 | async-start | bytes 1179648 | tf_op jit(solution)/shard_map/all_to_all | solution.py:960
  302.8 11.8 %all-to-all-done.1.in_ref = bf16[8,48,768]{2,1,0:T(8,128)(2,1)S(1)} async-done(((bf16[8,48,768]{2,1,0:T(8,128)(2,1)}), bf16[8,48,768]{2,1,0:T(8,128)(2,1)S(1)}, u32[]{:S(2)}, u32[]{:S(2)}) %all-to-all-start.1) | async-done | bytes 589856 | tf_op jit(solution)/shard_map/all_to_all | solution.py:960
  314.6 1.4 reload.1
  316.0 2.1 add_bitcast_fusion
  318.1 1.5 convert_add_fusion
  (216 shorter events, 55.8 us)
Async XLA Ops:
  7.2 55.5 %all-gather.5.cloned.1.call-start = ((), (), s32[]{:S(2)}) async-start(), calls=%async_computation.4 | async-start | bytes 1437696 | tf_op jit(solution)/shard_map/all_gather | solution.py:817
  12.4 128.2 %all-gather.7.cloned.1.call-start = ((), (), s32[]{:S(2)}) async-start(), calls=%async_computation.5 | async-start | bytes 11354112 | tf_op jit(solution)/shard_map/all_gather | solution.py:853
  14.5 10.2 %copy-start.41 = (s32[8,1536]{1,0:T(8,128)S(1)}, s32[8,1536]{1,0:T(8,128)}, u32[]{:S(2)}) copy-start(s32[8,1536]{1,0:T(8,128)} %param.45) | copy-start | bytes 147460
  16.8 32.5 %all-to-all-start = ((bf16[8,48,768]{2,1,0:T(8,128)(2,1)}), bf16[8,48,768]{2,1,0:T(8,128)(2,1)}, u32[]{:S(2)}, u32[]{:S(2)}) async-start(bf16[8,48,768]{2,1,0:T(8,128)(2,1)} %deal.1), calls=%async_computation | async-start | bytes 1179648 | tf_op jit(solution)/shard_map/all_to_all | solution.py:790
  23.2 249.1 %reduce-scatter.2.cloned.1.call-start = ((), (), s32[]{:S(2)}) async-start(), calls=%async_computation.3 | async-start | bytes 1437696 | tf_op jit(solution)/shard_map/reduce_scatter | solution.py:940
  28.4 55.8 %copy-start.13 = (s32[1536,1]{1,0:T(8,128)}, s32[1536,1]{1,0:T(8,128)S(1)}, u32[]{:S(2)}) copy-start(s32[1536,1]{1,0:T(8,128)S(1)} %broadcast_in_dim.38.tcol_ref) | copy-start | bytes 18436
  40.1 56.4 %copy-start.6 = (f32[1536,384]{1,0:T(8,128)}, f32[1536,384]{1,0:T(8,128)S(1)}, u32[]{:S(2)}) copy-start(f32[1536,384]{1,0:T(8,128)S(1)} %get-tuple-element.244.cs_ref) | copy-start | bytes 7077892
  49.3 12.9 %collective-permute-start = (bf16[384,768]{1,0:T(8,128)(2,1)}, bf16[384,768]{1,0:T(8,128)(2,1)}, u32[]{:S(2)}, u32[]{:S(2)}) collective-permute-start(bf16[384,768]{1,0:T(8,128)(2,1)} %bitcast.5.x0.x_ref), channel_id=1, source_target_pairs={{0,8},{1,17},{2,10},{3,19},{4,12},{5,21},{6,14},{7,23},{8,0},{9,25... | collective-permute-start | bytes 1769480 | tf_op jit(solution)/shard_map/ppermute | solution.py:618
  60.7 20.2 %collective-permute-start.1 = (bf16[384,768]{1,0:T(8,128)(2,1)}, bf16[384,768]{1,0:T(8,128)(2,1)}, u32[]{:S(2)}, u32[]{:S(2)}) collective-permute-start(bf16[384,768]{1,0:T(8,128)(2,1)} %bitcast.5.x0.x_ref), channel_id=1, source_target_pairs={{0,16},{1,9},{2,18},{3,11},{4,20},{5,13},{6,22},{7,15},{8,24},{9,1... | collective-permute-start | bytes 1769480 | tf_op jit(solution)/shard_map/ppermute | solution.py:618
  62.2 18.8 %collective-permute-start.2 = (bf16[384,768]{1,0:T(8,128)(2,1)}, bf16[384,768]{1,0:T(8,128)(2,1)}, u32[]{:S(2)}, u32[]{:S(2)}) collective-permute-start(bf16[384,768]{1,0:T(8,128)(2,1)} %collective-permute-done.x1), channel_id=1, source_target_pairs={{0,16},{1,9},{2,18},{3,11},{4,20},{5,13},{6,22},{7,15},{8,24},{9,1... | collective-permute-start | bytes 1769480 | tf_op jit(solution)/shard_map/ppermute | solution.py:618
  84.2 11.3 %copy-start.11 = (bf16[768,640]{1,0:T(8,128)(2,1)}, bf16[768,640]{1,0:T(8,128)(2,1)S(1)}, u32[]{:S(2)}) copy-start(bf16[768,640]{1,0:T(8,128)(2,1)S(1)} %maximum_maximum_fusion.w_ref) | copy-start | bytes 2949124
  84.2 12.3 %copy-start.7 = (f32[1536,384]{1,0:T(8,128)S(1)}, f32[1536,384]{1,0:T(8,128)}, u32[]{:S(2)}) copy-start(f32[1536,384]{1,0:T(8,128)} %get-tuple-element.247.sn_ref) | copy-start | bytes 7077892
  84.2 12.3 %copy-start.8 = (bf16[768,1536]{1,0:T(8,128)(2,1)S(1)}, bf16[768,1536]{1,0:T(8,128)(2,1)}, u32[]{:S(2)}) copy-start(bf16[768,1536]{1,0:T(8,128)(2,1)} %copy.72.kpt_ref) | copy-start | bytes 7077892
  84.2 12.3 %copy-start.17 = (bf16[3,128,768]{2,1,0:T(8,128)(2,1)S(1)}, bf16[3,128,768]{2,1,0:T(8,128)(2,1)}, u32[]{:S(2)}) copy-start(bf16[3,128,768]{2,1,0:T(8,128)(2,1)} %pad.79.wrt_ref) | copy-start | bytes 1769476
  96.5 26.1 %copy-start.24 = (bf16[3,1536,128]{2,1,0:T(8,128)(2,1)}, bf16[3,1536,128]{2,1,0:T(8,128)(2,1)S(1)}, u32[]{:S(2)}) copy-start(bf16[3,1536,128]{2,1,0:T(8,128)(2,1)S(1)} %get-tuple-element.107.qx_ref) | copy-start | bytes 3538948
  96.5 26.1 %copy-start.26 = (bf16[3,1536,128]{2,1,0:T(8,128)(2,1)}, bf16[3,1536,128]{2,1,0:T(8,128)(2,1)S(1)}, u32[]{:S(2)}) copy-start(bf16[3,1536,128]{2,1,0:T(8,128)(2,1)S(1)} %get-tuple-element.108.pq_ref) | copy-start | bytes 3538948
  96.5 26.1 %copy-start.30 = (bf16[3,128,1536]{2,1,0:T(8,128)(2,1)}, bf16[3,128,1536]{2,1,0:T(8,128)(2,1)S(1)}, u32[]{:S(2)}) copy-start(bf16[3,128,1536]{2,1,0:T(8,128)(2,1)S(1)} %get-tuple-element.141.vxt_ref) | copy-start | bytes 3538948
  96.6 44.0 %copy-start.19 = (bf16[1,384,768]{2,1,0:T(8,128)(2,1)S(1)}, bf16[1,384,768]{2,1,0:T(8,128)(2,1)}, u32[]{:S(2)}) copy-start(bf16[1,384,768]{2,1,0:T(8,128)(2,1)} %param.47) | copy-start | bytes 1769476
  125.9 8.0 %collective-permute-start.3 = (bf16[384,192]{1,0:T(8,128)(2,1)}, bf16[384,192]{1,0:T(8,128)(2,1)S(1)}, u32[]{:S(2)}, u32[]{:S(2)}) collective-permute-start(bf16[384,192]{1,0:T(8,128)(2,1)} %get-tuple-element.112), channel_id=1, source_target_pairs={{0,8},{1,17},{2,10},{3,19},{4,12},{5,21},{6,14},{7,23},{8,0},{9,25... | collective-permute-start | bytes 442376 | tf_op jit(solution)/shard_map/ppermute | solution.py:618
  126.3 7.6 %collective-permute-start.4 = (bf16[384,192]{1,0:T(8,128)(2,1)}, bf16[384,192]{1,0:T(8,128)(2,1)S(1)}, u32[]{:S(2)}, u32[]{:S(2)}) collective-permute-start(bf16[384,192]{1,0:T(8,128)(2,1)} %get-tuple-element.113), channel_id=1, source_target_pairs={{0,16},{1,9},{2,18},{3,11},{4,20},{5,13},{6,22},{7,15},{8,24},{9,1... | collective-permute-start | bytes 442376 | tf_op jit(solution)/shard_map/ppermute | solution.py:618
  127.8 9.6 %collective-permute-start.5 = (bf16[384,192]{1,0:T(8,128)(2,1)}, bf16[384,192]{1,0:T(8,128)(2,1)S(1)}, u32[]{:S(2)}, u32[]{:S(2)}) collective-permute-start(bf16[384,192]{1,0:T(8,128)(2,1)} %get-tuple-element.114), channel_id=1, source_target_pairs={{0,24},{1,25},{2,26},{3,27},{4,28},{5,29},{6,30},{7,31},{8,16},{9,... | collective-permute-start | bytes 442376 | tf_op jit(solution)/shard_map/ppermute | solution.py:618
  133.9 28.5 %copy-start.20 = (bf16[384,192]{1,0:T(8,128)(2,1)}, bf16[384,192]{1,0:T(8,128)(2,1)S(1)}, u32[]{:S(2)}) copy-start(bf16[384,192]{1,0:T(8,128)(2,1)S(1)} %collective-permute-done.4.a2) | copy-start | bytes 442372
  137.4 25.1 %copy-start.22 = (bf16[384,192]{1,0:T(8,128)(2,1)}, bf16[384,192]{1,0:T(8,128)(2,1)S(1)}, u32[]{:S(2)}) copy-start(bf16[384,192]{1,0:T(8,128)(2,1)S(1)} %collective-permute-done.5.a3) | copy-start | bytes 442372
  171.3 10.5 %copy-start.2 = (bf16[16,128,768]{2,1,0:T(8,128)(2,1)}, bf16[16,128,768]{2,1,0:T(8,128)(2,1)S(1)}, u32[]{:S(2)}) copy-start(bf16[16,128,768]{2,1,0:T(8,128)(2,1)S(1)} %get-tuple-element.175.refs_2_.refs_3_.refs_4_.refs_5_) | copy-start | bytes 9437188
  171.3 10.5 %collective-permute-start.10 = (bf16[16,128,768]{2,1,0:T(8,128)(2,1)S(1)}, bf16[16,128,768]{2,1,0:T(8,128)(2,1)S(1)}, u32[]{:S(2)}, u32[]{:S(2)}) collective-permute-start(bf16[16,128,768]{2,1,0:T(8,128)(2,1)S(1)} %get-tuple-element.130), channel_id=1, source_target_pairs={{0,1},{1,0},{2,3},{3,2},{4,5},{5,4},{6,7},{7,6},{8,9},{9,8},{10,11... | collective-permute-start | bytes 9437192 | tf_op jit(solution)/shard_map/ppermute | solution.py:618
  177.2 4.6 %collective-permute-start.9 = (bf16[16,96,768]{2,1,0:T(8,128)(2,1)S(1)}, bf16[16,96,768]{2,1,0:T(8,128)(2,1)S(1)}, u32[]{:S(2)}, u32[]{:S(2)}) collective-permute-start(bf16[16,96,768]{2,1,0:T(8,128)(2,1)S(1)} %get-tuple-element.124), channel_id=1, source_target_pairs={{0,1},{1,0},{2,3},{3,2},{4,5},{5,4},{6,7},{7,6},{8,9},{9,8},{10,11... | collective-permute-start | bytes 7077896 | tf_op jit(solution)/shard_map/ppermute | solution.py:618
  177.5 8.4 %collective-permute-start.6 = (bf16[384,192]{1,0:T(8,128)(2,1)S(1)}, bf16[384,192]{1,0:T(8,128)(2,1)S(1)}, u32[]{:S(2)}, u32[]{:S(2)}) collective-permute-start(bf16[384,192]{1,0:T(8,128)(2,1)S(1)} %get-tuple-element.118), channel_id=1, source_target_pairs={{0,8},{1,17},{2,10},{3,19},{4,12},{5,21},{6,14},{7,23},{8,0},{9,25... | collective-permute-start | bytes 442376 | tf_op jit(solution)/shard_map/ppermute | solution.py:618
  178.8 7.1 %collective-permute-start.7 = (bf16[384,192]{1,0:T(8,128)(2,1)S(1)}, bf16[384,192]{1,0:T(8,128)(2,1)S(1)}, u32[]{:S(2)}, u32[]{:S(2)}) collective-permute-start(bf16[384,192]{1,0:T(8,128)(2,1)S(1)} %get-tuple-element.119), channel_id=1, source_target_pairs={{0,16},{1,9},{2,18},{3,11},{4,20},{5,13},{6,22},{7,15},{8,24},{9,1... | collective-permute-start | bytes 442376 | tf_op jit(solution)/shard_map/ppermute | solution.py:618
  179.6 10.4 %collective-permute-start.8 = (bf16[384,192]{1,0:T(8,128)(2,1)S(1)}, bf16[384,192]{1,0:T(8,128)(2,1)S(1)}, u32[]{:S(2)}, u32[]{:S(2)}) collective-permute-start(bf16[384,192]{1,0:T(8,128)(2,1)S(1)} %get-tuple-element.120), channel_id=1, source_target_pairs={{0,24},{1,25},{2,26},{3,27},{4,28},{5,29},{6,30},{7,31},{8,16},{9,... | collective-permute-start | bytes 442376 | tf_op jit(solution)/shard_map/ppermute | solution.py:618
  181.8 9.9 %copy-start.14 = (s32[1536,1]{1,0:T(8,128)S(1)}, s32[1536,1]{1,0:T(8,128)}, u32[]{:S(2)}) copy-start(s32[1536,1]{1,0:T(8,128)} %copy-done.13) | copy-start | bytes 18436
  181.8 9.9 %copy-start.16 = (bf16[3,768,128]{2,1,0:T(8,128)(2,1)S(1)}, bf16[3,768,128]{2,1,0:T(8,128)(2,1)}, u32[]{:S(2)}) copy-start(bf16[3,768,128]{2,1,0:T(8,128)(2,1)} %pad.77.wr_ref) | copy-start | bytes 1769476
  181.8 9.9 %copy-start.25 = (bf16[3,1536,128]{2,1,0:T(8,128)(2,1)S(1)}, bf16[3,1536,128]{2,1,0:T(8,128)(2,1)}, u32[]{:S(2)}) copy-start(bf16[3,1536,128]{2,1,0:T(8,128)(2,1)} %copy-done.24) | copy-start | bytes 3538948
  190.0 42.6 %collective-permute-start.12 = (bf16[8,128,768]{2,1,0:T(8,128)(2,1)}, bf16[8,128,768]{2,1,0:T(8,128)(2,1)}, u32[]{:S(2)}, u32[]{:S(2)}) collective-permute-start(bf16[8,128,768]{2,1,0:T(8,128)(2,1)} %get-tuple-element.146), channel_id=1, source_target_pairs={{0,8},{1,17},{2,10},{3,19},{4,12},{5,21},{6,14},{7,23},{8,0},{9,25... | collective-permute-start | bytes 4718600 | tf_op jit(solution)/shard_map/ppermute | solution.py:618
  190.8 41.8 %collective-permute-start.11 = (bf16[8,96,768]{2,1,0:T(8,128)(2,1)}, bf16[8,96,768]{2,1,0:T(8,128)(2,1)}, u32[]{:S(2)}, u32[]{:S(2)}) collective-permute-start(bf16[8,96,768]{2,1,0:T(8,128)(2,1)} %get-tuple-element.145), channel_id=1, source_target_pairs={{0,2},{1,3},{2,0},{3,1},{4,6},{5,7},{6,4},{7,5},{8,10},{9,11},{10,... | collective-permute-start | bytes 3538952 | tf_op jit(solution)/shard_map/ppermute | solution.py:618
  232.6 31.2 %collective-permute-start.13 = (bf16[768,768]{1,0:T(8,128)(2,1)}, bf16[768,768]{1,0:T(8,128)(2,1)}, u32[]{:S(2)}, u32[]{:S(2)}) collective-permute-start(bf16[768,768]{1,0:T(8,128)(2,1)} %convolution_convert_fusion), channel_id=1, source_target_pairs={{0,8},{1,17},{2,10},{3,19},{4,12},{5,21},{6,14},{7,23},{8,0},{9,25... | collective-permute-start | bytes 3538952 | tf_op jit(solution)/shard_map/ppermute | solution.py:618
  237.4 26.4 %collective-permute-start.15 = (bf16[4,128,768]{2,1,0:T(8,128)(2,1)}, bf16[4,128,768]{2,1,0:T(8,128)(2,1)S(1)}, u32[]{:S(2)}, u32[]{:S(2)}) collective-permute-start(bf16[4,128,768]{2,1,0:T(8,128)(2,1)} %get-tuple-element.157), channel_id=1, source_target_pairs={{0,16},{1,9},{2,18},{3,11},{4,20},{5,13},{6,22},{7,15},{8,24},{9,1... | collective-permute-start | bytes 2359304 | tf_op jit(solution)/shard_map/ppermute | solution.py:618
  237.9 25.9 %collective-permute-start.14 = (bf16[4,96,768]{2,1,0:T(8,128)(2,1)}, bf16[4,96,768]{2,1,0:T(8,128)(2,1)S(1)}, u32[]{:S(2)}, u32[]{:S(2)}) collective-permute-start(bf16[4,96,768]{2,1,0:T(8,128)(2,1)} %get-tuple-element.156), channel_id=1, source_target_pairs={{0,8},{1,17},{2,10},{3,19},{4,12},{5,21},{6,14},{7,23},{8,0},{9,25... | collective-permute-start | bytes 1769480 | tf_op jit(solution)/shard_map/ppermute | solution.py:618
  240.3 23.4 %copy-start.39 = (f32[768,768]{1,0:T(8,128)}, f32[768,768]{1,0:T(8,128)S(1)}, u32[]{:S(2)}) copy-start(f32[768,768]{1,0:T(8,128)S(1)} %fusion.17) | copy-start | bytes 7077892
  266.2 13.6 %collective-permute-start.16 = (bf16[384,768]{1,0:T(8,128)(2,1)}, bf16[384,768]{1,0:T(8,128)(2,1)}, u32[]{:S(2)}, u32[]{:S(2)}) collective-permute-start(bf16[384,768]{1,0:T(8,128)(2,1)} %fusion), channel_id=1, source_target_pairs={{0,16},{1,9},{2,18},{3,11},{4,20},{5,13},{6,22},{7,15},{8,24},{9,1... | collective-permute-start | bytes 1769480 | tf_op jit(solution)/shard_map/ppermute | solution.py:618
  270.5 9.3 %collective-permute-start.18 = (bf16[2,128,768]{2,1,0:T(8,128)(2,1)}, bf16[2,128,768]{2,1,0:T(8,128)(2,1)}, u32[]{:S(2)}, u32[]{:S(2)}) collective-permute-start(bf16[2,128,768]{2,1,0:T(8,128)(2,1)} %get-tuple-element.168), channel_id=1, source_target_pairs={{0,2},{1,3},{2,0},{3,1},{4,6},{5,7},{6,4},{7,5},{8,10},{9,11},{10,... | collective-permute-start | bytes 1179656 | tf_op jit(solution)/shard_map/ppermute | solution.py:618
  271.4 8.2 %collective-permute-start.17 = (bf16[2,96,768]{2,1,0:T(8,128)(2,1)}, bf16[2,96,768]{2,1,0:T(8,128)(2,1)}, u32[]{:S(2)}, u32[]{:S(2)}) collective-permute-start(bf16[2,96,768]{2,1,0:T(8,128)(2,1)} %get-tuple-element.167), channel_id=1, source_target_pairs={{0,16},{1,9},{2,18},{3,11},{4,20},{5,13},{6,22},{7,15},{8,24},{9,1... | collective-permute-start | bytes 884744 | tf_op jit(solution)/shard_map/ppermute | solution.py:618
  273.2 14.6 %copy-start.10 = (f32[384,768]{1,0:T(8,128)S(1)}, f32[384,768]{1,0:T(8,128)}, u32[]{:S(2)}) copy-start(f32[384,768]{1,0:T(8,128)} %copy-done.9) | copy-start | bytes 3538948
  273.2 14.6 %copy-start.40 = (f32[768,768]{1,0:T(8,128)S(1)}, f32[768,768]{1,0:T(8,128)}, u32[]{:S(2)}) copy-start(f32[768,768]{1,0:T(8,128)} %copy-done.39) | copy-start | bytes 7077892
  283.0 14.7 %collective-permute-start.19 = (bf16[1,24,768]{2,1,0:T(8,128)(2,1)}, bf16[1,24,768]{2,1,0:T(8,128)(2,1)S(1)}, u32[]{:S(2)}, u32[]{:S(2)}) collective-permute-start(bf16[1,24,768]{2,1,0:T(8,128)(2,1)} %get-tuple-element.240), channel_id=1, source_target_pairs={{0,8},{1,17},{2,10},{3,19},{4,12},{5,21},{6,14},{7,23},{8,0},{9,25... | collective-permute-start | bytes 110600 | tf_op jit(solution)/shard_map/ppermute | solution.py:618
  284.3 13.5 %collective-permute-start.20 = (bf16[1,24,768]{2,1,0:T(8,128)(2,1)}, bf16[1,24,768]{2,1,0:T(8,128)(2,1)}, u32[]{:S(2)}, u32[]{:S(2)}) collective-permute-start(bf16[1,24,768]{2,1,0:T(8,128)(2,1)} %get-tuple-element.239), channel_id=1, source_target_pairs={{0,16},{1,9},{2,18},{3,11},{4,20},{5,13},{6,22},{7,15},{8,24},{9,1... | collective-permute-start | bytes 110600 | tf_op jit(solution)/shard_map/ppermute | solution.py:618
  285.1 12.6 %collective-permute-start.21 = (bf16[1,24,768]{2,1,0:T(8,128)(2,1)S(1)}, bf16[1,24,768]{2,1,0:T(8,128)(2,1)}, u32[]{:S(2)}, u32[]{:S(2)}) collective-permute-start(bf16[1,24,768]{2,1,0:T(8,128)(2,1)S(1)} %get-tuple-element.238), channel_id=1, source_target_pairs={{0,24},{1,25},{2,26},{3,27},{4,28},{5,29},{6,30},{7,31},{8,16},{9,... | collective-permute-start | bytes 110600 | tf_op jit(solution)/shard_map/ppermute | solution.py:618
  286.5 29.6 %collective-permute-start.22 = (bf16[1,224,768]{2,1,0:T(8,128)(2,1)}, bf16[1,224,768]{2,1,0:T(8,128)(2,1)}, u32[]{:S(2)}, u32[]{:S(2)}) collective-permute-start(bf16[1,224,768]{2,1,0:T(8,128)(2,1)} %merge.7), channel_id=1, source_target_pairs={{0,4},{1,5},{2,6},{3,7},{4,0},{5,1},{6,2},{7,3},{8,12},{9,13},{10,... | collective-permute-start | bytes 1032200 | tf_op jit(solution)/shard_map/ppermute | solution.py:618
  290.2 24.4 %all-to-all-start.1 = ((bf16[8,48,768]{2,1,0:T(8,128)(2,1)}), bf16[8,48,768]{2,1,0:T(8,128)(2,1)S(1)}, u32[]{:S(2)}, u32[]{:S(2)}) async-start(bf16[8,48,768]{2,1,0:T(8,128)(2,1)} %bitcast.121), calls=%async_computation.1 | async-start | bytes 1179648 | tf_op jit(solution)/shard_map/all_to_all | solution.py:960
  (24 other events, 108.1 us)
Sparse Core Ops, SparseCore 0:
  12.5 36.3 all-gather.4
  51.9 88.7 all-gather.6
  230.6 31.9 reduce-scatter.1

commit v3 on v2

--- a/solution.py
+++ b/solution.py
@@ -103,7 +103,7 @@
         out_specs=[VM] * 6,
         out_shape=[tall, tall, tall, wide, tall, wide],
         scratch_shapes=[pltpu.VMEM((5, 2 * rows, 128), F32)],
-        compiler_params=pltpu.CompilerParams(vmem_limit_bytes=32 * MIB),
+        compiler_params=pltpu.CompilerParams(vmem_limit_bytes=26 * MIB),
         cost_estimate=pl.CostEstimate(flops=2 * rows * 768 * 640, bytes_accessed=10_000_000, transcendentals=0),
         name="project",
     )(place, *pieces, w_qkv, head, tcol)
@@ -203,7 +203,7 @@
             pltpu.VMEM((QB, width + 128), BF),
             pltpu.VMEM((3, 2 * rows, 128), F32),
         ],
-        compiler_params=pltpu.CompilerParams(vmem_limit_bytes=32 * MIB, dimension_semantics=("arbitrary", "arbitrary")),
+        compiler_params=pltpu.CompilerParams(vmem_limit_bytes=26 * MIB, dimension_semantics=("arbitrary", "arbitrary")),
         cost_estimate=pl.CostEstimate(flops=12_000_000_000, bytes_accessed=20_000_000, transcendentals=4_000_000),
         name="attend",
     )(place, qx, pq, kxt, vx, kpt, wrt, sn, cs)
@@ -365,7 +365,7 @@
             pltpu.VMEM((64, width), F32),
             pltpu.VMEM((5, 2 * rows, 128), F32),
         ],
-        compiler_params=pltpu.CompilerParams(vmem_limit_bytes=44 * MIB, dimension_semantics=("arbitrary", "arbitrary")),
+        compiler_params=pltpu.CompilerParams(vmem_limit_bytes=36 * MIB, dimension_semantics=("arbitrary", "arbitrary")),
         cost_estimate=pl.CostEstimate(flops=20_000_000_000, bytes_accessed=25_000_000, transcendentals=0),
         name="attend_back",
     )(place, *douts, big, small, ox, qx, pq, kx, vxt, kp, wr, sn, cs, tcol, head)
@@ -422,7 +422,7 @@
         out_specs=VM,
         out_shape=jax.ShapeDtypeStruct((count, width // count + 8, width), BF),
         scratch_shapes=[pltpu.VMEM((width, 640), F32)],
-        compiler_params=pltpu.CompilerParams(vmem_limit_bytes=24 * MIB),
+        compiler_params=pltpu.CompilerParams(vmem_limit_bytes=20 * MIB),
         cost_estimate=pl.CostEstimate(flops=2_000_000_000, bytes_accessed=8_000_000, transcendentals=0),
         name="qkv_blocks",
     )(*pieces, tkeep, tsend, rel, sums)
@@ -475,12 +475,25 @@
 
 
 def middle_body(
-    place, a0, a1, a2, a3, x_ref, go_ref, w_ref, vec_ref, bin_ref,
+    place, a0, a1, a2, a3, x_ref, go_ref, w_far, vec_ref, bin_ref,
     act_ref, h_ref, u_ref, dz_ref, df_ref, dbr_ref, dr_ref, d0, d1, d2, d3, sum_ref,
-    wout, slope, high, normed, acc,
+    wout, slope, high, normed, acc, w_ref, arrived,
 ):
     own = place[0]
     width = x_ref.shape[1]
+
+    def piece_of(number, *at):
+        return pltpu.make_async_copy(w_far.at[at], w_ref.at[at], arrived.at[number])
+
+    every = slice(None)
+    out_piece = piece_of(0, every, every, every, slice(2 * width, w_far.shape[3]))
+    in_piece = lambda w: piece_of(1 + w, every, pl.ds(w, 1), every, slice(0, width))
+    back_piece = lambda w: piece_of(5 + w, pl.ds(2 * w, 2), every, every, slice(width, 2 * width))
+    out_piece.start()
+    for w in range(4):
+        in_piece(w).start()
+        back_piece(w).start()
+    out_piece.wait()
     cols = a0.shape[1]
     vector = lambda n: vec_ref[n : n + 1, :]
     for s in range(4):
@@ -506,6 +519,7 @@
 
     def forward(w, carry):
         at = pl.multiple_of(w * width, 128)
+        in_piece(w).wait()
         z = jnp.dot(h_ref[...], w_in_at(w), preferred_element_type=F32) + bin_ref[:, pl.ds(at, width)]
         square = z * z
         bend = jnp.tanh(GELU_A * z * (1.0 + GELU_B * square))
@@ -513,6 +527,7 @@
         u = (z * half).astype(BF)
         u_ref[:, pl.ds(at, width)] = u
         slope[:, pl.ds(at, width)] = half + 0.5 * z * (1.0 - bend * bend) * (GELU_A * (1.0 + 3.0 * GELU_B * square))
+        back_piece(w).wait()
         acc[...] += jnp.dot(u, w_back_at(w), preferred_element_type=F32)
         return carry
 
@@ -571,7 +586,7 @@
     full = lambda r, n: jax.ShapeDtypeStruct((r, n), F32)
     return pl.pallas_call(
         middle_body,
-        in_specs=[SM] + [VM] * 9,
+        in_specs=[SM] + [VM] * 6 + [pl.BlockSpec(memory_space=pl.ANY)] + [VM] * 2,
         out_specs=[VM] * 12,
         out_shape=[low(width), low(width), low(hidden), low(hidden), low(width), low(width), full(rows, width)]
         + [low(cols)] * 4
@@ -582,8 +597,10 @@
             pltpu.VMEM((rows, width), F32),
             pltpu.VMEM((rows, width), F32),
             pltpu.VMEM((rows, width), F32),
+            pltpu.VMEM(weights.shape, BF),
+            pltpu.SemaphoreType.DMA((9,)),
         ],
-        compiler_params=pltpu.CompilerParams(vmem_limit_bytes=44 * MIB),
+        compiler_params=pltpu.CompilerParams(vmem_limit_bytes=34 * MIB),
         cost_estimate=pl.CostEstimate(flops=8_000_000_000, bytes_accessed=20_000_000, transcendentals=1_000_000),
         name="middle",
     )(place, *pieces, x, out_grad, weights, vectors, bin_full)
@@ -678,7 +695,7 @@
         in_specs=[SM, pl.BlockSpec((rows, hidden // 8), lambda g: (0, g)), pl.BlockSpec((rows, width), lambda g: (0, 0))],
         out_specs=[pl.BlockSpec((16, hidden // 32, width), lambda g: (0, 0, 0))] * 2,
         out_shape=[out, out],
-        compiler_params=pltpu.CompilerParams(vmem_limit_bytes=24 * MIB, dimension_semantics=("arbitrary",)),
+        compiler_params=pltpu.CompilerParams(vmem_limit_bytes=16 * MIB, dimension_semantics=("arbitrary",)),
         cost_estimate=pl.CostEstimate(flops=2 * rows * hidden * width, bytes_accessed=8_000_000, transcendentals=0),
         name="back_blocks",
     )(place, u, df)
@@ -744,7 +761,7 @@
         + [pl.BlockSpec(sums.shape, lambda g: (0, 0))],
         out_specs=[pl.BlockSpec((16, 128, width), lambda g: (0, 0, 0))] * 2,
         out_shape=[out, out],
-        compiler_params=pltpu.CompilerParams(vmem_limit_bytes=26 * MIB, dimension_semantics=("arbitrary",)),
+        compiler_params=pltpu.CompilerParams(vmem_limit_bytes=18 * MIB, dimension_semantics=("arbitrary",)),
         cost_estimate=pl.CostEstimate(flops=2 * rows * width * (dz.shape[1] + width), bytes_accessed=12_000_000, transcendentals=0),
         name="in_blocks",
     )(place, hidden_low, dz, *attn, dbr, sums)
@@ -914,7 +931,7 @@
         kept, sent = back_blocks(back_table, act_low, ffn_grad)
         backs = [kept, to_core(sent)]
         back_out, in_out = merge(backs, ins, 8)
-        douts, back_out, in_out = lax.optimization_barrier((douts, back_out, in_out))
+        qx, back_out, in_out = lax.optimization_barrier((qx, back_out, in_out))
         backs.append(to_near(back_out))
         ins.append(to_first(in_out))
     else:

time: 330 us -> 324 us (0.982)
  Pallas kernels: 121 us -> 117 us
  waiting for transfers between devices: 66.5 us -> 62.6 us
    unnamed x94 -> x102, local copies, waits for them, and re-layouts: 13.4 us -> 14.3 us
where the time goes in v3:
time: 324 us; the launch traced here: 323 us
  Pallas kernels  117 us (36%)
  waiting for transfers between devices  62.6 us (19%)
  local copies, waits for them, and re-layouts  53.3 us (16%)
  starting transfers between devices  35.2 us (11%)
  other arithmetic  33.3 us (10%)
  between operations  17.8 us (5%)
    ppermute x23, waiting for transfers between devices, across(): return lax.ppermute(values, ('seq', 'fsdp'), pairs)  40.5 us
    pallas_call x1, Pallas kernels, attend_back(): pl.pallas_call(back_body, grid=(3, blocks), in_specs=[SM] + [pl.BlockSpec...  31.6 us
    pallas_call x1, Pallas kernels, attend(): pl.pallas_call(attend_body, grid=(3, blocks), in_specs=[SM, pl.BlockSpec(...  25.7 us
    ppermute x23, starting transfers between devices, across(): return lax.ppermute(values, ('seq', 'fsdp'), pairs)  25.2 us
    pallas_call x1, Pallas kernels, middle(): pl.pallas_call(middle_body, in_specs=[SM] + [VM] * 6 + [pl.BlockSpec(memo...  19.4 us
    unnamed x102, local copies, waits for them, and re-layouts  14.3 us
    all_to_all x1, waiting for transfers between devices, shards(): lax.all_to_all(input_rows, 'fsdp', split_axis=0, concat_axis=0, tiled=True)  11.9 us
    pallas_call x1, Pallas kernels, project(): pl.pallas_call(project_body, in_specs=[SM] + [VM] * 7, out_specs=[VM] * 6...  11.2 us
  transfers between devices with their start and end apart: 28, of which 10 were waited for; matrix products, arithmetic and copies ran while one was open for 20% of the time, Pallas kernels for 28%

profile of v3, /device:TPU:0, one launch (start us, length us, event | category | flops | bytes accessed | tf_op | source)
XLA Modules:
  0.0 322.7 jit_solution(9204231465915140452)
XLA Ops:
  16.8 6.4 %all-to-all-start = ((bf16[8,48,768]{2,1,0:T(8,128)(2,1)}), bf16[8,48,768]{2,1,0:T(8,128)(2,1)}, u32[]{:S(2)}, u32[]{:S(2)}) async-start(bf16[8,48,768]{2,1,0:T(8,128)(2,1)} %deal.1), calls=%async_computation | async-start | bytes 1179648 | tf_op jit(solution)/shard_map/all_to_all | solution.py:807
  29.7 10.4 %multiply_cosine_fusion = (f32[1536,384]{1,0:T(8,128)S(1)}, bf16[1536,384]{1,0:T(8,128)(2,1)}, bf16[1536,384]{1,0:T(8,128)(2,1)}, f32[1536,384]{1,0:T(8,128)}) fusion(f32[384]{0:T(512)S(1)} %negate_power_fusion, f32[1536]{0:T(1024)S(1)} %fusion.7), kind=kLoop, calls=%fused_computation.2 | loop fusion | flops 1769472 | bytes 7085568 | tf_op jit(solution)/shard_map/cos | solution.py:613
  40.1 9.2 %all-to-all-done = bf16[8,48,768]{2,1,0:T(8,128)(2,1)} async-done(((bf16[8,48,768]{2,1,0:T(8,128)(2,1)}), bf16[8,48,768]{2,1,0:T(8,128)(2,1)}, u32[]{:S(2)}, u32[]{:S(2)}) %all-to-all-start) | async-done | bytes 589856 | tf_op jit(solution)/shard_map/all_to_all | solution.py:807
  49.3 1.5 collective-permute-start
  50.8 4.0 %pad_maximum_fusion = (bf16[1536,768]{1,0:T(8,128)(2,1)}, bf16[768,1536]{0,1:T(8,128)(2,1)}) fusion(bf16[1536,384]{1,0:T(8,128)(2,1)} %get-tuple-element.239, bf16[1536,384]{1,0:T(8,128)(2,1)} %get-tuple-element.240), kind=kLoop, calls=%fused_computation.3 | loop fusion | flops 4718592 | bytes 7077888 | tf_op jit(solution)/shard_map/concatenate | solution.py:890
  54.8 4.3 %copy.72.kpt_ref = bf16[768,1536]{1,0:T(8,128)(2,1)} copy(bf16[768,1536]{0,1:T(8,128)(2,1)} %get-tuple-element.201) | data formatting | bytes 4718592 | tf_op jit(solution)/shard_map/transpose | solution.py:891
  60.7 1.5 collective-permute-start.1
  66.4 1.9 copy.67
  68.3 1.9 copy.68
  70.1 1.9 pad_maximum_fusion.1
  72.0 2.1 copy.69
  74.9 1.9 copy.65
  76.7 2.0 copy.66
  78.7 2.2 pad.77.wr_ref
  80.9 1.8 pad.79.wrt_ref
  84.2 11.2 %project.1 = (bf16[3,1536,128]{2,1,0:T(8,128)(2,1)S(1)}, bf16[3,1536,128]{2,1,0:T(8,128)(2,1)S(1)}, bf16[3,1536,128]{2,1,0:T(8,128)(2,1)S(1)}, bf16[3,128,1536]{...) custom-call(s32[5]{0:T(128)S(1)} %stack.29.place, ...), custom_call_target="tpu_custom_call" | custom-call | flops 1509949440 | bytes 10000000 | tf_op jit(solution)/shard_map/project/pallas_call | solution.py:100
  96.5 25.7 %attend.1 = (bf16[3,1024,1024]{2,1,0:T(8,128)(2,1)S(1)}, bf16[3,512,512]{2,1,0:T(8,128)(2,1)S(1)}, f32[3,1536,128]{2,1,0:T(8,128)S(1)}, bf16[384,192]{1,0:T(8,12...) custom-call(s32[5]{0:T(128)S(1)} %stack.29.place, ...), custom_call_target="tpu_custom_call" | custom-call | flops 12000000000 | bytes 20000000 | tf_op jit(solution)/shard_map/attend/pallas_call | solution.py:175
  122.9 2.6 copy-done.36
  125.5 1.4 copy-done.37
  128.5 1.5 collective-permute-start.4
  129.9 1.6 collective-permute-start.5
  132.1 3.9 %collective-permute-done.3.a1 = bf16[384,192]{1,0:T(8,128)(2,1)S(1)} collective-permute-done((bf16[384,192]{1,0:T(8,128)(2,1)}, bf16[384,192]{1,0:T(8,128)(2,1)S(1)}, u32[]{:S(2)}, u32[]{:S(2)}) %collective-permute-start.3) | collective-permute-done | bytes 147488 | tf_op jit(solution)/shard_map/ppermute | solution.py:635
  136.1 3.5 %collective-permute-done.5.a3 = bf16[384,192]{1,0:T(8,128)(2,1)S(1)} collective-permute-done((bf16[384,192]{1,0:T(8,128)(2,1)}, bf16[384,192]{1,0:T(8,128)(2,1)S(1)}, u32[]{:S(2)}, u32[]{:S(2)}) %collective-permute-start.5) | collective-permute-done | bytes 147488 | tf_op jit(solution)/shard_map/ppermute | solution.py:635
  141.5 19.4 %middle.1 = (bf16[384,768]{1,0:T(8,128)(2,1)}, bf16[384,768]{1,0:T(8,128)(2,1)S(1)}, bf16[384,3072]{1,0:T(8,128)(2,1)S(1)}, bf16[384,3072]{1,0:T(8,128)(2,1)S(1)...) custom-call(s32[5]{0:T(128)S(1)} %stack.29.place, ...), custom_call_target="tpu_custom_call" | custom-call | flops 8000000000 | bytes 20000000 | tf_op jit(solution)/shard_map/middle/pallas_call | solution.py:587
  163.0 5.0 %in_blocks.1 = (bf16[16,128,768]{2,1,0:T(8,128)(2,1)S(1)}, bf16[16,128,768]{2,1,0:T(8,128)(2,1)S(1)}) custom-call(s32[35]{0:T(128)S(1)} %get-tuple-element.245.place, bf16[384,768]{1,0:T(8,128)(2,1)S(1)} %get-tuple-element.125.h_ref, bf16[384,3072]{1,0:T(8,128)(2,1)S(1)} %get-tuple-element.126.dz_ref, bf16[384,192]{1,0:T(8,128)(2,1)S(1)} %copy-done.35, ...), custom_call_target="tpu_custom_call" | custom-call | flops 2264924160 | bytes 12000000 | tf_op jit(solution)/shard_map/in_blocks/pallas_call | solution.py:755
  168.4 5.6 %back_blocks.1 = (bf16[16,96,768]{2,1,0:T(8,128)(2,1)S(1)}, bf16[16,96,768]{2,1,0:T(8,128)(2,1)S(1)}) custom-call(s32[35]{0:T(128)S(1)} %get-tuple-element.244.place, bf16[384,3072]{1,0:T(8,128)(2,1)S(1)} %get-tuple-element.121.u_ref, bf16[384,768]{1,0:T(8,128)(2,1)S(1)} %get-tuple-element.122.df_ref), custom_call_target="tpu_custom_call" | custom-call | flops 1811939328 | bytes 8000000 | tf_op jit(solution)/shard_map/back_blocks/pallas_call | solution.py:692
  176.4 1.4 collective-permute-start.8
  178.7 2.1 merge.4
  181.1 1.6 copy-done.3
  186.9 31.6 %attend_back.1 = (bf16[768,640]{1,0:T(8,128)(2,1)S(1)}, bf16[768,640]{1,0:T(8,128)(2,1)S(1)}, f32[768,256]{1,0:T(8,128)S(1)}, f32[3,8,128]{2,1,0:T(8,128)S(1)}) custom-call(s32[5]{0:T(128)S(1)} %stack.29.place, bf16[384,192]{1,0:T(8,128)(2,1)S(1)} %get-tuple-element.114.d0, bf16[384,192]{1,0:T(8,128)(2,1)S(1)} %collective-permute-done.6.d1, ...), custom_call_target="tpu_custom_call" | custom-call | flops 20000000000 | bytes 25000000 | tf_op jit(solution)/shard_map/attend_back/pallas_call | solution.py:337
  218.5 5.2 %qkv_blocks.1 = bf16[8,104,768]{2,1,0:T(8,128)(2,1)} custom-call(bf16[384,768]{1,0:T(8,128)(2,1)} %bitcast.5.x0.x_ref, bf16[384,768]{1,0:T(8,128)(2,1)} %collective-permute-done.x1, bf16[384,768]{1,0:T(8,128)(2,1)} %collective-permute-done.1.x2, bf16[384,768]{1,0:T(8,128)(2,1)} %collective-permute-done.2.x3, ...), custom_call_target="tpu_custom_call" | custom-call | flops 2000000000 | bytes 8000000 | tf_op jit(solution)/shard_map/qkv_blocks/pallas_call | solution.py:419
  223.8 2.1 convolution_convert_fusion
  226.5 3.2 merge.5
  229.7 1.4 collective-permute-start.15
  232.7 24.4 %collective-permute-done.14.refs_3_ = bf16[4,96,768]{2,1,0:T(8,128)(2,1)S(1)} collective-permute-done((bf16[4,96,768]{2,1,0:T(8,128)(2,1)}, bf16[4,96,768]{2,1,0:T(8,128)(2,1)S(1)}, u32[]{:S(2)}, u32[]{:S(2)}) %collective-permute-start.14) | collective-permute-done | bytes 589856 | tf_op jit(solution)/shard_map/ppermute | solution.py:635
  257.1 2.4 fusion
  260.0 2.8 merge.6
  262.8 1.5 collective-permute-start.18
  264.3 1.6 collective-permute-start.17
  266.8 6.0 %collective-permute-done.17.refs_4_ = bf16[2,96,768]{2,1,0:T(8,128)(2,1)} collective-permute-done((bf16[2,96,768]{2,1,0:T(8,128)(2,1)}, bf16[2,96,768]{2,1,0:T(8,128)(2,1)}, u32[]{:S(2)}, u32[]{:S(2)}) %collective-permute-start.17) | collective-permute-done | bytes 294944 | tf_op jit(solution)/shard_map/ppermute | solution.py:635
  273.4 2.5 merge.7
  278.5 1.5 collective-permute-start.21
  280.0 1.8 collective-permute-start.22
  281.8 2.3 fusion.3
  284.2 3.5 %all-to-all-start.1 = ((bf16[8,48,768]{2,1,0:T(8,128)(2,1)}), bf16[8,48,768]{2,1,0:T(8,128)(2,1)S(1)}, u32[]{:S(2)}, u32[]{:S(2)}) async-start(bf16[8,48,768]{2,1,0:T(8,128)(2,1)} %bitcast.121), calls=%async_computation.1 | async-start | bytes 1179648 | tf_op jit(solution)/shard_map/all_to_all | solution.py:977
  296.8 11.9 %all-to-all-done.1.in_ref = bf16[8,48,768]{2,1,0:T(8,128)(2,1)S(1)} async-done(((bf16[8,48,768]{2,1,0:T(8,128)(2,1)}), bf16[8,48,768]{2,1,0:T(8,128)(2,1)S(1)}, u32[]{:S(2)}, u32[]{:S(2)}) %all-to-all-start.1) | async-done | bytes 589856 | tf_op jit(solution)/shard_map/all_to_all | solution.py:977
  310.1 2.1 add_bitcast_fusion
  312.2 1.5 convert_add_fusion
  (224 shorter events, 56.1 us)
Async XLA Ops:
  7.2 55.5 %all-gather.5.cloned.1.call-start = ((), (), s32[]{:S(2)}) async-start(), calls=%async_computation.4 | async-start | bytes 1437696 | tf_op jit(solution)/shard_map/all_gather | solution.py:834
  12.4 128.1 %all-gather.7.cloned.1.call-start = ((), (), s32[]{:S(2)}) async-start(), calls=%async_computation.5 | async-start | bytes 11354112 | tf_op jit(solution)/shard_map/all_gather | solution.py:870
  14.5 8.8 %copy-start.47 = (s32[8,3]{0,1:T(4,128)S(1)}, s32[8,3]{0,1:T(4,128)}, u32[]{:S(2)}) copy-start(s32[8,3]{0,1:T(4,128)} %param.44) | copy-start | bytes 292
  14.5 10.2 %copy-start.45 = (s32[8,1536]{1,0:T(8,128)S(1)}, s32[8,1536]{1,0:T(8,128)}, u32[]{:S(2)}) copy-start(s32[8,1536]{1,0:T(8,128)} %param.45) | copy-start | bytes 147460
  16.8 32.5 %all-to-all-start = ((bf16[8,48,768]{2,1,0:T(8,128)(2,1)}), bf16[8,48,768]{2,1,0:T(8,128)(2,1)}, u32[]{:S(2)}, u32[]{:S(2)}) async-start(bf16[8,48,768]{2,1,0:T(8,128)(2,1)} %deal.1), calls=%async_computation | async-start | bytes 1179648 | tf_op jit(solution)/shard_map/all_to_all | solution.py:807
  23.2 242.7 %reduce-scatter.2.cloned.1.call-start = ((), (), s32[]{:S(2)}) async-start(), calls=%async_computation.3 | async-start | bytes 1437696 | tf_op jit(solution)/shard_map/reduce_scatter | solution.py:957
  28.4 55.8 %copy-start.15 = (s32[1536,1]{1,0:T(8,128)}, s32[1536,1]{1,0:T(8,128)S(1)}, u32[]{:S(2)}) copy-start(s32[1536,1]{1,0:T(8,128)S(1)} %broadcast_in_dim.38.tcol_ref) | copy-start | bytes 18436
  40.1 56.3 %copy-start.6 = (f32[1536,384]{1,0:T(8,128)}, f32[1536,384]{1,0:T(8,128)S(1)}, u32[]{:S(2)}) copy-start(f32[1536,384]{1,0:T(8,128)S(1)} %get-tuple-element.238.cs_ref) | copy-start | bytes 7077892
  49.3 12.8 %collective-permute-start = (bf16[384,768]{1,0:T(8,128)(2,1)}, bf16[384,768]{1,0:T(8,128)(2,1)}, u32[]{:S(2)}, u32[]{:S(2)}) collective-permute-start(bf16[384,768]{1,0:T(8,128)(2,1)} %bitcast.5.x0.x_ref), channel_id=1, source_target_pairs={{0,8},{1,17},{2,10},{3,19},{4,12},{5,21},{6,14},{7,23},{8,0},{9,25... | collective-permute-start | bytes 1769480 | tf_op jit(solution)/shard_map/ppermute | solution.py:635
  60.7 20.2 %collective-permute-start.1 = (bf16[384,768]{1,0:T(8,128)(2,1)}, bf16[384,768]{1,0:T(8,128)(2,1)}, u32[]{:S(2)}, u32[]{:S(2)}) collective-permute-start(bf16[384,768]{1,0:T(8,128)(2,1)} %bitcast.5.x0.x_ref), channel_id=1, source_target_pairs={{0,16},{1,9},{2,18},{3,11},{4,20},{5,13},{6,22},{7,15},{8,24},{9,1... | collective-permute-start | bytes 1769480 | tf_op jit(solution)/shard_map/ppermute | solution.py:635
  62.2 18.7 %collective-permute-start.2 = (bf16[384,768]{1,0:T(8,128)(2,1)}, bf16[384,768]{1,0:T(8,128)(2,1)}, u32[]{:S(2)}, u32[]{:S(2)}) collective-permute-start(bf16[384,768]{1,0:T(8,128)(2,1)} %collective-permute-done.x1), channel_id=1, source_target_pairs={{0,16},{1,9},{2,18},{3,11},{4,20},{5,13},{6,22},{7,15},{8,24},{9,1... | collective-permute-start | bytes 1769480 | tf_op jit(solution)/shard_map/ppermute | solution.py:635
  84.2 11.2 %copy-start.13 = (bf16[768,640]{1,0:T(8,128)(2,1)}, bf16[768,640]{1,0:T(8,128)(2,1)S(1)}, u32[]{:S(2)}) copy-start(bf16[768,640]{1,0:T(8,128)(2,1)S(1)} %maximum_maximum_fusion.w_ref) | copy-start | bytes 2949124
  84.2 12.3 %copy-start.7 = (f32[1536,384]{1,0:T(8,128)S(1)}, f32[1536,384]{1,0:T(8,128)}, u32[]{:S(2)}) copy-start(f32[1536,384]{1,0:T(8,128)} %get-tuple-element.241.sn_ref) | copy-start | bytes 7077892
  84.2 12.3 %copy-start.10 = (bf16[768,1536]{1,0:T(8,128)(2,1)S(1)}, bf16[768,1536]{1,0:T(8,128)(2,1)}, u32[]{:S(2)}) copy-start(bf16[768,1536]{1,0:T(8,128)(2,1)} %copy.72.kpt_ref) | copy-start | bytes 7077892
  84.2 12.3 %copy-start.19 = (bf16[3,128,768]{2,1,0:T(8,128)(2,1)S(1)}, bf16[3,128,768]{2,1,0:T(8,128)(2,1)}, u32[]{:S(2)}) copy-start(bf16[3,128,768]{2,1,0:T(8,128)(2,1)} %pad.79.wrt_ref) | copy-start | bytes 1769476
  96.4 25.8 %copy-start.26 = (bf16[3,1536,128]{2,1,0:T(8,128)(2,1)}, bf16[3,1536,128]{2,1,0:T(8,128)(2,1)S(1)}, u32[]{:S(2)}) copy-start(bf16[3,1536,128]{2,1,0:T(8,128)(2,1)S(1)} %get-tuple-element.133.qx_ref) | copy-start | bytes 3538948
  96.4 25.8 %copy-start.28 = (bf16[3,1536,128]{2,1,0:T(8,128)(2,1)}, bf16[3,1536,128]{2,1,0:T(8,128)(2,1)S(1)}, u32[]{:S(2)}) copy-start(bf16[3,1536,128]{2,1,0:T(8,128)(2,1)S(1)} %get-tuple-element.105.pq_ref) | copy-start | bytes 3538948
  96.4 25.8 %copy-start.32 = (bf16[3,128,1536]{2,1,0:T(8,128)(2,1)}, bf16[3,128,1536]{2,1,0:T(8,128)(2,1)S(1)}, u32[]{:S(2)}) copy-start(bf16[3,128,1536]{2,1,0:T(8,128)(2,1)S(1)} %get-tuple-element.135.vxt_ref) | copy-start | bytes 3538948
  96.5 44.0 %copy-start.21 = (bf16[1,384,768]{2,1,0:T(8,128)(2,1)S(1)}, bf16[1,384,768]{2,1,0:T(8,128)(2,1)}, u32[]{:S(2)}) copy-start(bf16[1,384,768]{2,1,0:T(8,128)(2,1)} %param.47) | copy-start | bytes 1769476
  128.1 8.0 %collective-permute-start.3 = (bf16[384,192]{1,0:T(8,128)(2,1)}, bf16[384,192]{1,0:T(8,128)(2,1)S(1)}, u32[]{:S(2)}, u32[]{:S(2)}) collective-permute-start(bf16[384,192]{1,0:T(8,128)(2,1)} %get-tuple-element.109), channel_id=1, source_target_pairs={{0,8},{1,17},{2,10},{3,19},{4,12},{5,21},{6,14},{7,23},{8,0},{9,25... | collective-permute-start | bytes 442376 | tf_op jit(solution)/shard_map/ppermute | solution.py:635
  128.5 7.6 %collective-permute-start.4 = (bf16[384,192]{1,0:T(8,128)(2,1)}, bf16[384,192]{1,0:T(8,128)(2,1)S(1)}, u32[]{:S(2)}, u32[]{:S(2)}) collective-permute-start(bf16[384,192]{1,0:T(8,128)(2,1)} %get-tuple-element.110), channel_id=1, source_target_pairs={{0,16},{1,9},{2,18},{3,11},{4,20},{5,13},{6,22},{7,15},{8,24},{9,1... | collective-permute-start | bytes 442376 | tf_op jit(solution)/shard_map/ppermute | solution.py:635
  129.9 9.6 %collective-permute-start.5 = (bf16[384,192]{1,0:T(8,128)(2,1)}, bf16[384,192]{1,0:T(8,128)(2,1)S(1)}, u32[]{:S(2)}, u32[]{:S(2)}) collective-permute-start(bf16[384,192]{1,0:T(8,128)(2,1)} %get-tuple-element.111), channel_id=1, source_target_pairs={{0,24},{1,25},{2,26},{3,27},{4,28},{5,29},{6,30},{7,31},{8,16},{9,... | collective-permute-start | bytes 442376 | tf_op jit(solution)/shard_map/ppermute | solution.py:635
  136.1 24.8 %copy-start.22 = (bf16[384,192]{1,0:T(8,128)(2,1)}, bf16[384,192]{1,0:T(8,128)(2,1)S(1)}, u32[]{:S(2)}) copy-start(bf16[384,192]{1,0:T(8,128)(2,1)S(1)} %collective-permute-done.4.a2) | copy-start | bytes 442372
  139.5 21.4 %copy-start.24 = (bf16[384,192]{1,0:T(8,128)(2,1)}, bf16[384,192]{1,0:T(8,128)(2,1)S(1)}, u32[]{:S(2)}) copy-start(bf16[384,192]{1,0:T(8,128)(2,1)S(1)} %collective-permute-done.5.a3) | copy-start | bytes 442372
  168.1 10.5 %copy-start.2 = (bf16[16,128,768]{2,1,0:T(8,128)(2,1)}, bf16[16,128,768]{2,1,0:T(8,128)(2,1)S(1)}, u32[]{:S(2)}) copy-start(bf16[16,128,768]{2,1,0:T(8,128)(2,1)S(1)} %get-tuple-element.169.refs_2_.refs_3_.refs_4_.refs_5_) | copy-start | bytes 9437188
  168.1 10.5 %collective-permute-start.10 = (bf16[16,128,768]{2,1,0:T(8,128)(2,1)S(1)}, bf16[16,128,768]{2,1,0:T(8,128)(2,1)S(1)}, u32[]{:S(2)}, u32[]{:S(2)}) collective-permute-start(bf16[16,128,768]{2,1,0:T(8,128)(2,1)S(1)} %get-tuple-element.130), channel_id=1, source_target_pairs={{0,1},{1,0},{2,3},{3,2},{4,5},{5,4},{6,7},{7,6},{8,9},{9,8},{10,11... | collective-permute-start | bytes 9437192 | tf_op jit(solution)/shard_map/ppermute | solution.py:635
  168.4 18.5 %copy-start.38 = (f32[3,1536,128]{2,1,0:T(8,128)S(1)}, f32[3,1536,128]{2,1,0:T(8,128)}, u32[]{:S(2)}) copy-start(f32[3,1536,128]{2,1,0:T(8,128)} %copy-done.37) | copy-start | bytes 7077892
  168.4 18.5 %copy-start.40 = (bf16[3,512,512]{2,1,0:T(8,128)(2,1)S(1)}, bf16[3,512,512]{2,1,0:T(8,128)(2,1)}, u32[]{:S(2)}) copy-start(bf16[3,512,512]{2,1,0:T(8,128)(2,1)} %copy-done.39) | copy-start | bytes 4718596
  174.0 4.6 %collective-permute-start.9 = (bf16[16,96,768]{2,1,0:T(8,128)(2,1)S(1)}, bf16[16,96,768]{2,1,0:T(8,128)(2,1)S(1)}, u32[]{:S(2)}, u32[]{:S(2)}) collective-permute-start(bf16[16,96,768]{2,1,0:T(8,128)(2,1)S(1)} %get-tuple-element.124), channel_id=1, source_target_pairs={{0,1},{1,0},{2,3},{3,2},{4,5},{5,4},{6,7},{7,6},{8,9},{9,8},{10,11... | collective-permute-start | bytes 7077896 | tf_op jit(solution)/shard_map/ppermute | solution.py:635
  174.3 11.1 %collective-permute-start.6 = (bf16[384,192]{1,0:T(8,128)(2,1)S(1)}, bf16[384,192]{1,0:T(8,128)(2,1)S(1)}, u32[]{:S(2)}, u32[]{:S(2)}) collective-permute-start(bf16[384,192]{1,0:T(8,128)(2,1)S(1)} %get-tuple-element.115), channel_id=1, source_target_pairs={{0,8},{1,17},{2,10},{3,19},{4,12},{5,21},{6,14},{7,23},{8,0},{9,25... | collective-permute-start | bytes 442376 | tf_op jit(solution)/shard_map/ppermute | solution.py:635
  175.7 9.7 %collective-permute-start.7 = (bf16[384,192]{1,0:T(8,128)(2,1)S(1)}, bf16[384,192]{1,0:T(8,128)(2,1)S(1)}, u32[]{:S(2)}, u32[]{:S(2)}) collective-permute-start(bf16[384,192]{1,0:T(8,128)(2,1)S(1)} %get-tuple-element.116), channel_id=1, source_target_pairs={{0,16},{1,9},{2,18},{3,11},{4,20},{5,13},{6,22},{7,15},{8,24},{9,1... | collective-permute-start | bytes 442376 | tf_op jit(solution)/shard_map/ppermute | solution.py:635
  176.4 10.5 %collective-permute-start.8 = (bf16[384,192]{1,0:T(8,128)(2,1)S(1)}, bf16[384,192]{1,0:T(8,128)(2,1)S(1)}, u32[]{:S(2)}, u32[]{:S(2)}) collective-permute-start(bf16[384,192]{1,0:T(8,128)(2,1)S(1)} %get-tuple-element.117), channel_id=1, source_target_pairs={{0,24},{1,25},{2,26},{3,27},{4,28},{5,29},{6,30},{7,31},{8,16},{9,... | collective-permute-start | bytes 442376 | tf_op jit(solution)/shard_map/ppermute | solution.py:635
  182.7 43.2 %collective-permute-start.12 = (bf16[8,128,768]{2,1,0:T(8,128)(2,1)}, bf16[8,128,768]{2,1,0:T(8,128)(2,1)}, u32[]{:S(2)}, u32[]{:S(2)}) collective-permute-start(bf16[8,128,768]{2,1,0:T(8,128)(2,1)} %get-tuple-element.140), channel_id=1, source_target_pairs={{0,8},{1,17},{2,10},{3,19},{4,12},{5,21},{6,14},{7,23},{8,0},{9,25... | collective-permute-start | bytes 4718600 | tf_op jit(solution)/shard_map/ppermute | solution.py:635
  184.1 41.8 %collective-permute-start.11 = (bf16[8,96,768]{2,1,0:T(8,128)(2,1)}, bf16[8,96,768]{2,1,0:T(8,128)(2,1)}, u32[]{:S(2)}, u32[]{:S(2)}) collective-permute-start(bf16[8,96,768]{2,1,0:T(8,128)(2,1)} %get-tuple-element.139), channel_id=1, source_target_pairs={{0,2},{1,3},{2,0},{3,1},{4,6},{5,7},{6,4},{7,5},{8,10},{9,11},{10,... | collective-permute-start | bytes 3538952 | tf_op jit(solution)/shard_map/ppermute | solution.py:635
  225.9 31.2 %collective-permute-start.13 = (bf16[768,768]{1,0:T(8,128)(2,1)}, bf16[768,768]{1,0:T(8,128)(2,1)}, u32[]{:S(2)}, u32[]{:S(2)}) collective-permute-start(bf16[768,768]{1,0:T(8,128)(2,1)} %convolution_convert_fusion), channel_id=1, source_target_pairs={{0,8},{1,17},{2,10},{3,19},{4,12},{5,21},{6,14},{7,23},{8,0},{9,25... | collective-permute-start | bytes 3538952 | tf_op jit(solution)/shard_map/ppermute | solution.py:635
  229.7 27.4 %collective-permute-start.15 = (bf16[4,128,768]{2,1,0:T(8,128)(2,1)}, bf16[4,128,768]{2,1,0:T(8,128)(2,1)S(1)}, u32[]{:S(2)}, u32[]{:S(2)}) collective-permute-start(bf16[4,128,768]{2,1,0:T(8,128)(2,1)} %get-tuple-element.151), channel_id=1, source_target_pairs={{0,16},{1,9},{2,18},{3,11},{4,20},{5,13},{6,22},{7,15},{8,24},{9,1... | collective-permute-start | bytes 2359304 | tf_op jit(solution)/shard_map/ppermute | solution.py:635
  231.1 26.0 %collective-permute-start.14 = (bf16[4,96,768]{2,1,0:T(8,128)(2,1)}, bf16[4,96,768]{2,1,0:T(8,128)(2,1)S(1)}, u32[]{:S(2)}, u32[]{:S(2)}) collective-permute-start(bf16[4,96,768]{2,1,0:T(8,128)(2,1)} %get-tuple-element.150), channel_id=1, source_target_pairs={{0,8},{1,17},{2,10},{3,19},{4,12},{5,21},{6,14},{7,23},{8,0},{9,25... | collective-permute-start | bytes 1769480 | tf_op jit(solution)/shard_map/ppermute | solution.py:635
  232.7 24.4 %copy-start.43 = (f32[768,768]{1,0:T(8,128)}, f32[768,768]{1,0:T(8,128)S(1)}, u32[]{:S(2)}) copy-start(f32[768,768]{1,0:T(8,128)S(1)} %fusion.17) | copy-start | bytes 7077892
  259.5 13.9 %collective-permute-start.16 = (bf16[384,768]{1,0:T(8,128)(2,1)}, bf16[384,768]{1,0:T(8,128)(2,1)}, u32[]{:S(2)}, u32[]{:S(2)}) collective-permute-start(bf16[384,768]{1,0:T(8,128)(2,1)} %fusion), channel_id=1, source_target_pairs={{0,16},{1,9},{2,18},{3,11},{4,20},{5,13},{6,22},{7,15},{8,24},{9,1... | collective-permute-start | bytes 1769480 | tf_op jit(solution)/shard_map/ppermute | solution.py:635
  262.8 10.6 %collective-permute-start.18 = (bf16[2,128,768]{2,1,0:T(8,128)(2,1)}, bf16[2,128,768]{2,1,0:T(8,128)(2,1)}, u32[]{:S(2)}, u32[]{:S(2)}) collective-permute-start(bf16[2,128,768]{2,1,0:T(8,128)(2,1)} %get-tuple-element.162), channel_id=1, source_target_pairs={{0,2},{1,3},{2,0},{3,1},{4,6},{5,7},{6,4},{7,5},{8,10},{9,11},{10,... | collective-permute-start | bytes 1179656 | tf_op jit(solution)/shard_map/ppermute | solution.py:635
  264.3 8.6 %collective-permute-start.17 = (bf16[2,96,768]{2,1,0:T(8,128)(2,1)}, bf16[2,96,768]{2,1,0:T(8,128)(2,1)}, u32[]{:S(2)}, u32[]{:S(2)}) collective-permute-start(bf16[2,96,768]{2,1,0:T(8,128)(2,1)} %get-tuple-element.161), channel_id=1, source_target_pairs={{0,16},{1,9},{2,18},{3,11},{4,20},{5,13},{6,22},{7,15},{8,24},{9,1... | collective-permute-start | bytes 884744 | tf_op jit(solution)/shard_map/ppermute | solution.py:635
  266.8 15.0 %copy-start.12 = (f32[384,768]{1,0:T(8,128)S(1)}, f32[384,768]{1,0:T(8,128)}, u32[]{:S(2)}) copy-start(f32[384,768]{1,0:T(8,128)} %copy-done.11) | copy-start | bytes 3538948
  266.8 15.0 %copy-start.44 = (f32[768,768]{1,0:T(8,128)S(1)}, f32[768,768]{1,0:T(8,128)}, u32[]{:S(2)}) copy-start(f32[768,768]{1,0:T(8,128)} %copy-done.43) | copy-start | bytes 7077892
  276.5 15.2 %collective-permute-start.19 = (bf16[1,24,768]{2,1,0:T(8,128)(2,1)}, bf16[1,24,768]{2,1,0:T(8,128)(2,1)S(1)}, u32[]{:S(2)}, u32[]{:S(2)}) collective-permute-start(bf16[1,24,768]{2,1,0:T(8,128)(2,1)} %get-tuple-element.234), channel_id=1, source_target_pairs={{0,8},{1,17},{2,10},{3,19},{4,12},{5,21},{6,14},{7,23},{8,0},{9,25... | collective-permute-start | bytes 110600 | tf_op jit(solution)/shard_map/ppermute | solution.py:635
  277.3 14.5 %collective-permute-start.20 = (bf16[1,24,768]{2,1,0:T(8,128)(2,1)}, bf16[1,24,768]{2,1,0:T(8,128)(2,1)}, u32[]{:S(2)}, u32[]{:S(2)}) collective-permute-start(bf16[1,24,768]{2,1,0:T(8,128)(2,1)} %get-tuple-element.233), channel_id=1, source_target_pairs={{0,16},{1,9},{2,18},{3,11},{4,20},{5,13},{6,22},{7,15},{8,24},{9,1... | collective-permute-start | bytes 110600 | tf_op jit(solution)/shard_map/ppermute | solution.py:635
  278.5 13.3 %collective-permute-start.21 = (bf16[1,24,768]{2,1,0:T(8,128)(2,1)S(1)}, bf16[1,24,768]{2,1,0:T(8,128)(2,1)}, u32[]{:S(2)}, u32[]{:S(2)}) collective-permute-start(bf16[1,24,768]{2,1,0:T(8,128)(2,1)S(1)} %get-tuple-element.232), channel_id=1, source_target_pairs={{0,24},{1,25},{2,26},{3,27},{4,28},{5,29},{6,30},{7,31},{8,16},{9,... | collective-permute-start | bytes 110600 | tf_op jit(solution)/shard_map/ppermute | solution.py:635
  280.0 30.1 %collective-permute-start.22 = (bf16[1,224,768]{2,1,0:T(8,128)(2,1)}, bf16[1,224,768]{2,1,0:T(8,128)(2,1)}, u32[]{:S(2)}, u32[]{:S(2)}) collective-permute-start(bf16[1,224,768]{2,1,0:T(8,128)(2,1)} %merge.7), channel_id=1, source_target_pairs={{0,4},{1,5},{2,6},{3,7},{4,0},{5,1},{6,2},{7,3},{8,12},{9,13},{10,... | collective-permute-start | bytes 1032200 | tf_op jit(solution)/shard_map/ppermute | solution.py:635
  284.2 24.5 %all-to-all-start.1 = ((bf16[8,48,768]{2,1,0:T(8,128)(2,1)}), bf16[8,48,768]{2,1,0:T(8,128)(2,1)S(1)}, u32[]{:S(2)}, u32[]{:S(2)}) async-start(bf16[8,48,768]{2,1,0:T(8,128)(2,1)} %bitcast.121), calls=%async_computation.1 | async-start | bytes 1179648 | tf_op jit(solution)/shard_map/all_to_all | solution.py:977
  (28 other events, 133.1 us)
Sparse Core Ops, SparseCore 0:
  12.5 36.3 all-gather.4
  51.9 88.6 all-gather.6
  223.9 32.0 reduce-scatter.1

commit v4 on v3

--- a/solution.py
+++ b/solution.py
@@ -721,10 +721,9 @@
                 h_ref[:, g * 384 : (g + 1) * 384], dz_ref[...], (((0,), (0,)), ((), ())), preferred_element_type=F32
             )
             for j in range(0, 16, 2):
-                put(g * 16 + j, which * 24, acc[j * 24 : (j + 2) * 24])
-
-    for which in range(4):
-        pl.when(step == which)(lambda which=which: chunk(which))
+                put(g * 16 + j, pl.multiple_of(which * 24, 8), acc[j * 24 : (j + 2) * 24])
+
+    pl.when(step < 4)(lambda: chunk(step))
 
     @pl.when(step == 4)
     def _():

time: 324 us -> 324 us (level)
  no operation moved by 1% of the time
where the time goes in v4:
time: 324 us; the launch traced here: 322 us
  Pallas kernels  117 us (36%)
  waiting for transfers between devices  62.5 us (19%)
  local copies, waits for them, and re-layouts  53.3 us (16%)
  starting transfers between devices  34.8 us (11%)
  other arithmetic  33.3 us (10%)
  between operations  17.8 us (5%)
    ppermute x23, waiting for transfers between devices, across(): return lax.ppermute(values, ('seq', 'fsdp'), pairs)  40.6 us
    pallas_call x1, Pallas kernels, attend_back(): pl.pallas_call(back_body, grid=(3, blocks), in_specs=[SM] + [pl.BlockSpec...  31.8 us
    pallas_call x1, Pallas kernels, attend(): pl.pallas_call(attend_body, grid=(3, blocks), in_specs=[SM, pl.BlockSpec(...  25.7 us
    ppermute x23, starting transfers between devices, across(): return lax.ppermute(values, ('seq', 'fsdp'), pairs)  24.8 us
    pallas_call x1, Pallas kernels, middle(): pl.pallas_call(middle_body, in_specs=[SM] + [VM] * 6 + [pl.BlockSpec(memo...  19.4 us
    unnamed x102, local copies, waits for them, and re-layouts  14.3 us
    all_to_all x1, waiting for transfers between devices, shards(): lax.all_to_all(input_rows, 'fsdp', split_axis=0, concat_axis=0, tiled=True)  11.7 us
    pallas_call x1, Pallas kernels, project(): pl.pallas_call(project_body, in_specs=[SM] + [VM] * 7, out_specs=[VM] * 6...  11.2 us
  transfers between devices with their start and end apart: 28, of which 10 were waited for; matrix products, arithmetic and copies ran while one was open for 20% of the time, Pallas kernels for 28%

profile of v4, /device:TPU:0, one launch (start us, length us, event | category | flops | bytes accessed | tf_op | source)
XLA Modules:
  0.0 322.4 jit_solution(15845147239337428411)
XLA Ops:
  15.4 1.4 deal.1
  16.8 6.4 %all-to-all-start = ((bf16[8,48,768]{2,1,0:T(8,128)(2,1)}), bf16[8,48,768]{2,1,0:T(8,128)(2,1)}, u32[]{:S(2)}, u32[]{:S(2)}) async-start(bf16[8,48,768]{2,1,0:T(8,128)(2,1)} %deal.1), calls=%async_computation | async-start | bytes 1179648 | tf_op jit(solution)/shard_map/all_to_all | solution.py:806
  29.7 10.4 %multiply_cosine_fusion = (f32[1536,384]{1,0:T(8,128)S(1)}, bf16[1536,384]{1,0:T(8,128)(2,1)}, bf16[1536,384]{1,0:T(8,128)(2,1)}, f32[1536,384]{1,0:T(8,128)}) fusion(f32[384]{0:T(512)S(1)} %negate_power_fusion, f32[1536]{0:T(1024)S(1)} %fusion.7), kind=kLoop, calls=%fused_computation.2 | loop fusion | flops 1769472 | bytes 7085568 | tf_op jit(solution)/shard_map/cos | solution.py:613
  40.1 9.2 %all-to-all-done = bf16[8,48,768]{2,1,0:T(8,128)(2,1)} async-done(((bf16[8,48,768]{2,1,0:T(8,128)(2,1)}), bf16[8,48,768]{2,1,0:T(8,128)(2,1)}, u32[]{:S(2)}, u32[]{:S(2)}) %all-to-all-start) | async-done | bytes 589856 | tf_op jit(solution)/shard_map/all_to_all | solution.py:806
  49.3 1.5 collective-permute-start
  50.8 4.0 %pad_maximum_fusion = (bf16[1536,768]{1,0:T(8,128)(2,1)}, bf16[768,1536]{0,1:T(8,128)(2,1)}) fusion(bf16[1536,384]{1,0:T(8,128)(2,1)} %get-tuple-element.239, bf16[1536,384]{1,0:T(8,128)(2,1)} %get-tuple-element.240), kind=kLoop, calls=%fused_computation.3 | loop fusion | flops 4718592 | bytes 7077888 | tf_op jit(solution)/shard_map/concatenate | solution.py:889
  54.8 4.3 %copy.72.kpt_ref = bf16[768,1536]{1,0:T(8,128)(2,1)} copy(bf16[768,1536]{0,1:T(8,128)(2,1)} %get-tuple-element.201) | data formatting | bytes 4718592 | tf_op jit(solution)/shard_map/transpose | solution.py:890
  60.7 1.5 collective-permute-start.1
  65.0 1.4 fusion.13
  66.4 1.9 copy.67
  68.3 1.9 copy.68
  70.1 1.9 pad_maximum_fusion.1
  72.0 2.1 copy.69
  74.9 1.9 copy.65
  76.7 2.0 copy.66
  78.7 2.2 pad.77.wr_ref
  80.9 1.8 pad.79.wrt_ref
  84.2 11.2 %project.1 = (bf16[3,1536,128]{2,1,0:T(8,128)(2,1)S(1)}, bf16[3,1536,128]{2,1,0:T(8,128)(2,1)S(1)}, bf16[3,1536,128]{2,1,0:T(8,128)(2,1)S(1)}, bf16[3,128,1536]{...) custom-call(s32[5]{0:T(128)S(1)} %stack.29.place, ...), custom_call_target="tpu_custom_call" | custom-call | flops 1509949440 | bytes 10000000 | tf_op jit(solution)/shard_map/project/pallas_call | solution.py:100
  96.5 25.7 %attend.1 = (bf16[3,1024,1024]{2,1,0:T(8,128)(2,1)S(1)}, bf16[3,512,512]{2,1,0:T(8,128)(2,1)S(1)}, f32[3,1536,128]{2,1,0:T(8,128)S(1)}, bf16[384,192]{1,0:T(8,12...) custom-call(s32[5]{0:T(128)S(1)} %stack.29.place, ...), custom_call_target="tpu_custom_call" | custom-call | flops 12000000000 | bytes 20000000 | tf_op jit(solution)/shard_map/attend/pallas_call | solution.py:175
  122.9 2.6 copy-done.36
  125.5 1.4 copy-done.37
  128.5 1.5 collective-permute-start.4
  130.0 1.6 collective-permute-start.5
  132.2 3.9 %collective-permute-done.3.a1 = bf16[384,192]{1,0:T(8,128)(2,1)S(1)} collective-permute-done((bf16[384,192]{1,0:T(8,128)(2,1)}, bf16[384,192]{1,0:T(8,128)(2,1)S(1)}, u32[]{:S(2)}, u32[]{:S(2)}) %collective-permute-start.3) | collective-permute-done | bytes 147488 | tf_op jit(solution)/shard_map/ppermute | solution.py:635
  136.1 3.4 %collective-permute-done.5.a3 = bf16[384,192]{1,0:T(8,128)(2,1)S(1)} collective-permute-done((bf16[384,192]{1,0:T(8,128)(2,1)}, bf16[384,192]{1,0:T(8,128)(2,1)S(1)}, u32[]{:S(2)}, u32[]{:S(2)}) %collective-permute-start.5) | collective-permute-done | bytes 147488 | tf_op jit(solution)/shard_map/ppermute | solution.py:635
  141.3 19.4 %middle.1 = (bf16[384,768]{1,0:T(8,128)(2,1)}, bf16[384,768]{1,0:T(8,128)(2,1)S(1)}, bf16[384,3072]{1,0:T(8,128)(2,1)S(1)}, bf16[384,3072]{1,0:T(8,128)(2,1)S(1)...) custom-call(s32[5]{0:T(128)S(1)} %stack.29.place, ...), custom_call_target="tpu_custom_call" | custom-call | flops 8000000000 | bytes 20000000 | tf_op jit(solution)/shard_map/middle/pallas_call | solution.py:587
  162.9 5.0 %in_blocks.1 = (bf16[16,128,768]{2,1,0:T(8,128)(2,1)S(1)}, bf16[16,128,768]{2,1,0:T(8,128)(2,1)S(1)}) custom-call(s32[35]{0:T(128)S(1)} %get-tuple-element.245.place, bf16[384,768]{1,0:T(8,128)(2,1)S(1)} %get-tuple-element.125.h_ref, bf16[384,3072]{1,0:T(8,128)(2,1)S(1)} %get-tuple-element.126.dz_ref, bf16[384,192]{1,0:T(8,128)(2,1)S(1)} %copy-done.35, ...), custom_call_target="tpu_custom_call" | custom-call | flops 2264924160 | bytes 12000000 | tf_op jit(solution)/shard_map/in_blocks/pallas_call | solution.py:754
  168.2 5.6 %back_blocks.1 = (bf16[16,96,768]{2,1,0:T(8,128)(2,1)S(1)}, bf16[16,96,768]{2,1,0:T(8,128)(2,1)S(1)}) custom-call(s32[35]{0:T(128)S(1)} %get-tuple-element.244.place, bf16[384,3072]{1,0:T(8,128)(2,1)S(1)} %get-tuple-element.121.u_ref, bf16[384,768]{1,0:T(8,128)(2,1)S(1)} %get-tuple-element.122.df_ref), custom_call_target="tpu_custom_call" | custom-call | flops 1811939328 | bytes 8000000 | tf_op jit(solution)/shard_map/back_blocks/pallas_call | solution.py:692
  178.5 2.1 merge.4
  180.9 1.6 copy-done.3
  186.7 31.8 %attend_back.1 = (bf16[768,640]{1,0:T(8,128)(2,1)S(1)}, bf16[768,640]{1,0:T(8,128)(2,1)S(1)}, f32[768,256]{1,0:T(8,128)S(1)}, f32[3,8,128]{2,1,0:T(8,128)S(1)}) custom-call(s32[5]{0:T(128)S(1)} %stack.29.place, bf16[384,192]{1,0:T(8,128)(2,1)S(1)} %get-tuple-element.114.d0, bf16[384,192]{1,0:T(8,128)(2,1)S(1)} %collective-permute-done.6.d1, ...), custom_call_target="tpu_custom_call" | custom-call | flops 20000000000 | bytes 25000000 | tf_op jit(solution)/shard_map/attend_back/pallas_call | solution.py:337
  218.5 5.2 %qkv_blocks.1 = bf16[8,104,768]{2,1,0:T(8,128)(2,1)} custom-call(bf16[384,768]{1,0:T(8,128)(2,1)} %bitcast.5.x0.x_ref, bf16[384,768]{1,0:T(8,128)(2,1)} %collective-permute-done.x1, bf16[384,768]{1,0:T(8,128)(2,1)} %collective-permute-done.1.x2, bf16[384,768]{1,0:T(8,128)(2,1)} %collective-permute-done.2.x3, ...), custom_call_target="tpu_custom_call" | custom-call | flops 2000000000 | bytes 8000000 | tf_op jit(solution)/shard_map/qkv_blocks/pallas_call | solution.py:419
  223.8 2.1 convolution_convert_fusion
  226.6 3.3 %merge.5 = (bf16[4,96,768]{2,1,0:T(8,128)(2,1)}, bf16[4,128,768]{2,1,0:T(8,128)(2,1)}) custom-call(bf16[16,96,768]{2,1,0:T(8,128)(2,1)} %copy-done.4, bf16[16,96,768]{2,1,0:T(8,128)(2,1)} %copy-done.5, bf16[8,96,768]{2,1,0:T(8,128)(2,1)} %collective-permute-done.11.refs_2_, bf16[16,128,768]{2,1,0:T(8,128)(2,1)} %copy-done.2, ...), custom_call_target="tpu_custom_call" | custom-call | flops 4128768 | bytes 5505024 | tf_op jit(solution)/shard_map/merge/pallas_call | solution.py:455
  232.7 24.4 %collective-permute-done.14.refs_3_ = bf16[4,96,768]{2,1,0:T(8,128)(2,1)S(1)} collective-permute-done((bf16[4,96,768]{2,1,0:T(8,128)(2,1)}, bf16[4,96,768]{2,1,0:T(8,128)(2,1)S(1)}, u32[]{:S(2)}, u32[]{:S(2)}) %collective-permute-start.14) | collective-permute-done | bytes 589856 | tf_op jit(solution)/shard_map/ppermute | solution.py:635
  257.1 2.4 fusion
  260.0 2.8 merge.6
  264.0 1.5 collective-permute-start.17
  266.5 6.3 %collective-permute-done.17.refs_4_ = bf16[2,96,768]{2,1,0:T(8,128)(2,1)} collective-permute-done((bf16[2,96,768]{2,1,0:T(8,128)(2,1)}, bf16[2,96,768]{2,1,0:T(8,128)(2,1)}, u32[]{:S(2)}, u32[]{:S(2)}) %collective-permute-start.17) | collective-permute-done | bytes 294944 | tf_op jit(solution)/shard_map/ppermute | solution.py:635
  273.2 2.5 merge.7
  278.3 1.5 collective-permute-start.21
  279.9 1.8 collective-permute-start.22
  281.7 2.3 fusion.3
  284.1 3.5 %all-to-all-start.1 = ((bf16[8,48,768]{2,1,0:T(8,128)(2,1)}), bf16[8,48,768]{2,1,0:T(8,128)(2,1)S(1)}, u32[]{:S(2)}, u32[]{:S(2)}) async-start(bf16[8,48,768]{2,1,0:T(8,128)(2,1)} %bitcast.121), calls=%async_computation.1 | async-start | bytes 1179648 | tf_op jit(solution)/shard_map/all_to_all | solution.py:976
  296.7 11.7 %all-to-all-done.1.in_ref = bf16[8,48,768]{2,1,0:T(8,128)(2,1)S(1)} async-done(((bf16[8,48,768]{2,1,0:T(8,128)(2,1)}), bf16[8,48,768]{2,1,0:T(8,128)(2,1)S(1)}, u32[]{:S(2)}, u32[]{:S(2)}) %all-to-all-start.1) | async-done | bytes 589856 | tf_op jit(solution)/shard_map/all_to_all | solution.py:976
  308.5 1.4 reload.1
  309.9 2.1 add_bitcast_fusion
  312.0 1.5 convert_add_fusion
  (224 shorter events, 55.5 us)
Async XLA Ops:
  7.2 55.5 %all-gather.5.cloned.1.call-start = ((), (), s32[]{:S(2)}) async-start(), calls=%async_computation.4 | async-start | bytes 1437696 | tf_op jit(solution)/shard_map/all_gather | solution.py:833
  12.4 128.0 %all-gather.7.cloned.1.call-start = ((), (), s32[]{:S(2)}) async-start(), calls=%async_computation.5 | async-start | bytes 11354112 | tf_op jit(solution)/shard_map/all_gather | solution.py:869
  14.5 8.8 %copy-start.47 = (s32[8,3]{0,1:T(4,128)S(1)}, s32[8,3]{0,1:T(4,128)}, u32[]{:S(2)}) copy-start(s32[8,3]{0,1:T(4,128)} %param.44) | copy-start | bytes 292
  14.5 10.2 %copy-start.45 = (s32[8,1536]{1,0:T(8,128)S(1)}, s32[8,1536]{1,0:T(8,128)}, u32[]{:S(2)}) copy-start(s32[8,1536]{1,0:T(8,128)} %param.45) | copy-start | bytes 147460
  16.8 32.5 %all-to-all-start = ((bf16[8,48,768]{2,1,0:T(8,128)(2,1)}), bf16[8,48,768]{2,1,0:T(8,128)(2,1)}, u32[]{:S(2)}, u32[]{:S(2)}) async-start(bf16[8,48,768]{2,1,0:T(8,128)(2,1)} %deal.1), calls=%async_computation | async-start | bytes 1179648 | tf_op jit(solution)/shard_map/all_to_all | solution.py:806
  23.2 242.4 %reduce-scatter.2.cloned.1.call-start = ((), (), s32[]{:S(2)}) async-start(), calls=%async_computation.3 | async-start | bytes 1437696 | tf_op jit(solution)/shard_map/reduce_scatter | solution.py:956
  28.4 55.8 %copy-start.15 = (s32[1536,1]{1,0:T(8,128)}, s32[1536,1]{1,0:T(8,128)S(1)}, u32[]{:S(2)}) copy-start(s32[1536,1]{1,0:T(8,128)S(1)} %broadcast_in_dim.38.tcol_ref) | copy-start | bytes 18436
  40.1 56.4 %copy-start.6 = (f32[1536,384]{1,0:T(8,128)}, f32[1536,384]{1,0:T(8,128)S(1)}, u32[]{:S(2)}) copy-start(f32[1536,384]{1,0:T(8,128)S(1)} %get-tuple-element.238.cs_ref) | copy-start | bytes 7077892
  49.3 12.8 %collective-permute-start = (bf16[384,768]{1,0:T(8,128)(2,1)}, bf16[384,768]{1,0:T(8,128)(2,1)}, u32[]{:S(2)}, u32[]{:S(2)}) collective-permute-start(bf16[384,768]{1,0:T(8,128)(2,1)} %bitcast.5.x0.x_ref), channel_id=1, source_target_pairs={{0,8},{1,17},{2,10},{3,19},{4,12},{5,21},{6,14},{7,23},{8,0},{9,25... | collective-permute-start | bytes 1769480 | tf_op jit(solution)/shard_map/ppermute | solution.py:635
  60.7 20.2 %collective-permute-start.1 = (bf16[384,768]{1,0:T(8,128)(2,1)}, bf16[384,768]{1,0:T(8,128)(2,1)}, u32[]{:S(2)}, u32[]{:S(2)}) collective-permute-start(bf16[384,768]{1,0:T(8,128)(2,1)} %bitcast.5.x0.x_ref), channel_id=1, source_target_pairs={{0,16},{1,9},{2,18},{3,11},{4,20},{5,13},{6,22},{7,15},{8,24},{9,1... | collective-permute-start | bytes 1769480 | tf_op jit(solution)/shard_map/ppermute | solution.py:635
  62.2 18.7 %collective-permute-start.2 = (bf16[384,768]{1,0:T(8,128)(2,1)}, bf16[384,768]{1,0:T(8,128)(2,1)}, u32[]{:S(2)}, u32[]{:S(2)}) collective-permute-start(bf16[384,768]{1,0:T(8,128)(2,1)} %collective-permute-done.x1), channel_id=1, source_target_pairs={{0,16},{1,9},{2,18},{3,11},{4,20},{5,13},{6,22},{7,15},{8,24},{9,1... | collective-permute-start | bytes 1769480 | tf_op jit(solution)/shard_map/ppermute | solution.py:635
  84.2 11.3 %copy-start.13 = (bf16[768,640]{1,0:T(8,128)(2,1)}, bf16[768,640]{1,0:T(8,128)(2,1)S(1)}, u32[]{:S(2)}) copy-start(bf16[768,640]{1,0:T(8,128)(2,1)S(1)} %maximum_maximum_fusion.w_ref) | copy-start | bytes 2949124
  84.2 12.3 %copy-start.7 = (f32[1536,384]{1,0:T(8,128)S(1)}, f32[1536,384]{1,0:T(8,128)}, u32[]{:S(2)}) copy-start(f32[1536,384]{1,0:T(8,128)} %get-tuple-element.241.sn_ref) | copy-start | bytes 7077892
  84.2 12.3 %copy-start.10 = (bf16[768,1536]{1,0:T(8,128)(2,1)S(1)}, bf16[768,1536]{1,0:T(8,128)(2,1)}, u32[]{:S(2)}) copy-start(bf16[768,1536]{1,0:T(8,128)(2,1)} %copy.72.kpt_ref) | copy-start | bytes 7077892
  84.2 12.3 %copy-start.19 = (bf16[3,128,768]{2,1,0:T(8,128)(2,1)S(1)}, bf16[3,128,768]{2,1,0:T(8,128)(2,1)}, u32[]{:S(2)}) copy-start(bf16[3,128,768]{2,1,0:T(8,128)(2,1)} %pad.79.wrt_ref) | copy-start | bytes 1769476
  96.5 25.8 %copy-start.26 = (bf16[3,1536,128]{2,1,0:T(8,128)(2,1)}, bf16[3,1536,128]{2,1,0:T(8,128)(2,1)S(1)}, u32[]{:S(2)}) copy-start(bf16[3,1536,128]{2,1,0:T(8,128)(2,1)S(1)} %get-tuple-element.133.qx_ref) | copy-start | bytes 3538948
  96.5 25.8 %copy-start.28 = (bf16[3,1536,128]{2,1,0:T(8,128)(2,1)}, bf16[3,1536,128]{2,1,0:T(8,128)(2,1)S(1)}, u32[]{:S(2)}) copy-start(bf16[3,1536,128]{2,1,0:T(8,128)(2,1)S(1)} %get-tuple-element.105.pq_ref) | copy-start | bytes 3538948
  96.5 25.8 %copy-start.32 = (bf16[3,128,1536]{2,1,0:T(8,128)(2,1)}, bf16[3,128,1536]{2,1,0:T(8,128)(2,1)S(1)}, u32[]{:S(2)}) copy-start(bf16[3,128,1536]{2,1,0:T(8,128)(2,1)S(1)} %get-tuple-element.135.vxt_ref) | copy-start | bytes 3538948
  96.5 43.9 %copy-start.21 = (bf16[1,384,768]{2,1,0:T(8,128)(2,1)S(1)}, bf16[1,384,768]{2,1,0:T(8,128)(2,1)}, u32[]{:S(2)}) copy-start(bf16[1,384,768]{2,1,0:T(8,128)(2,1)} %param.47) | copy-start | bytes 1769476
  128.1 8.0 %collective-permute-start.3 = (bf16[384,192]{1,0:T(8,128)(2,1)}, bf16[384,192]{1,0:T(8,128)(2,1)S(1)}, u32[]{:S(2)}, u32[]{:S(2)}) collective-permute-start(bf16[384,192]{1,0:T(8,128)(2,1)} %get-tuple-element.109), channel_id=1, source_target_pairs={{0,8},{1,17},{2,10},{3,19},{4,12},{5,21},{6,14},{7,23},{8,0},{9,25... | collective-permute-start | bytes 442376 | tf_op jit(solution)/shard_map/ppermute | solution.py:635
  128.5 7.6 %collective-permute-start.4 = (bf16[384,192]{1,0:T(8,128)(2,1)}, bf16[384,192]{1,0:T(8,128)(2,1)S(1)}, u32[]{:S(2)}, u32[]{:S(2)}) collective-permute-start(bf16[384,192]{1,0:T(8,128)(2,1)} %get-tuple-element.110), channel_id=1, source_target_pairs={{0,16},{1,9},{2,18},{3,11},{4,20},{5,13},{6,22},{7,15},{8,24},{9,1... | collective-permute-start | bytes 442376 | tf_op jit(solution)/shard_map/ppermute | solution.py:635
  130.0 9.6 %collective-permute-start.5 = (bf16[384,192]{1,0:T(8,128)(2,1)}, bf16[384,192]{1,0:T(8,128)(2,1)S(1)}, u32[]{:S(2)}, u32[]{:S(2)}) collective-permute-start(bf16[384,192]{1,0:T(8,128)(2,1)} %get-tuple-element.111), channel_id=1, source_target_pairs={{0,24},{1,25},{2,26},{3,27},{4,28},{5,29},{6,30},{7,31},{8,16},{9,... | collective-permute-start | bytes 442376 | tf_op jit(solution)/shard_map/ppermute | solution.py:635
  136.1 24.7 %copy-start.22 = (bf16[384,192]{1,0:T(8,128)(2,1)}, bf16[384,192]{1,0:T(8,128)(2,1)S(1)}, u32[]{:S(2)}) copy-start(bf16[384,192]{1,0:T(8,128)(2,1)S(1)} %collective-permute-done.4.a2) | copy-start | bytes 442372
  139.5 21.2 %copy-start.24 = (bf16[384,192]{1,0:T(8,128)(2,1)}, bf16[384,192]{1,0:T(8,128)(2,1)S(1)}, u32[]{:S(2)}) copy-start(bf16[384,192]{1,0:T(8,128)(2,1)S(1)} %collective-permute-done.5.a3) | copy-start | bytes 442372
  167.9 10.5 %copy-start.2 = (bf16[16,128,768]{2,1,0:T(8,128)(2,1)}, bf16[16,128,768]{2,1,0:T(8,128)(2,1)S(1)}, u32[]{:S(2)}) copy-start(bf16[16,128,768]{2,1,0:T(8,128)(2,1)S(1)} %get-tuple-element.169.refs_2_.refs_3_.refs_4_.refs_5_) | copy-start | bytes 9437188
  167.9 10.5 %collective-permute-start.10 = (bf16[16,128,768]{2,1,0:T(8,128)(2,1)S(1)}, bf16[16,128,768]{2,1,0:T(8,128)(2,1)S(1)}, u32[]{:S(2)}, u32[]{:S(2)}) collective-permute-start(bf16[16,128,768]{2,1,0:T(8,128)(2,1)S(1)} %get-tuple-element.130), channel_id=1, source_target_pairs={{0,1},{1,0},{2,3},{3,2},{4,5},{5,4},{6,7},{7,6},{8,9},{9,8},{10,11... | collective-permute-start | bytes 9437192 | tf_op jit(solution)/shard_map/ppermute | solution.py:635
  168.2 18.5 %copy-start.38 = (f32[3,1536,128]{2,1,0:T(8,128)S(1)}, f32[3,1536,128]{2,1,0:T(8,128)}, u32[]{:S(2)}) copy-start(f32[3,1536,128]{2,1,0:T(8,128)} %copy-done.37) | copy-start | bytes 7077892
  168.2 18.5 %copy-start.40 = (bf16[3,512,512]{2,1,0:T(8,128)(2,1)S(1)}, bf16[3,512,512]{2,1,0:T(8,128)(2,1)}, u32[]{:S(2)}) copy-start(bf16[3,512,512]{2,1,0:T(8,128)(2,1)} %copy-done.39) | copy-start | bytes 4718596
  173.8 4.6 %collective-permute-start.9 = (bf16[16,96,768]{2,1,0:T(8,128)(2,1)S(1)}, bf16[16,96,768]{2,1,0:T(8,128)(2,1)S(1)}, u32[]{:S(2)}, u32[]{:S(2)}) collective-permute-start(bf16[16,96,768]{2,1,0:T(8,128)(2,1)S(1)} %get-tuple-element.124), channel_id=1, source_target_pairs={{0,1},{1,0},{2,3},{3,2},{4,5},{5,4},{6,7},{7,6},{8,9},{9,8},{10,11... | collective-permute-start | bytes 7077896 | tf_op jit(solution)/shard_map/ppermute | solution.py:635
  174.1 11.2 %collective-permute-start.6 = (bf16[384,192]{1,0:T(8,128)(2,1)S(1)}, bf16[384,192]{1,0:T(8,128)(2,1)S(1)}, u32[]{:S(2)}, u32[]{:S(2)}) collective-permute-start(bf16[384,192]{1,0:T(8,128)(2,1)S(1)} %get-tuple-element.115), channel_id=1, source_target_pairs={{0,8},{1,17},{2,10},{3,19},{4,12},{5,21},{6,14},{7,23},{8,0},{9,25... | collective-permute-start | bytes 442376 | tf_op jit(solution)/shard_map/ppermute | solution.py:635
  175.5 9.7 %collective-permute-start.7 = (bf16[384,192]{1,0:T(8,128)(2,1)S(1)}, bf16[384,192]{1,0:T(8,128)(2,1)S(1)}, u32[]{:S(2)}, u32[]{:S(2)}) collective-permute-start(bf16[384,192]{1,0:T(8,128)(2,1)S(1)} %get-tuple-element.116), channel_id=1, source_target_pairs={{0,16},{1,9},{2,18},{3,11},{4,20},{5,13},{6,22},{7,15},{8,24},{9,1... | collective-permute-start | bytes 442376 | tf_op jit(solution)/shard_map/ppermute | solution.py:635
  176.2 10.5 %collective-permute-start.8 = (bf16[384,192]{1,0:T(8,128)(2,1)S(1)}, bf16[384,192]{1,0:T(8,128)(2,1)S(1)}, u32[]{:S(2)}, u32[]{:S(2)}) collective-permute-start(bf16[384,192]{1,0:T(8,128)(2,1)S(1)} %get-tuple-element.117), channel_id=1, source_target_pairs={{0,24},{1,25},{2,26},{3,27},{4,28},{5,29},{6,30},{7,31},{8,16},{9,... | collective-permute-start | bytes 442376 | tf_op jit(solution)/shard_map/ppermute | solution.py:635
  182.5 43.4 %collective-permute-start.12 = (bf16[8,128,768]{2,1,0:T(8,128)(2,1)}, bf16[8,128,768]{2,1,0:T(8,128)(2,1)}, u32[]{:S(2)}, u32[]{:S(2)}) collective-permute-start(bf16[8,128,768]{2,1,0:T(8,128)(2,1)} %get-tuple-element.140), channel_id=1, source_target_pairs={{0,8},{1,17},{2,10},{3,19},{4,12},{5,21},{6,14},{7,23},{8,0},{9,25... | collective-permute-start | bytes 4718600 | tf_op jit(solution)/shard_map/ppermute | solution.py:635
  183.9 42.0 %collective-permute-start.11 = (bf16[8,96,768]{2,1,0:T(8,128)(2,1)}, bf16[8,96,768]{2,1,0:T(8,128)(2,1)}, u32[]{:S(2)}, u32[]{:S(2)}) collective-permute-start(bf16[8,96,768]{2,1,0:T(8,128)(2,1)} %get-tuple-element.139), channel_id=1, source_target_pairs={{0,2},{1,3},{2,0},{3,1},{4,6},{5,7},{6,4},{7,5},{8,10},{9,11},{10,... | collective-permute-start | bytes 3538952 | tf_op jit(solution)/shard_map/ppermute | solution.py:635
  225.9 31.2 %collective-permute-start.13 = (bf16[768,768]{1,0:T(8,128)(2,1)}, bf16[768,768]{1,0:T(8,128)(2,1)}, u32[]{:S(2)}, u32[]{:S(2)}) collective-permute-start(bf16[768,768]{1,0:T(8,128)(2,1)} %convolution_convert_fusion), channel_id=1, source_target_pairs={{0,8},{1,17},{2,10},{3,19},{4,12},{5,21},{6,14},{7,23},{8,0},{9,25... | collective-permute-start | bytes 3538952 | tf_op jit(solution)/shard_map/ppermute | solution.py:635
  229.8 27.2 %collective-permute-start.15 = (bf16[4,128,768]{2,1,0:T(8,128)(2,1)}, bf16[4,128,768]{2,1,0:T(8,128)(2,1)S(1)}, u32[]{:S(2)}, u32[]{:S(2)}) collective-permute-start(bf16[4,128,768]{2,1,0:T(8,128)(2,1)} %get-tuple-element.151), channel_id=1, source_target_pairs={{0,16},{1,9},{2,18},{3,11},{4,20},{5,13},{6,22},{7,15},{8,24},{9,1... | collective-permute-start | bytes 2359304 | tf_op jit(solution)/shard_map/ppermute | solution.py:635
  231.1 25.9 %collective-permute-start.14 = (bf16[4,96,768]{2,1,0:T(8,128)(2,1)}, bf16[4,96,768]{2,1,0:T(8,128)(2,1)S(1)}, u32[]{:S(2)}, u32[]{:S(2)}) collective-permute-start(bf16[4,96,768]{2,1,0:T(8,128)(2,1)} %get-tuple-element.150), channel_id=1, source_target_pairs={{0,8},{1,17},{2,10},{3,19},{4,12},{5,21},{6,14},{7,23},{8,0},{9,25... | collective-permute-start | bytes 1769480 | tf_op jit(solution)/shard_map/ppermute | solution.py:635
  232.7 24.4 %copy-start.43 = (f32[768,768]{1,0:T(8,128)}, f32[768,768]{1,0:T(8,128)S(1)}, u32[]{:S(2)}) copy-start(f32[768,768]{1,0:T(8,128)S(1)} %fusion.17) | copy-start | bytes 7077892
  259.5 13.7 %collective-permute-start.16 = (bf16[384,768]{1,0:T(8,128)(2,1)}, bf16[384,768]{1,0:T(8,128)(2,1)}, u32[]{:S(2)}, u32[]{:S(2)}) collective-permute-start(bf16[384,768]{1,0:T(8,128)(2,1)} %fusion), channel_id=1, source_target_pairs={{0,16},{1,9},{2,18},{3,11},{4,20},{5,13},{6,22},{7,15},{8,24},{9,1... | collective-permute-start | bytes 1769480 | tf_op jit(solution)/shard_map/ppermute | solution.py:635
  262.8 10.4 %collective-permute-start.18 = (bf16[2,128,768]{2,1,0:T(8,128)(2,1)}, bf16[2,128,768]{2,1,0:T(8,128)(2,1)}, u32[]{:S(2)}, u32[]{:S(2)}) collective-permute-start(bf16[2,128,768]{2,1,0:T(8,128)(2,1)} %get-tuple-element.162), channel_id=1, source_target_pairs={{0,2},{1,3},{2,0},{3,1},{4,6},{5,7},{6,4},{7,5},{8,10},{9,11},{10,... | collective-permute-start | bytes 1179656 | tf_op jit(solution)/shard_map/ppermute | solution.py:635
  264.0 8.8 %collective-permute-start.17 = (bf16[2,96,768]{2,1,0:T(8,128)(2,1)}, bf16[2,96,768]{2,1,0:T(8,128)(2,1)}, u32[]{:S(2)}, u32[]{:S(2)}) collective-permute-start(bf16[2,96,768]{2,1,0:T(8,128)(2,1)} %get-tuple-element.161), channel_id=1, source_target_pairs={{0,16},{1,9},{2,18},{3,11},{4,20},{5,13},{6,22},{7,15},{8,24},{9,1... | collective-permute-start | bytes 884744 | tf_op jit(solution)/shard_map/ppermute | solution.py:635
  266.5 15.2 %copy-start.12 = (f32[384,768]{1,0:T(8,128)S(1)}, f32[384,768]{1,0:T(8,128)}, u32[]{:S(2)}) copy-start(f32[384,768]{1,0:T(8,128)} %copy-done.11) | copy-start | bytes 3538948
  266.5 15.2 %copy-start.44 = (f32[768,768]{1,0:T(8,128)S(1)}, f32[768,768]{1,0:T(8,128)}, u32[]{:S(2)}) copy-start(f32[768,768]{1,0:T(8,128)} %copy-done.43) | copy-start | bytes 7077892
  276.4 15.2 %collective-permute-start.19 = (bf16[1,24,768]{2,1,0:T(8,128)(2,1)}, bf16[1,24,768]{2,1,0:T(8,128)(2,1)S(1)}, u32[]{:S(2)}, u32[]{:S(2)}) collective-permute-start(bf16[1,24,768]{2,1,0:T(8,128)(2,1)} %get-tuple-element.234), channel_id=1, source_target_pairs={{0,8},{1,17},{2,10},{3,19},{4,12},{5,21},{6,14},{7,23},{8,0},{9,25... | collective-permute-start | bytes 110600 | tf_op jit(solution)/shard_map/ppermute | solution.py:635
  277.1 14.5 %collective-permute-start.20 = (bf16[1,24,768]{2,1,0:T(8,128)(2,1)}, bf16[1,24,768]{2,1,0:T(8,128)(2,1)}, u32[]{:S(2)}, u32[]{:S(2)}) collective-permute-start(bf16[1,24,768]{2,1,0:T(8,128)(2,1)} %get-tuple-element.233), channel_id=1, source_target_pairs={{0,16},{1,9},{2,18},{3,11},{4,20},{5,13},{6,22},{7,15},{8,24},{9,1... | collective-permute-start | bytes 110600 | tf_op jit(solution)/shard_map/ppermute | solution.py:635
  278.3 13.3 %collective-permute-start.21 = (bf16[1,24,768]{2,1,0:T(8,128)(2,1)S(1)}, bf16[1,24,768]{2,1,0:T(8,128)(2,1)}, u32[]{:S(2)}, u32[]{:S(2)}) collective-permute-start(bf16[1,24,768]{2,1,0:T(8,128)(2,1)S(1)} %get-tuple-element.232), channel_id=1, source_target_pairs={{0,24},{1,25},{2,26},{3,27},{4,28},{5,29},{6,30},{7,31},{8,16},{9,... | collective-permute-start | bytes 110600 | tf_op jit(solution)/shard_map/ppermute | solution.py:635
  279.9 30.0 %collective-permute-start.22 = (bf16[1,224,768]{2,1,0:T(8,128)(2,1)}, bf16[1,224,768]{2,1,0:T(8,128)(2,1)}, u32[]{:S(2)}, u32[]{:S(2)}) collective-permute-start(bf16[1,224,768]{2,1,0:T(8,128)(2,1)} %merge.7), channel_id=1, source_target_pairs={{0,4},{1,5},{2,6},{3,7},{4,0},{5,1},{6,2},{7,3},{8,12},{9,13},{10,... | collective-permute-start | bytes 1032200 | tf_op jit(solution)/shard_map/ppermute | solution.py:635
  284.1 24.4 %all-to-all-start.1 = ((bf16[8,48,768]{2,1,0:T(8,128)(2,1)}), bf16[8,48,768]{2,1,0:T(8,128)(2,1)S(1)}, u32[]{:S(2)}, u32[]{:S(2)}) async-start(bf16[8,48,768]{2,1,0:T(8,128)(2,1)} %bitcast.121), calls=%async_computation.1 | async-start | bytes 1179648 | tf_op jit(solution)/shard_map/all_to_all | solution.py:976
  (28 other events, 133.0 us)
Sparse Core Ops, SparseCore 0:
  12.5 36.3 all-gather.4
  51.9 88.4 all-gather.6
  223.9 31.8 reduce-scatter.1
